TPU v7x, 128 devices: a whole 4x4x4 slice. The times are simulated.
128 devices in a mesh: table: 8 (over x, core), row: 16 (over z, y).
Axes of the slice: x: 4, y: 4, z: 4, core: 2. Of those that a mesh axis runs over, the one named last changes fastest.
Arguments:
- features: bfloat16 [8192, 8192], P('row', 'table'), may hold values from -6 to 6
- cotangent: bfloat16 [8192, 8192], P('row', 'table'), may hold values from -6 to 6
- cross_in: bfloat16 [8192, 512], P('table'), may hold values from -0.0625 to 0.0625
- cross_out: bfloat16 [8192, 512], P('table'), may hold values from -0.25 to 0.25
- bias: float32 [8192], P('table'), may hold values from -6 to 6
- dest_shard: int32 [64, 8192, 1], P('table', 'row'), may hold values from 0 to 15; in each aligned block of 512 rows (0 to 511, 512 to 1023, ..., all dimensions but the last counted through in order) at most 48 rows name the same one
- quot_row: int32 [64, 8192], P('table', 'row'), may hold values from 0 to 1023
- rem_row: int32 [64, 8192], P('table', 'row'), may hold values from 0 to 2047
- quot_slab: bfloat16 [64, 16384, 128], P('table', 'row'), may hold values from -6 to 6
- quot_accum: float32 [64, 16384], P('table', 'row'), may hold values from 0.05 to 2
- rem_table: bfloat16 [64, 2048, 128], P('table'), may hold values from -6 to 6
- rem_accum: float32 [64, 2048], P('table'), may hold values from 0.5 to 20
Outputs:
- quot_out: bfloat16 [64, 16384, 128], P('table', 'row')
- quot_acc_out: float32 [64, 16384], P('table', 'row')
- rem_out: bfloat16 [64, 2048, 128], P('table')
- rem_acc_out: float32 [64, 2048], P('table', 'row')
Inputs may be any that keep to these rules, and one draw needn't show every extreme that they name: `dest_shard`: for each table, the 512 samples of one index of row name one row shard at most 48 times, a bound that some block reaches.
All inputs are finite; a program needn't handle non-finite values.
Results may differ from a plain program's by a relative error of at most 0.004.
Values may be sent and summed in bfloat16 or wider, within the bound.
No kernel may reach another device: no remote copies, remote signals or barrier semaphores. Data moves between devices by JAX's collectives and lax.ppermute only.
A program may use at most 128 MiB of HBM per device.

v0:
```python
import jax
import jax.numpy as jnp
from jax import lax
from jax.sharding import PartitionSpec as P

step_rate = 0.3
epsilon = 1e-06


def table_grads(items):
    grads, keys, slab, rtab = items
    rem_count = rtab.shape[0]
    qlocal = keys // rem_count
    rlocal = keys % rem_count
    q_hot = (qlocal[:, None] == jnp.arange(slab.shape[0], dtype=jnp.int32)[None, :]).astype(
        jnp.bfloat16
    )
    r_hot = (rlocal[:, None] == jnp.arange(rem_count, dtype=jnp.int32)[None, :]).astype(
        jnp.bfloat16
    )
    rem_pick = jnp.dot(r_hot, rtab, preferred_element_type=jnp.float32)
    quot_pick = jnp.dot(q_hot, slab, preferred_element_type=jnp.float32)
    grad_f = grads.astype(jnp.float32)
    over_rows = (((0,), (0,)), ((), ()))
    grad_q = lax.dot_general(
        q_hot.astype(jnp.float32),
        grad_f * rem_pick,
        over_rows,
        precision=lax.Precision.HIGHEST,
        preferred_element_type=jnp.float32,
    )
    grad_r = lax.dot_general(
        r_hot.astype(jnp.float32),
        grad_f * quot_pick,
        over_rows,
        precision=lax.Precision.HIGHEST,
        preferred_element_type=jnp.float32,
    )
    return (grad_q, grad_r)


def per_device(
    features,
    cotangent,
    cross_in,
    cross_out,
    bias,
    dest_shard,
    quot_row,
    rem_row,
    quot_slab,
    quot_accum,
    rem_table,
    rem_accum,
):
    contract = (((1,), (1,)), ((), ()))
    samples = features.shape[0]
    tables_dev = quot_slab.shape[0]
    row_width = quot_slab.shape[2]
    rem_rows = rem_table.shape[1]
    row_count = lax.axis_size("row")
    capacity = 3 * samples // (2 * row_count)
    slots = row_count * capacity
    product = (cotangent.astype(jnp.float32) * features.astype(jnp.float32)).astype(jnp.bfloat16)
    rank_left = jnp.dot(features, cross_in, preferred_element_type=jnp.float32)
    rank_right = jnp.dot(product, cross_out, preferred_element_type=jnp.float32)
    rank_left, rank_right = lax.psum((rank_left, rank_right), "table")
    cross_gate = (
        lax.dot_general(
            rank_left.astype(jnp.bfloat16), cross_out, contract, preferred_element_type=jnp.float32
        )
        + bias
    )
    cross_back = lax.dot_general(
        rank_right.astype(jnp.bfloat16), cross_in, contract, preferred_element_type=jnp.float32
    )
    pooled = (cotangent.astype(jnp.float32) * (cross_gate + 1.0) + cross_back).astype(jnp.bfloat16)
    pooled = pooled.reshape(samples, tables_dev, row_width)
    target = dest_shard[:, :, 0]
    onehot = target[:, :, None] == jnp.arange(row_count, dtype=jnp.int32)[None, None, :]
    lower = (
        jnp.arange(samples, dtype=jnp.int32)[:, None]
        >= jnp.arange(samples, dtype=jnp.int32)[None, :]
    ).astype(jnp.bfloat16)
    running = jnp.einsum(
        "ij,tjn->tin", lower, onehot.astype(jnp.bfloat16), preferred_element_type=jnp.float32
    )
    slot_index = jnp.sum(jnp.where(onehot, running, 0.0), axis=2).astype(jnp.int32) - 1
    position = target * capacity + slot_index
    placed = position[:, :, None] == jnp.arange(slots, dtype=jnp.int32)[None, None, :]
    send_rows = jnp.einsum(
        "tsk,ste->tke", placed.astype(jnp.bfloat16), pooled, preferred_element_type=jnp.float32
    ).astype(jnp.bfloat16)
    key_words = quot_row * rem_rows + rem_row
    send_keys = jnp.sum(jnp.where(placed, key_words[:, :, None], 0), axis=1)
    send_rows = send_rows.reshape(tables_dev, row_count, capacity, row_width)
    send_keys = send_keys.reshape(tables_dev, row_count, capacity)
    got_rows, got_keys = (
        lax.all_to_all(send_rows, "row", split_axis=1, concat_axis=1, tiled=True),
        lax.all_to_all(send_keys, "row", split_axis=1, concat_axis=1, tiled=True),
    )
    got_rows = got_rows.reshape(tables_dev, slots, row_width)
    got_keys = got_keys.reshape(tables_dev, slots)
    quot_grad, rem_grad = lax.map(table_grads, (got_rows, got_keys, quot_slab, rem_table))
    quot_acc_out = quot_accum + jnp.mean(quot_grad * quot_grad, axis=-1)
    quot_out = (
        quot_slab.astype(jnp.float32)
        - step_rate * quot_grad * lax.rsqrt(quot_acc_out + epsilon)[..., None]
    ).astype(jnp.bfloat16)
    share = rem_rows // row_count
    start = lax.axis_index("row") * share
    rem_total = lax.psum(rem_grad, "row")
    acc_all = rem_accum + jnp.mean(rem_total * rem_total, axis=-1)
    rem_out = (
        rem_table.astype(jnp.float32)
        - step_rate * rem_total * lax.rsqrt(acc_all + epsilon)[..., None]
    ).astype(jnp.bfloat16)
    rem_acc_out = lax.dynamic_slice_in_dim(acc_all, start, share, 1)
    return (quot_out, quot_acc_out, rem_out, rem_acc_out)


def solution(mesh):
    placed = (
        P("row", "table"),
        P("row", "table"),
        P("table", None),
        P("table", None),
        P("table"),
        P("table", "row", None),
        P("table", "row"),
        P("table", "row"),
        P("table", "row", None),
        P("table", "row"),
        P("table", None, None),
        P("table", None),
    )
    return jax.shard_map(
        per_device,
        mesh=mesh,
        in_specs=placed,
        out_specs=(
            P("table", "row", None),
            P("table", "row"),
            P("table", None, None),
            P("table", "row"),
        ),
        check_vma=False,
    )
```

profile of v0, /device:TPU:0, one launch (start us, length us, event | category | flops | bytes accessed | tf_op | source)
XLA Modules:
  0.0 384.6 jit_solution(17063767426417080916)
XLA Ops:
  12.3 8.2 %all-to-all-start = ((s32[16,1,384]{2,1,0:T(1,128)}), s32[16,1,384]{2,1,0:T(1,128)S(1)}, u32[]{:S(2)}, u32[]{:S(2)}) async-start(s32[16,1,384]{2,1,0:T(1,128)} %reshape.100), calls=%async_computation | async-start | bytes 49152 | tf_op jit(solution)/shard_map/all_to_all | solution.py:100
  20.5 2.4 fusion.31
  23.6 54.4 %all-reduce.5 = (bf16[512,512]{1,0:T(8,128)(2,1)}, bf16[512,512]{1,0:T(8,128)(2,1)}) all-reduce(f32[512,512]{1,0:T(8,128)S(1)} %fusion.41, f32[512,512]{1,0:T(8,128)S(1)} %fusion.31), channel_id=1, replica_groups=mesh['table'=8,'row'=16] {'table'}, use_global_device_ids=true, to_apply=%region_1.0 | all-reduce | flops 524288 | bytes 3145728 | tf_op jit(solution)/shard_map/psum | solution.py:67
  79.8 2.5 fusion.28
  85.8 6.9 %all-to-all-start.1 = ((bf16[8,16,48,128]{3,2,0,1:T(8,128)(2,1)}), bf16[8,16,48,128]{3,2,0,1:T(8,128)(2,1)S(1)}, u32[]{:S(2)}, u32[]{:S(2)}) async-start(bf16[8,16,48,128]{3,2,0,1:T(8,128)(2,1)} %copy.22), calls=%async_computation.1 | async-start | bytes 3145728 | tf_op jit(solution)/shard_map/all_to_all | solution.py:99
  94.4 20.0 %all-to-all-done.1 = bf16[8,16,48,128]{3,2,0,1:T(8,128)(2,1)S(1)} async-done(((bf16[8,16,48,128]{3,2,0,1:T(8,128)(2,1)}), bf16[8,16,48,128]{3,2,0,1:T(8,128)(2,1)S(1)}, u32[]{:S(2)}, u32[]{:S(2)}) %all-to-all-start.1) | async-done | bytes 1572896 | tf_op jit(solution)/shard_map/all_to_all | solution.py:99
  115.6 110.1 %while.14 = (s32[]{:T(128)}, f32[8,1024,128]{2,1,0:T(8,128)}, f32[8,2048,128]{2,1,0:T(8,128)}, s32[8,768]{1,0:T(8,128)S(1)}, bf16[8,768,128]{2,1,0:T(8,128)(2,1)...) while((s32[]{:T(128)}, f32[8,1024,128]{2,1,0:T(8,128)}, ...), condition=%wide.region_5.6_spmd, body=%wide.region_4.5_spmd.sunk | while | flops 4232984832 | bytes 4356185 | solution.py:104
  117.3 6.3 %fusion.67 = f32[8,2048,128]{2,1,0:T(8,128)} fusion(f32[8,2048,128]{2,1,0:T(8,128)} %get-tuple-element.178, s32[]{:T(128)} %get-tuple-element.176, f32[768,128]{1,0:T(8,128)S(1)} %fusion.66, s32[768]{0:T(1024)S(1)} %get-tuple-element.166), kind=kOutput, calls=%fused_computation.9.clone.1 | convolution fusion | flops 2417491968 | bytes 1445376 | tf_op jit(solution)/shard_map/while/body/eval_jaxpr/dot_general | solution.py:32
  123.6 2.2 fusion.64
  125.9 3.6 fusion.65
  131.2 6.2 %fusion.67 = f32[8,2048,128]{2,1,0:T(8,128)} fusion(f32[8,2048,128]{2,1,0:T(8,128)} %get-tuple-element.178, s32[]{:T(128)} %get-tuple-element.176, f32[768,128]{1,0:T(8,128)S(1)} %fusion.66, s32[768]{0:T(1024)S(1)} %get-tuple-element.166), kind=kOutput, calls=%fused_computation.9.clone.1 | convolution fusion | flops 2417491968 | bytes 1445376 | tf_op jit(solution)/shard_map/while/body/eval_jaxpr/dot_general | solution.py:32
  137.3 2.3 fusion.64
  139.6 3.6 fusion.65
  144.9 6.2 %fusion.67 = f32[8,2048,128]{2,1,0:T(8,128)} fusion(f32[8,2048,128]{2,1,0:T(8,128)} %get-tuple-element.178, s32[]{:T(128)} %get-tuple-element.176, f32[768,128]{1,0:T(8,128)S(1)} %fusion.66, s32[768]{0:T(1024)S(1)} %get-tuple-element.166), kind=kOutput, calls=%fused_computation.9.clone.1 | convolution fusion | flops 2417491968 | bytes 1445376 | tf_op jit(solution)/shard_map/while/body/eval_jaxpr/dot_general | solution.py:32
  153.3 3.6 fusion.65
  158.6 6.2 %fusion.67 = f32[8,2048,128]{2,1,0:T(8,128)} fusion(f32[8,2048,128]{2,1,0:T(8,128)} %get-tuple-element.178, s32[]{:T(128)} %get-tuple-element.176, f32[768,128]{1,0:T(8,128)S(1)} %fusion.66, s32[768]{0:T(1024)S(1)} %get-tuple-element.166), kind=kOutput, calls=%fused_computation.9.clone.1 | convolution fusion | flops 2417491968 | bytes 1445376 | tf_op jit(solution)/shard_map/while/body/eval_jaxpr/dot_general | solution.py:32
  167.1 3.6 fusion.65
  172.4 6.3 %fusion.67 = f32[8,2048,128]{2,1,0:T(8,128)} fusion(f32[8,2048,128]{2,1,0:T(8,128)} %get-tuple-element.178, s32[]{:T(128)} %get-tuple-element.176, f32[768,128]{1,0:T(8,128)S(1)} %fusion.66, s32[768]{0:T(1024)S(1)} %get-tuple-element.166), kind=kOutput, calls=%fused_computation.9.clone.1 | convolution fusion | flops 2417491968 | bytes 1445376 | tf_op jit(solution)/shard_map/while/body/eval_jaxpr/dot_general | solution.py:32
  180.9 3.6 fusion.65
  186.2 6.2 %fusion.67 = f32[8,2048,128]{2,1,0:T(8,128)} fusion(f32[8,2048,128]{2,1,0:T(8,128)} %get-tuple-element.178, s32[]{:T(128)} %get-tuple-element.176, f32[768,128]{1,0:T(8,128)S(1)} %fusion.66, s32[768]{0:T(1024)S(1)} %get-tuple-element.166), kind=kOutput, calls=%fused_computation.9.clone.1 | convolution fusion | flops 2417491968 | bytes 1445376 | tf_op jit(solution)/shard_map/while/body/eval_jaxpr/dot_general | solution.py:32
  192.3 2.3 fusion.64
  194.6 3.6 fusion.65
  199.9 6.2 %fusion.67 = f32[8,2048,128]{2,1,0:T(8,128)} fusion(f32[8,2048,128]{2,1,0:T(8,128)} %get-tuple-element.178, s32[]{:T(128)} %get-tuple-element.176, f32[768,128]{1,0:T(8,128)S(1)} %fusion.66, s32[768]{0:T(1024)S(1)} %get-tuple-element.166), kind=kOutput, calls=%fused_computation.9.clone.1 | convolution fusion | flops 2417491968 | bytes 1445376 | tf_op jit(solution)/shard_map/while/body/eval_jaxpr/dot_general | solution.py:32
  208.3 3.6 fusion.65
  213.6 6.2 %fusion.67 = f32[8,2048,128]{2,1,0:T(8,128)} fusion(f32[8,2048,128]{2,1,0:T(8,128)} %get-tuple-element.178, s32[]{:T(128)} %get-tuple-element.176, f32[768,128]{1,0:T(8,128)S(1)} %fusion.66, s32[768]{0:T(1024)S(1)} %get-tuple-element.166), kind=kOutput, calls=%fused_computation.9.clone.1 | convolution fusion | flops 2417491968 | bytes 1445376 | tf_op jit(solution)/shard_map/while/body/eval_jaxpr/dot_general | solution.py:32
  219.8 2.3 fusion.64
  222.1 3.6 fusion.65
  225.7 3.5 multiply_reduce_fusion.1
  229.8 4.1 %subtract_convert_fusion.1 = bf16[8,1024,128]{2,1,0:T(8,128)(2,1)} fusion(f32[8,1024,128]{2,1,0:T(8,128)} %get-tuple-element.97, bf16[8,1024,128]{2,1,0:T(8,128)(2,1)S(1)} %copy-done.2, f32[8,1024]{1,0:T(8,128)S(1)} %get-tuple-element.117), kind=kLoop, calls=%fused_computation.37 | loop fusion | flops 4194304 | bytes 8421376 | tf_op jit(solution)/shard_map/convert_element_type | solution.py:109
  233.9 131.6 %all-reduce.4.cloned.1.call-done = f32[8,2048,128]{2,1,0:T(8,128)} async-done(((f32[8,2048,128]{2,1,0:T(8,128)}), f32[8,2048,128]{2,1,0:T(8,128)}) %all-reduce.4.cloned.1.call-update) | async-done | bytes 8388624 | tf_op jit(solution)/shard_map/psum | solution.py:112
  365.5 5.8 %multiply_reduce_fusion = f32[8,2048]{1,0:T(8,128)S(1)} fusion(f32[8,2048,128]{2,1,0:T(8,128)} %all-reduce.4.cloned.1.call-done), kind=kLoop, calls=%fused_computation.35 | loop fusion | flops 4177920 | bytes 8454144 | tf_op jit(solution)/shard_map/reduce_sum | solution.py:113
  372.0 5.8 %subtract_convert_fusion = bf16[8,2048,128]{2,1,0:T(8,128)(2,1)} fusion(f32[8,2048,128]{2,1,0:T(8,128)S(1)} %copy-done.1, bf16[8,2048,128]{2,1,0:T(8,128)(2,1)} %get-tuple-element.197, f32[8,2048]{1,0:T(8,128)S(1)} %get-tuple-element.115), kind=kLoop, calls=%fused_computation.34 | loop fusion | flops 8388608 | bytes 16842752 | tf_op jit(solution)/shard_map/convert_element_type | solution.py:117
  (72 shorter events, 38.0 us)
Async XLA Ops:
  7.2 13.3 %copy-start = (bf16[1024,512]{1,0:T(8,128)(2,1)S(1)}, bf16[1024,512]{1,0:T(8,128)(2,1)}, u32[]{:S(2)}) copy-start(bf16[1024,512]{1,0:T(8,128)(2,1)} %param.17) | copy-start | bytes 3145732
  12.3 73.5 %all-to-all-start = ((s32[16,1,384]{2,1,0:T(1,128)}), s32[16,1,384]{2,1,0:T(1,128)S(1)}, u32[]{:S(2)}, u32[]{:S(2)}) async-start(s32[16,1,384]{2,1,0:T(1,128)} %reshape.100), calls=%async_computation | async-start | bytes 49152 | tf_op jit(solution)/shard_map/all_to_all | solution.py:100
  20.5 2.4 copy-start.3
  20.5 2.4 copy-start.6
  22.9 56.9 %copy-start.7 = (f32[1024]{0:T(1024)S(1)}, f32[1024]{0:T(1024)}, u32[]{:S(2)}) copy-start(f32[1024]{0:T(1024)} %param.18) | copy-start | bytes 12292
  85.8 28.6 %all-to-all-start.1 = ((bf16[8,16,48,128]{3,2,0,1:T(8,128)(2,1)}), bf16[8,16,48,128]{3,2,0,1:T(8,128)(2,1)S(1)}, u32[]{:S(2)}, u32[]{:S(2)}) async-start(bf16[8,16,48,128]{3,2,0,1:T(8,128)(2,1)} %copy.22), calls=%async_computation.1 | async-start | bytes 3145728 | tf_op jit(solution)/shard_map/all_to_all | solution.py:99
  92.7 272.8 %all-reduce.4.cloned.1.call-start = ((), (), s32[]{:S(2)}) async-start(), calls=%async_computation.2 | async-start | bytes 16777216 | tf_op jit(solution)/shard_map/psum | solution.py:112
  225.7 3.5 copy-start.5
  225.7 4.1 %copy-start.2 = (bf16[8,1024,128]{2,1,0:T(8,128)(2,1)S(1)}, bf16[8,1024,128]{2,1,0:T(8,128)(2,1)}, u32[]{:S(2)}) copy-start(bf16[8,1024,128]{2,1,0:T(8,128)(2,1)} %get-tuple-element.198) | copy-start | bytes 6291460
  233.9 137.4 %copy-start.4 = (f32[8,2048]{1,0:T(8,128)S(1)}, f32[8,2048]{1,0:T(8,128)}, u32[]{:S(2)}) copy-start(f32[8,2048]{1,0:T(8,128)} %param.25) | copy-start | bytes 196612
  365.5 6.4 %copy-start.1 = (f32[8,2048,128]{2,1,0:T(8,128)S(1)}, f32[8,2048,128]{2,1,0:T(8,128)}, u32[]{:S(2)}) copy-start(f32[8,2048,128]{2,1,0:T(8,128)} %all-reduce.4.cloned.1.call-done) | copy-start | bytes 25165828
Sparse Core Ops, SparseCore 0:
  225.8 139.6 all-reduce.3
where the time goes:
time: 386 us; the launch traced here: 385 us
  waiting for transfers between devices  152 us (39%)
  matrix products  120 us (31%)
  blocking collectives  54.4 us (14%)
  other arithmetic  23.7 us (6%)
  starting transfers between devices  15.3 us (4%)
  between operations  14.3 us (4%)
  local copies, waits for them, and re-layouts  5.69 us (1%)
    psum x1, waiting for transfers between devices, per_device(): rem_total = lax.psum(rem_grad, 'row')  132 us
    psum x1, blocking collectives, per_device(): rank_left, rank_right = lax.psum((rank_left, rank_right), 'table')  54.4 us
    dot_general x8, matrix products, table_grads(): lax.dot_general(r_hot.astype(jnp.float32), grad_f * quot_pick, over_rows,...  49.7 us
    dot_general x8, matrix products, table_grads(): lax.dot_general(q_hot.astype(jnp.float32), grad_f * rem_pick, over_rows,...  28.4 us
    all_to_all x1, waiting for transfers between devices, per_device(): lax.all_to_all(send_rows, 'row', split_axis=1, concat_axis=1, tiled=True)  20 us
    dot_general x8, matrix products, table_grads(): rem_pick = jnp.dot(r_hot, rtab, preferred_element_type=jnp.float32)  18 us
    dot_general x8, matrix products, table_grads(): quot_pick = jnp.dot(q_hot, slab, preferred_element_type=jnp.float32)  13.6 us
    all_to_all x1, starting transfers between devices, per_device(): lax.all_to_all(send_keys, 'row', split_axis=1, concat_axis=1, tiled=True)  8.16 us
  transfers between devices with their start and end apart: 3, of which 2 were waited for; matrix products, arithmetic and copies ran while one was open for 5% of the time, Pallas kernels for 0%

commit v1 on v0

v1 whole, which is shorter than its diff:
```python
import functools

import jax
import jax.numpy as jnp
from jax import lax
from jax.experimental import pallas as pl
from jax.experimental.pallas import tpu as pltpu
from jax.sharding import Mesh
from jax.sharding import PartitionSpec as P

step_rate = 0.3
epsilon = 1e-06
bf = jnp.bfloat16
f32 = jnp.float32
NX, NC, NZ, NY = 4, 2, 4, 4
CZY = ("c", "z", "y")
NT = (((1,), (1,)), ((), ()))


def ring(n, s):
    return [(i, (i + s) % n) for i in range(n)]


def spot(c, z, y):
    return (c * NZ + z) * NY + y


def turn_pairs(s, flip):
    out = []
    for c in range(NC):
        for z in range(NZ):
            for y in range(NY):
                if (c == 0) != flip:
                    to = spot(c, (z + s) % NZ, y)
                else:
                    to = spot(c, z, (y + s) % NY)
                out.append((spot(c, z, y), to))
    return out


def turn_groups(flip):
    out = []
    for c in range(NC):
        if (c == 0) != flip:
            out += [[spot(c, z, y) for z in range(NZ)] for y in range(NY)]
        else:
            out += [[spot(c, z, y) for y in range(NY)] for z in range(NZ)]
    return out


def pooled_kernel(rank_ref, cot_ref, co_ref, ci_ref, bias_ref, pos_ref, out_ref):
    rank = co_ref.shape[1]
    dests, tables, cap, width = out_ref.shape
    samples = cot_ref.shape[0]
    gate = (
        lax.dot_general(rank_ref[:, :rank], co_ref[...], NT, preferred_element_type=f32)
        + bias_ref[...]
    )
    back = lax.dot_general(rank_ref[:, rank:], ci_ref[...], NT, preferred_element_type=f32)
    pooled = (cot_ref[...].astype(f32) * (gate + 1.0) + back).astype(bf)
    slot = lax.broadcasted_iota(jnp.int32, (dests * cap, samples), 0)
    for t in range(tables):
        placed = jnp.where(slot == pos_ref[t], 1.0, 0.0).astype(bf)
        rows = jnp.dot(
            placed, pooled[:, t * width : (t + 1) * width], preferred_element_type=f32
        ).astype(bf)
        out_ref[:, t] = rows.reshape(dests, cap, width)


def pooled_dispatch(rank, cot, co, ci, bias, pos, dests, cap, width):
    samples = cot.shape[0]
    tables = pos.shape[0]
    pair = 2
    return pl.pallas_call(
        pooled_kernel,
        grid=(tables // pair,),
        out_shape=jax.ShapeDtypeStruct((dests, tables, cap, width), bf),
        in_specs=[
            pl.BlockSpec(rank.shape, lambda i: (0, 0)),
            pl.BlockSpec((samples, pair * width), lambda i: (0, i)),
            pl.BlockSpec((pair * width, co.shape[1]), lambda i: (i, 0)),
            pl.BlockSpec((pair * width, co.shape[1]), lambda i: (i, 0)),
            pl.BlockSpec((1, pair * width), lambda i: (0, i)),
            pl.BlockSpec((pair, 1, samples), lambda i: (i, 0, 0)),
        ],
        out_specs=pl.BlockSpec((dests, pair, cap, width), lambda i: (0, i, 0, 0)),
        name="pooled_dispatch",
    )(rank, cot, co, ci, bias, pos)


def table_kernel(core_ref, g_ref, krow_ref, kcol_ref, slab_ref, rtab_ref, rem_ref, quot_ref):
    sources, _, cap, width = g_ref.shape
    slots = sources * cap
    rem_rows = rtab_ref.shape[1]
    quot_rows = slab_ref.shape[1]
    rem_half = rem_rows // 2
    quot_half = quot_rows // 2
    g = g_ref[:, 0].reshape(slots, width).astype(f32)
    kcol = kcol_ref[0]
    krow = krow_ref[0]
    m_col, q_col = kcol % rem_rows, kcol // rem_rows
    m_row, q_row = krow % rem_rows, krow // rem_rows

    def pick(col, half, tab):
        hot = jnp.where(
            lax.broadcasted_iota(jnp.int32, (slots, half), 1) == col % half, 1.0, 0.0
        ).astype(bf)
        both = jnp.concatenate([tab[:half], tab[half:]], axis=1)
        got = jnp.dot(hot, both, preferred_element_type=f32)
        return jnp.where(col >= half, got[:, width:], got[:, :width])

    def spread(row, col, half, val):
        hot = jnp.where(
            lax.broadcasted_iota(jnp.int32, (half, slots), 0) == row % half, 1.0, 0.0
        ).astype(bf)
        both = jnp.concatenate(
            [jnp.where(col < half, val, 0.0), jnp.where(col >= half, val, 0.0)], axis=1
        ).astype(bf)
        return jnp.dot(hot, both, preferred_element_type=f32)

    quot_pick = pick(q_col, quot_half, slab_ref[0])
    rem_sum = spread(m_row, m_col, rem_half, g * quot_pick)
    first = core_ref[0] == 0
    sub_rows = rem_ref.shape[3]
    for z in range(NZ):
        for y in range(NY):
            start = (z * NY + y) * sub_rows
            at = start % rem_half
            side = start // rem_half
            block = rem_sum[at : at + sub_rows, side * width : (side + 1) * width]
            rem_ref[jnp.where(first, z, y), 0, jnp.where(first, y, z)] = block.astype(bf)
    rem_pick = pick(m_col, rem_half, rtab_ref[0])
    quot_sum = spread(q_row, q_col, quot_half, g * rem_pick)
    quot_ref[0, :quot_half] = quot_sum[:, :width]
    quot_ref[0, quot_half:] = quot_sum[:, width:]


def table_grads(core, g, keys, slab, rtab):
    sources, tables, cap, width = g.shape
    slots = sources * cap
    quot_rows, rem_rows = slab.shape[1], rtab.shape[1]
    sub = rem_rows // (NZ * NY)
    return pl.pallas_call(
        table_kernel,
        out_shape=(
            jax.ShapeDtypeStruct((NZ, tables, NY, sub, width), bf),
            jax.ShapeDtypeStruct((tables, quot_rows, width), f32),
        ),
        grid_spec=pltpu.PrefetchScalarGridSpec(
            num_scalar_prefetch=1,
            grid=(tables,),
            in_specs=[
                pl.BlockSpec((sources, 1, cap, width), lambda t, c: (0, t, 0, 0)),
                pl.BlockSpec((1, 1, slots), lambda t, c: (t, 0, 0)),
                pl.BlockSpec((1, slots, 1), lambda t, c: (t, 0, 0)),
                pl.BlockSpec((1, quot_rows, width), lambda t, c: (t, 0, 0)),
                pl.BlockSpec((1, rem_rows, width), lambda t, c: (t, 0, 0)),
            ],
            out_specs=(
                pl.BlockSpec((NZ, 1, NY, sub, width), lambda t, c: (0, t, 0, 0, 0)),
                pl.BlockSpec((1, quot_rows, width), lambda t, c: (t, 0, 0)),
            ),
        ),
        name="table_grads",
    )(core, g, keys.reshape(tables, 1, slots), keys.reshape(tables, slots, 1), slab, rtab)


def rank_sums(part):
    ci = lax.axis_index("c")
    xi = lax.axis_index("x")
    swap = [(0, 1), (1, 0)]
    half = part.shape[0] // NC
    size = half // NX
    keep = lax.dynamic_slice_in_dim(part, ci * half, half, 0)
    give = lax.dynamic_slice_in_dim(part, (1 - ci) * half, half, 0).astype(bf)
    got = lax.ppermute(give, "c", swap)
    both = (keep + got.astype(f32)).astype(bf).reshape(NX, size, -1)
    take = lambda k: lax.dynamic_index_in_dim(both, (xi + k) % NX, 0, keepdims=False)
    total = take(0).astype(f32)
    for k in (2, 1, 3):
        total = total + lax.ppermute(take(k), "x", ring(NX, k)).astype(f32)
    mine = total.astype(bf)
    parts = jnp.zeros_like(both)
    parts = lax.dynamic_update_index_in_dim(parts, mine, xi, 0)
    for k in (2, 1, 3):
        parts = lax.dynamic_update_index_in_dim(
            parts, lax.ppermute(mine, "x", ring(NX, k)), (xi - k) % NX, 0
        )
    own = parts.reshape(half, -1)
    other = lax.ppermute(own, "c", swap)
    low = jnp.where(ci == 0, own, other)
    high = jnp.where(ci == 0, other, own)
    return jnp.concatenate([low, high], axis=0)


def ring_gather(a, flip):
    ci = lax.axis_index("c")
    along_z = (ci == 0) != flip
    at = jnp.where(along_z, lax.axis_index("z"), lax.axis_index("y"))
    n = a.shape[0] // 2
    left = lax.ppermute(a, CZY, turn_pairs(1, flip))
    right = lax.ppermute(a, CZY, turn_pairs(-1, flip))
    far_low = lax.ppermute(left[:n], CZY, turn_pairs(1, flip))
    far_high = lax.ppermute(right[n:], CZY, turn_pairs(-1, flip))
    out = jnp.zeros((4,) + a.shape, a.dtype)
    out = lax.dynamic_update_index_in_dim(out, a, at, 0)
    out = lax.dynamic_update_index_in_dim(out, left, (at + 3) % 4, 0)
    out = lax.dynamic_update_index_in_dim(out, right, (at + 1) % 4, 0)
    zeros = (0,) * (a.ndim - 1)
    out = lax.dynamic_update_slice(out, far_low[None], ((at + 2) % 4, 0) + zeros)
    out = lax.dynamic_update_slice(out, far_high[None], ((at + 2) % 4, n) + zeros)
    return out


def per_device(
    features, cotangent, cross_in, cross_out, bias, dest_shard, quot_row, rem_row,
    quot_slab, quot_accum, rem_table, rem_accum,
):
    samples = features.shape[0]
    tables = quot_slab.shape[0]
    width = quot_slab.shape[2]
    rem_rows = rem_table.shape[1]
    rows = NZ * NY
    cap = 3 * samples // (2 * rows)
    slots = rows * cap
    ci, zi, yi = lax.axis_index("c"), lax.axis_index("z"), lax.axis_index("y")

    target = dest_shard[:, :, 0]
    onehot = target[:, :, None] == jnp.arange(rows, dtype=jnp.int32)[None, None, :]
    lower = (
        jnp.arange(samples, dtype=jnp.int32)[:, None]
        >= jnp.arange(samples, dtype=jnp.int32)[None, :]
    ).astype(bf)
    running = jnp.einsum("ij,tjn->tin", lower, onehot.astype(bf), preferred_element_type=f32)
    slot_index = jnp.sum(jnp.where(onehot, running, 0.0), axis=2).astype(jnp.int32) - 1
    position = target * cap + slot_index
    placed = position[:, :, None] == jnp.arange(slots, dtype=jnp.int32)[None, None, :]
    key_words = quot_row * rem_rows + rem_row
    send_keys = jnp.sum(jnp.where(placed, key_words[:, :, None], 0), axis=1)
    send_keys = send_keys.reshape(tables, rows, cap)
    got_keys = lax.all_to_all(send_keys, ("z", "y"), split_axis=1, concat_axis=1, tiled=True)
    got_keys = got_keys.reshape(tables, slots)

    product = (cotangent.astype(f32) * features.astype(f32)).astype(bf)
    part = jnp.concatenate(
        [
            jnp.dot(features, cross_in, preferred_element_type=f32),
            jnp.dot(product, cross_out, preferred_element_type=f32),
        ],
        axis=1,
    )
    rank = rank_sums(part)

    send = pooled_dispatch(
        rank, cotangent, cross_out, cross_in, bias.reshape(1, -1),
        position.reshape(tables, 1, samples), rows, cap, width,
    )
    got = lax.all_to_all(send, ("z", "y"), split_axis=0, concat_axis=0, tiled=True)
    rem_part, quot_grad = table_grads(ci.reshape(1), got, got_keys, quot_slab, rem_table)

    one = lax.all_to_all(
        rem_part, CZY, 0, 0, tiled=True, axis_index_groups=turn_groups(False)
    )
    one = jnp.sum(one.astype(f32), axis=0).astype(bf)
    two = lax.all_to_all(
        one.transpose(1, 0, 2, 3), CZY, 0, 0, tiled=True, axis_index_groups=turn_groups(True)
    )
    rem_grad = jnp.sum(two.astype(f32), axis=0)
    share = rem_rows // rows
    start = (zi * NY + yi) * share
    acc_in = lax.dynamic_slice_in_dim(rem_accum, start, share, 1)
    tab_in = lax.dynamic_slice_in_dim(rem_table, start, share, 1)
    rem_acc_out = acc_in + jnp.mean(rem_grad * rem_grad, axis=-1)
    rem_new = (
        tab_in.astype(f32) - step_rate * rem_grad * lax.rsqrt(rem_acc_out + epsilon)[..., None]
    ).astype(bf)
    four = ring_gather(rem_new, True)
    full = ring_gather(four.transpose(1, 0, 2, 3), False)
    rem_out = jnp.where(ci == 0, full.transpose(1, 0, 2, 3, 4), full.transpose(1, 2, 0, 3, 4))
    rem_out = rem_out.reshape(tables, rem_rows, width)

    quot_acc_out = quot_accum + jnp.mean(quot_grad * quot_grad, axis=-1)
    quot_out = (
        quot_slab.astype(f32)
        - step_rate * quot_grad * lax.rsqrt(quot_acc_out + epsilon)[..., None]
    ).astype(bf)
    return (quot_out, quot_acc_out, rem_out, rem_acc_out)


def solution(mesh):
    fine = Mesh(mesh.devices.reshape(NX, NC, NZ, NY), ("x", "c", "z", "y"))
    T, R = ("x", "c"), ("z", "y")
    return jax.shard_map(
        per_device,
        mesh=fine,
        in_specs=(
            P(R, T), P(R, T), P(T, None), P(T, None), P(T), P(T, R, None), P(T, R), P(T, R),
            P(T, R, None), P(T, R), P(T, None, None), P(T, None),
        ),
        out_specs=(P(T, R, None), P(T, R), P(T, None, None), P(T, R)),
        check_vma=False,
    )
```

time: 386 us -> 204 us (0.53)
  matrix products: 120 us -> 5.24 us
  waiting for transfers between devices: 152 us -> 58.7 us
  starting transfers between devices: 15.3 us -> 44.3 us
  Pallas kernels: 0 us -> 26.6 us
  blocking collectives: 54.4 us -> 33.4 us
  between operations: 14.3 us -> 1.22 us
  local copies, waits for them, and re-layouts: 5.69 us -> 11.9 us
    psum x1 -> x0, waiting for transfers between devices: 132 us -> none  [per_device(): rem_total = lax.psum(rem_grad, 'row')]
    dot_general x38 -> x3, matrix products: 120 us -> 5.24 us  [the longest x1 2.64 us: per_device(): jnp.dot(product, cross_out, preferred_element_type=f32)]
    psum x1 -> x0, blocking collectives: 54.4 us -> none  [per_device(): rank_left, rank_right = lax.psum((rank_left, rank_right), 'table')]
    all_to_all x0 -> x1, blocking collectives: none -> 33.4 us  [per_device(): lax.all_to_all(rem_part, CZY, 0, 0, tiled=True, axis_index_groups=turn_gr...]
    ppermute x0 -> x16, waiting for transfers between devices: none -> 28.7 us  [the longest x2 9.93 us: ring_gather(): left = lax.ppermute(a, CZY, turn_pairs(1, flip))]
    pallas_call x0 -> x2, Pallas kernels: none -> 26.6 us  [the longest x1 19.9 us: table_grads(): pl.pallas_call(table_kernel, out_shape=(jax.ShapeDtypeStruct((NZ, tables,...]
    ppermute x0 -> x16, starting transfers between devices: none -> 25.3 us  [the longest x2 6.59 us: ring_gather(): far_high = lax.ppermute(right[n:], CZY, turn_pairs(-1, flip))]
    all_to_all x2 -> x3, waiting for transfers between devices: 20 us -> 30 us  [the longest x1 19.3 us: per_device(): lax.all_to_all(send, ('z', 'y'), split_axis=0, concat_axis=0, tiled=True)]
  transfers between devices with their start and end apart: 3 -> 19, of which waited for: 2 -> 12; matrix products, arithmetic and copies ran while one was open for 5% -> 10% of each run, Pallas kernels for 0% -> 3%
where the time goes in v1:
time: 204 us; the launch traced here: 202 us
  waiting for transfers between devices  58.7 us (29%)
  starting transfers between devices  44.3 us (22%)
  blocking collectives  33.4 us (16%)
  Pallas kernels  26.6 us (13%)
  other arithmetic  20.9 us (10%)
  local copies, waits for them, and re-layouts  11.9 us (6%)
  matrix products  5.24 us (3%)
    all_to_all x1, blocking collectives, per_device(): lax.all_to_all(rem_part, CZY, 0, 0, tiled=True, axis_index_groups=turn_gr...  33.4 us
    pallas_call x1, Pallas kernels, table_grads(): pl.pallas_call(table_kernel, out_shape=(jax.ShapeDtypeStruct((NZ, tables,...  19.9 us
    all_to_all x1, waiting for transfers between devices, per_device(): lax.all_to_all(send, ('z', 'y'), split_axis=0, concat_axis=0, tiled=True)  19.3 us
    all_to_all x1, waiting for transfers between devices, per_device(): lax.all_to_all(one.transpose(1, 0, 2, 3), CZY, 0, 0, tiled=True, axis_ind...  10.7 us
    ppermute x2, waiting for transfers between devices, ring_gather(): left = lax.ppermute(a, CZY, turn_pairs(1, flip))  9.93 us
    ppermute x2, waiting for transfers between devices, ring_gather(): far_low = lax.ppermute(left[:n], CZY, turn_pairs(1, flip))  9.04 us
    all_to_all x1, starting transfers between devices, per_device(): lax.all_to_all(send_keys, ('z', 'y'), split_axis=1, concat_axis=1, tiled=...  8.1 us
    all_to_all x1, starting transfers between devices, per_device(): lax.all_to_all(send, ('z', 'y'), split_axis=0, concat_axis=0, tiled=True)  7.21 us
  transfers between devices with their start and end apart: 19, of which 12 were waited for; matrix products, arithmetic and copies ran while one was open for 10% of the time, Pallas kernels for 3%

profile of v1, /device:TPU:0, one launch (start us, length us, event | category | flops | bytes accessed | tf_op | source)
XLA Modules:
  0.0 202.2 jit_solution(14098399534184920824)
XLA Ops:
  0.6 2.3 %fusion.19 = f32[512,512]{0,1:T(8,128)S(1)} fusion(bf16[512,1024]{1,0:T(8,128)(2,1)} %param.12, bf16[1024,512]{1,0:T(8,128)(2,1)} %ci_ref.1), kind=kOutput, calls=%fused_computation.64 | convolution fusion | flops 536870912 | bytes 3145728 | tf_op jit(solution)/shard_map/dot_general | solution.py:247
  3.0 2.6 %fusion.2 = f32[512,512]{0,1:T(8,128)S(1)} fusion(bf16[1024,512]{1,0:T(8,128)(2,1)} %co_ref.1, bf16[512,1024]{1,0:T(8,128)(2,1)} %param.12, bf16[512,1024]{1,0:T(8,128)(2,1)} %cot_ref.1), kind=kOutput, calls=%fused_computation.14 | convolution fusion | flops 538968064 | bytes 4194304 | tf_op jit(solution)/shard_map/dot_general | solution.py:248
  8.1 3.2 %collective-permute-start.1 = (bf16[64,1024]{1,0:T(8,128)(2,1)S(1)}, bf16[64,1024]{1,0:T(8,128)(2,1)S(1)}, u32[]{:S(2)}, u32[]{:S(2)}) collective-permute-start(bf16[64,1024]{1,0:T(8,128)(2,1)S(1)} %get-tuple-element.18), channel_id=1, source_target_pairs={{0,64},{32,96},{64,0},{96,32},{1,65},{33,97},{65,1},{97,33},{2,66}... | collective-permute-start | bytes 393224 | tf_op jit(solution)/shard_map/ppermute | solution.py:181
  11.9 2.6 %collective-permute-start.3 = (bf16[64,1024]{1,0:T(8,128)(2,1)S(1)}, bf16[64,1024]{1,0:T(8,128)(2,1)S(1)}, u32[]{:S(2)}, u32[]{:S(2)}) collective-permute-start(bf16[64,1024]{1,0:T(8,128)(2,1)S(1)} %get-tuple-element.19), channel_id=1, source_target_pairs={{0,96},{32,0},{64,32},{96,64},{1,97},{33,1},{65,33},{97,65},{2,98}... | collective-permute-start | bytes 393224 | tf_op jit(solution)/shard_map/ppermute | solution.py:181
  16.1 2.3 %collective-permute-done.2 = bf16[64,1024]{1,0:T(8,128)(2,1)S(1)} collective-permute-done((bf16[64,1024]{1,0:T(8,128)(2,1)S(1)}, bf16[64,1024]{1,0:T(8,128)(2,1)S(1)}, u32[]{:S(2)}, u32[]{:S(2)}) %collective-permute-start.2) | collective-permute-done | bytes 131104 | tf_op jit(solution)/shard_map/ppermute | solution.py:181
  18.5 2.1 %collective-permute-start.4 = (bf16[64,1024]{1,0:T(8,128)(2,1)S(1)}, bf16[64,1024]{1,0:T(8,128)(2,1)S(1)}, u32[]{:S(2)}, u32[]{:S(2)}) collective-permute-start(bf16[64,1024]{1,0:T(8,128)(2,1)S(1)} %get-tuple-element.15), channel_id=1, source_target_pairs={{0,64},{32,96},{64,0},{96,32},{1,65},{33,97},{65,1},{97,33},{2,66}... | collective-permute-start | bytes 393224 | tf_op jit(solution)/shard_map/ppermute | solution.py:187
  20.6 1.8 collective-permute-start.5
  23.9 1.8 collective-permute-done.4
  25.7 2.1 %collective-permute-done.5 = bf16[64,1024]{1,0:T(8,128)(2,1)S(1)} collective-permute-done((bf16[64,1024]{1,0:T(8,128)(2,1)S(1)}, bf16[64,1024]{1,0:T(8,128)(2,1)S(1)}, u32[]{:S(2)}, u32[]{:S(2)}) %collective-permute-start.5) | collective-permute-done | bytes 131104 | tf_op jit(solution)/shard_map/ppermute | solution.py:187
  28.0 1.7 select_reduce_fusion
  30.6 8.1 %all-to-all-start.1 = ((s32[16,1,384]{2,1,0:T(1,128)}), s32[16,1,384]{2,1,0:T(1,128)S(1)}, u32[]{:S(2)}, u32[]{:S(2)}) async-start(s32[16,1,384]{2,1,0:T(1,128)} %reshape.81), calls=%async_computation.1 | async-start | bytes 49152 | tf_op jit(solution)/shard_map/all_to_all | solution.py:241
  40.5 6.7 %pooled_dispatch.1 = bf16[16,8,48,128]{3,2,1,0:T(8,128)(2,1)} custom-call(bf16[512,1024]{1,0:T(8,128)(2,1)} %pad_maximum_fusion.rank_ref, bf16[512,1024]{1,0:T(8,128)(2,1)} %cot_ref.1, bf16[1024,512]{1,0:T(8,128)(2,1)} %co_ref.1, bf16[1024,512]{1,0:T(8,128)(2,1)} %ci_ref.1, f32[1,1024]{1,0:T(1,128)} %bitcast.108, s32[8,1,512]{2,1,0:T(1,128)} %copy_add_fusion.pos_ref), custom_call_target="tpu_custom_call" | custom-call | tf_op jit(solution)/shard_map/pooled_dispatch/pallas_call | solution.py:74
  47.2 7.2 %all-to-all-start = ((bf16[16,8,48,128]{3,2,1,0:T(8,128)(2,1)}), bf16[16,8,48,128]{3,2,1,0:T(8,128)(2,1)S(1)}, u32[]{:S(2)}, u32[]{:S(2)}) async-start(bf16[16,8,48,128]{3,2,1,0:T(8,128)(2,1)} %pooled_dispatch.1), calls=%async_computation | async-start | bytes 3145728 | tf_op jit(solution)/shard_map/all_to_all | solution.py:258
  55.7 3.3 %reshape_reshape.8.kcol_ref = s32[8,768,1]{2,1,0:T(8,128)} reshape(s32[8,16,48]{2,1,0:T(8,128)S(1)} %copy.101) | data formatting | bytes 49152 | tf_op jit(solution)/shard_map/reshape;reshape | solution.py:165
  59.8 19.3 %all-to-all-done.g_ref = bf16[16,8,48,128]{3,2,1,0:T(8,128)(2,1)S(1)} async-done(((bf16[16,8,48,128]{3,2,1,0:T(8,128)(2,1)}), bf16[16,8,48,128]{3,2,1,0:T(8,128)(2,1)S(1)}, u32[]{:S(2)}, u32[]{:S(2)}) %all-to-all-start) | async-done | bytes 1572896 | tf_op jit(solution)/shard_map/all_to_all | solution.py:258
  80.2 19.9 %table_grads.1 = (bf16[4,8,4,128,128]{4,3,2,1,0:T(8,128)(2,1)}, f32[8,1024,128]{2,1,0:T(8,128)}) custom-call(s32[1]{0:T(128)} %bitcast.core_ref, bf16[16,8,48,128]{3,2,1,0:T(8,128)(2,1)} %copy-done.2, s32[8,1,768]{2,1,0:T(1,128)} %reshape_reshape.6.krow_ref, s32[8,768,1]{2,1,0:T(8,128)} %reshape_reshape.8.kcol_ref, bf16[8,1024,128]{2,1,0:T(8,128)(2,1)} %slab_ref.1, ...), custom_call_target="tpu_custom_call" | custom-call | tf_op jit(solution)/shard_map/table_grads/pallas_call | solution.py:143
  100.1 33.4 %all_to_all.20 = bf16[4,8,4,128,128]{4,3,2,1,0:T(8,128)(2,1)} all-to-all(bf16[4,8,4,128,128]{4,3,2,1,0:T(8,128)(2,1)} %get-tuple-element.7), channel_id=1, replica_groups={{0,4,8,12},{1,5,9,13},{2,6,10,14},{3,7,11,15},{16,17,18,19},{20,21,22,2..., dimensions={0} | all-to-all | bytes 8388608 | tf_op jit(solution)/shard_map/all_to_all | solution.py:261
  133.6 3.1 %reduce_sum.60 = bf16[8,4,128,128]{3,2,1,0:T(8,128)(2,1)S(1)} reduce(bf16[4,8,4,128,128]{4,3,2,1,0:T(8,128)(2,1)} %all_to_all.20, bf16[]{:T(256)} %constant.142.clone.1), dimensions={0}, to_apply=%region_3.4 | reduce | flops 1572864 | bytes 5242882 | tf_op jit(solution)/shard_map/reduce_sum | solution.py:264
  137.7 3.7 %all-to-all-start.3 = ((bf16[4,8,128,128]{3,2,1,0:T(8,128)(2,1)}), bf16[4,8,128,128]{3,2,1,0:T(8,128)(2,1)S(1)}, u32[]{:S(2)}, u32[]{:S(2)}) async-start(bf16[4,8,128,128]{3,2,1,0:T(8,128)(2,1)} %copy.104), calls=%async_computation.3 | async-start | bytes 2097152 | tf_op jit(solution)/shard_map/all_to_all | solution.py:265
  141.4 10.7 %all-to-all-done.3 = bf16[4,8,128,128]{3,2,1,0:T(8,128)(2,1)S(1)} async-done(((bf16[4,8,128,128]{3,2,1,0:T(8,128)(2,1)}), bf16[4,8,128,128]{3,2,1,0:T(8,128)(2,1)S(1)}, u32[]{:S(2)}, u32[]{:S(2)}) %all-to-all-start.3) | async-done | bytes 1048608 | tf_op jit(solution)/shard_map/all_to_all | solution.py:265
  154.0 2.1 %bitcast_dynamic-update-slice_fusion.7 = (bf16[4,8,128,128]{3,2,0,1:T(8,128)(2,1)S(1)}, bf16[8,128,128]{2,1,0:T(8,128)(2,1)}) fusion(bf16[4,8,128,128]{3,2,0,1:T(8,128)(2,1)S(1)} %broadcast_in_dim.87, s32[]{:T(128)S(6)} %select_n.182, f32[8,128,128]{2,1,0:T(8,128)S(1)} %convert_reduce_fusion, f32[8,128]{1,0:T(8,128)S(1)} %get-tuple-element.10, ...), kind=kLoop, calls=%fused_computation.34 | loop fusion | flops 524288 | bytes 1314824 | tf_op jit(solution)/shard_map/jit(dynamic_update_index_in_dim)/dynamic_update_slice | solution.py:206
  156.7 2.7 %collective-permute-start.9 = (bf16[8,128,128]{2,1,0:T(8,128)(2,1)}, bf16[8,128,128]{2,1,0:T(8,128)(2,1)}, u32[]{:S(2)}, u32[]{:S(2)}) collective-permute-start(bf16[8,128,128]{2,1,0:T(8,128)(2,1)} %get-tuple-element.9), channel_id=1, source_target_pairs={{0,3},{1,0},{2,1},{3,2},{4,7},{5,4},{6,5},{7,6},{8,11},{9,8},{10,9... | collective-permute-start | bytes 786440 | tf_op jit(solution)/shard_map/ppermute | solution.py:202
  159.3 4.6 %collective-permute-done.8 = bf16[8,128,128]{2,1,0:T(8,128)(2,1)S(1)} collective-permute-done((bf16[8,128,128]{2,1,0:T(8,128)(2,1)}, bf16[8,128,128]{2,1,0:T(8,128)(2,1)S(1)}, u32[]{:S(2)}, u32[]{:S(2)}) %collective-permute-start.8) | collective-permute-done | bytes 262176 | tf_op jit(solution)/shard_map/ppermute | solution.py:201
  164.9 3.3 %collective-permute-start.11 = (bf16[4,128,128]{2,1,0:T(8,128)(2,1)S(1)}, bf16[4,128,128]{2,1,0:T(8,128)(2,1)S(1)}, u32[]{:S(2)}, u32[]{:S(2)}) collective-permute-start(bf16[4,128,128]{2,1,0:T(8,128)(2,1)S(1)} %slice.17), channel_id=1, source_target_pairs={{0,3},{1,0},{2,1},{3,2},{4,7},{5,4},{6,5},{7,6},{8,11},{9,8},{10,9... | collective-permute-start | bytes 393224 | tf_op jit(solution)/shard_map/ppermute | solution.py:204
  169.3 2.3 %collective-permute-done.10 = bf16[4,128,128]{2,1,0:T(8,128)(2,1)S(1)} collective-permute-done((bf16[4,128,128]{2,1,0:T(8,128)(2,1)S(1)}, bf16[4,128,128]{2,1,0:T(8,128)(2,1)S(1)}, u32[]{:S(2)}, u32[]{:S(2)}) %collective-permute-start.10) | collective-permute-done | bytes 131104 | tf_op jit(solution)/shard_map/ppermute | solution.py:203
  172.8 2.7 %collective-permute-start.13 = (bf16[8,4,128,128]{3,2,1,0:T(8,128)(2,1)S(1)}, bf16[8,4,128,128]{3,2,1,0:T(8,128)(2,1)S(1)}, u32[]{:S(2)}, u32[]{:S(2)}) collective-permute-start(bf16[8,4,128,128]{3,2,1,0:T(8,128)(2,1)S(1)} %bitcast.99), channel_id=1, source_target_pairs={{0,12},{1,13},{2,14},{3,15},{4,0},{5,1},{6,2},{7,3},{8,4},{9,5},{1... | collective-permute-start | bytes 3145736 | tf_op jit(solution)/shard_map/ppermute | solution.py:202
  175.4 3.3 %multiply_reduce_fusion = f32[8,1024]{1,0:T(8,128)S(1)} fusion(f32[8,1024,128]{2,1,0:T(8,128)} %get-tuple-element.6), kind=kLoop, calls=%fused_computation.4 | loop fusion | flops 2088960 | bytes 4227072 | tf_op jit(solution)/shard_map/reduce_sum | solution.py:282
  179.4 2.2 %subtract_convert_fusion = bf16[8,1024,128]{2,1,0:T(8,128)(2,1)} fusion(f32[8,1024,128]{2,1,0:T(8,128)S(1)} %copy-done, bf16[8,1024,128]{2,1,0:T(8,128)(2,1)S(1)} %copy-done.1, f32[8,1024]{1,0:T(8,128)S(1)} %get-tuple-element.12), kind=kLoop, calls=%fused_computation.3 | loop fusion | flops 4194304 | bytes 8421376 | tf_op jit(solution)/shard_map/convert_element_type | solution.py:286
  182.8 5.4 %collective-permute-done.12 = bf16[8,4,128,128]{3,2,1,0:T(8,128)(2,1)S(1)} collective-permute-done((bf16[8,4,128,128]{3,2,1,0:T(8,128)(2,1)S(1)}, bf16[8,4,128,128]{3,2,1,0:T(8,128)(2,1)S(1)}, u32[]{:S(2)}, u32[]{:S(2)}) %collective-permute-start.12) | collective-permute-done | bytes 1048608 | tf_op jit(solution)/shard_map/ppermute | solution.py:201
  188.4 3.3 %collective-permute-start.15 = (bf16[4,4,128,128]{3,2,1,0:T(8,128)(2,1)S(1)}, bf16[4,4,128,128]{3,2,1,0:T(8,128)(2,1)S(1)}, u32[]{:S(2)}, u32[]{:S(2)}) collective-permute-start(bf16[4,4,128,128]{3,2,1,0:T(8,128)(2,1)S(1)} %slice.19), channel_id=1, source_target_pairs={{0,12},{1,13},{2,14},{3,15},{4,0},{5,1},{6,2},{7,3},{8,4},{9,5},{1... | collective-permute-start | bytes 1572872 | tf_op jit(solution)/shard_map/ppermute | solution.py:204
  192.0 6.7 %collective-permute-done.14 = bf16[4,4,128,128]{3,2,1,0:T(8,128)(2,1)S(1)} collective-permute-done((bf16[4,4,128,128]{3,2,1,0:T(8,128)(2,1)S(1)}, bf16[4,4,128,128]{3,2,1,0:T(8,128)(2,1)S(1)}, u32[]{:S(2)}, u32[]{:S(2)}) %collective-permute-start.14) | collective-permute-done | bytes 524320 | tf_op jit(solution)/shard_map/ppermute | solution.py:203
  198.9 3.3 %bitcast_select_fusion = bf16[8,4,4,128,128]{4,3,2,1,0:T(8,128)(2,1)} fusion(bf16[4,8,4,128,128]{4,3,0,2,1:T(8,128)(2,1)S(1)} %bitcast_dynamic-update-slice_fusion.4, pred[]{:T(512)S(6)} %eq.53), kind=kLoop, calls=%fused_computation.2 | loop fusion | flops 2097152 | bytes 8388609 | tf_op jit(solution)/shard_map/jit(_where)/select_n | solution.py:279
  (77 shorter events, 21.1 us)
Async XLA Ops:
  2.9 3.0 %copy-start.3 = (s32[8,512,1]{1,2,0:T(1,128)S(1)}, s32[8,512,1]{1,2,0:T(1,128)}, u32[]{:S(2)}) copy-start(s32[8,512,1]{1,2,0:T(1,128)} %param.17) | copy-start | bytes 49156
  5.7 14.9 %copy-start.5 = (s32[8,512]{1,0:T(8,128)S(1)}, s32[8,512]{1,0:T(8,128)}, u32[]{:S(2)}) copy-start(s32[8,512]{1,0:T(8,128)} %param.19) | copy-start | bytes 49156
  5.7 14.9 %copy-start.6 = (s32[8,512]{1,0:T(8,128)S(1)}, s32[8,512]{1,0:T(8,128)}, u32[]{:S(2)}) copy-start(s32[8,512]{1,0:T(8,128)} %param.18) | copy-start | bytes 49156
  5.7 2.0 collective-permute-start
  8.1 8.0 %collective-permute-start.1 = (bf16[64,1024]{1,0:T(8,128)(2,1)S(1)}, bf16[64,1024]{1,0:T(8,128)(2,1)S(1)}, u32[]{:S(2)}, u32[]{:S(2)}) collective-permute-start(bf16[64,1024]{1,0:T(8,128)(2,1)S(1)} %get-tuple-element.18), channel_id=1, source_target_pairs={{0,64},{32,96},{64,0},{96,32},{1,65},{33,97},{65,1},{97,33},{2,66}... | collective-permute-start | bytes 393224 | tf_op jit(solution)/shard_map/ppermute | solution.py:181
  11.3 7.0 %collective-permute-start.2 = (bf16[64,1024]{1,0:T(8,128)(2,1)S(1)}, bf16[64,1024]{1,0:T(8,128)(2,1)S(1)}, u32[]{:S(2)}, u32[]{:S(2)}) collective-permute-start(bf16[64,1024]{1,0:T(8,128)(2,1)S(1)} %get-tuple-element.20), channel_id=1, source_target_pairs={{0,32},{32,64},{64,96},{96,0},{1,33},{33,65},{65,97},{97,1},{2,34}... | collective-permute-start | bytes 393224 | tf_op jit(solution)/shard_map/ppermute | solution.py:181
  11.9 6.4 %collective-permute-start.3 = (bf16[64,1024]{1,0:T(8,128)(2,1)S(1)}, bf16[64,1024]{1,0:T(8,128)(2,1)S(1)}, u32[]{:S(2)}, u32[]{:S(2)}) collective-permute-start(bf16[64,1024]{1,0:T(8,128)(2,1)S(1)} %get-tuple-element.19), channel_id=1, source_target_pairs={{0,96},{32,0},{64,32},{96,64},{1,97},{33,1},{65,33},{97,65},{2,98}... | collective-permute-start | bytes 393224 | tf_op jit(solution)/shard_map/ppermute | solution.py:181
  18.5 7.2 %collective-permute-start.4 = (bf16[64,1024]{1,0:T(8,128)(2,1)S(1)}, bf16[64,1024]{1,0:T(8,128)(2,1)S(1)}, u32[]{:S(2)}, u32[]{:S(2)}) collective-permute-start(bf16[64,1024]{1,0:T(8,128)(2,1)S(1)} %get-tuple-element.15), channel_id=1, source_target_pairs={{0,64},{32,96},{64,0},{96,32},{1,65},{33,97},{65,1},{97,33},{2,66}... | collective-permute-start | bytes 393224 | tf_op jit(solution)/shard_map/ppermute | solution.py:187
  20.6 7.3 %collective-permute-start.5 = (bf16[64,1024]{1,0:T(8,128)(2,1)S(1)}, bf16[64,1024]{1,0:T(8,128)(2,1)S(1)}, u32[]{:S(2)}, u32[]{:S(2)}) collective-permute-start(bf16[64,1024]{1,0:T(8,128)(2,1)S(1)} %get-tuple-element.15), channel_id=1, source_target_pairs={{0,32},{32,64},{64,96},{96,0},{1,33},{33,65},{65,97},{97,1},{2,34}... | collective-permute-start | bytes 393224 | tf_op jit(solution)/shard_map/ppermute | solution.py:187
  22.4 5.5 %collective-permute-start.6 = (bf16[64,1024]{1,0:T(8,128)(2,1)S(1)}, bf16[64,1024]{1,0:T(8,128)(2,1)S(1)}, u32[]{:S(2)}, u32[]{:S(2)}) collective-permute-start(bf16[64,1024]{1,0:T(8,128)(2,1)S(1)} %get-tuple-element.15), channel_id=1, source_target_pairs={{0,96},{32,0},{64,32},{96,64},{1,97},{33,1},{65,33},{97,65},{2,98}... | collective-permute-start | bytes 393224 | tf_op jit(solution)/shard_map/ppermute | solution.py:187
  27.9 11.4 %collective-permute-start.7 = (bf16[256,1024]{1,0:T(8,128)(2,1)S(1)}, bf16[256,1024]{1,0:T(8,128)(2,1)S(1)}, u32[]{:S(2)}, u32[]{:S(2)}) collective-permute-start(bf16[256,1024]{1,0:T(8,128)(2,1)S(1)} %bitcast.102), channel_id=1, source_target_pairs={{0,16},{16,0},{1,17},{17,1},{2,18},{18,2},{3,19},{19,3},{4,20},{20... | collective-permute-start | bytes 1572872 | tf_op jit(solution)/shard_map/ppermute | solution.py:190
  30.6 16.6 %all-to-all-start.1 = ((s32[16,1,384]{2,1,0:T(1,128)}), s32[16,1,384]{2,1,0:T(1,128)S(1)}, u32[]{:S(2)}, u32[]{:S(2)}) async-start(s32[16,1,384]{2,1,0:T(1,128)} %reshape.81), calls=%async_computation.1 | async-start | bytes 49152 | tf_op jit(solution)/shard_map/all_to_all | solution.py:241
  47.2 31.9 %all-to-all-start = ((bf16[16,8,48,128]{3,2,1,0:T(8,128)(2,1)}), bf16[16,8,48,128]{3,2,1,0:T(8,128)(2,1)S(1)}, u32[]{:S(2)}, u32[]{:S(2)}) async-start(bf16[16,8,48,128]{3,2,1,0:T(8,128)(2,1)} %pooled_dispatch.1), calls=%async_computation | async-start | bytes 3145728 | tf_op jit(solution)/shard_map/all_to_all | solution.py:258
  79.1 1.1 copy-start.2
  137.7 14.4 %all-to-all-start.3 = ((bf16[4,8,128,128]{3,2,1,0:T(8,128)(2,1)}), bf16[4,8,128,128]{3,2,1,0:T(8,128)(2,1)S(1)}, u32[]{:S(2)}, u32[]{:S(2)}) async-start(bf16[4,8,128,128]{3,2,1,0:T(8,128)(2,1)} %copy.104), calls=%async_computation.3 | async-start | bytes 2097152 | tf_op jit(solution)/shard_map/all_to_all | solution.py:265
  153.7 25.1 %copy-start.4 = (f32[8,1024]{1,0:T(8,128)S(1)}, f32[8,1024]{1,0:T(8,128)}, u32[]{:S(2)}) copy-start(f32[8,1024]{1,0:T(8,128)} %param.21) | copy-start | bytes 98308
  154.0 25.5 %copy-start.1 = (bf16[8,1024,128]{2,1,0:T(8,128)(2,1)S(1)}, bf16[8,1024,128]{2,1,0:T(8,128)(2,1)}, u32[]{:S(2)}) copy-start(bf16[8,1024,128]{2,1,0:T(8,128)(2,1)} %slab_ref.1) | copy-start | bytes 6291460
  156.1 7.8 %collective-permute-start.8 = (bf16[8,128,128]{2,1,0:T(8,128)(2,1)}, bf16[8,128,128]{2,1,0:T(8,128)(2,1)S(1)}, u32[]{:S(2)}, u32[]{:S(2)}) collective-permute-start(bf16[8,128,128]{2,1,0:T(8,128)(2,1)} %get-tuple-element.9), channel_id=1, source_target_pairs={{0,1},{1,2},{2,3},{3,0},{4,5},{5,6},{6,7},{7,4},{8,9},{9,10},{10,1... | collective-permute-start | bytes 786440 | tf_op jit(solution)/shard_map/ppermute | solution.py:201
  156.7 7.3 %collective-permute-start.9 = (bf16[8,128,128]{2,1,0:T(8,128)(2,1)}, bf16[8,128,128]{2,1,0:T(8,128)(2,1)}, u32[]{:S(2)}, u32[]{:S(2)}) collective-permute-start(bf16[8,128,128]{2,1,0:T(8,128)(2,1)} %get-tuple-element.9), channel_id=1, source_target_pairs={{0,3},{1,0},{2,1},{3,2},{4,7},{5,4},{6,5},{7,6},{8,11},{9,8},{10,9... | collective-permute-start | bytes 786440 | tf_op jit(solution)/shard_map/ppermute | solution.py:202
  159.3 20.1 %copy-start = (f32[8,1024,128]{2,1,0:T(8,128)S(1)}, f32[8,1024,128]{2,1,0:T(8,128)}, u32[]{:S(2)}) copy-start(f32[8,1024,128]{2,1,0:T(8,128)} %get-tuple-element.6) | copy-start | bytes 12582916
  163.9 7.7 %collective-permute-start.10 = (bf16[4,128,128]{2,1,0:T(8,128)(2,1)S(1)}, bf16[4,128,128]{2,1,0:T(8,128)(2,1)S(1)}, u32[]{:S(2)}, u32[]{:S(2)}) collective-permute-start(bf16[4,128,128]{2,1,0:T(8,128)(2,1)S(1)} %slice.16), channel_id=1, source_target_pairs={{0,1},{1,2},{2,3},{3,0},{4,5},{5,6},{6,7},{7,4},{8,9},{9,10},{10,1... | collective-permute-start | bytes 393224 | tf_op jit(solution)/shard_map/ppermute | solution.py:203
  164.9 7.2 %collective-permute-start.11 = (bf16[4,128,128]{2,1,0:T(8,128)(2,1)S(1)}, bf16[4,128,128]{2,1,0:T(8,128)(2,1)S(1)}, u32[]{:S(2)}, u32[]{:S(2)}) collective-permute-start(bf16[4,128,128]{2,1,0:T(8,128)(2,1)S(1)} %slice.17), channel_id=1, source_target_pairs={{0,3},{1,0},{2,1},{3,2},{4,7},{5,4},{6,5},{7,6},{8,11},{9,8},{10,9... | collective-permute-start | bytes 393224 | tf_op jit(solution)/shard_map/ppermute | solution.py:204
  172.1 16.1 %collective-permute-start.12 = (bf16[8,4,128,128]{3,2,1,0:T(8,128)(2,1)S(1)}, bf16[8,4,128,128]{3,2,1,0:T(8,128)(2,1)S(1)}, u32[]{:S(2)}, u32[]{:S(2)}) collective-permute-start(bf16[8,4,128,128]{3,2,1,0:T(8,128)(2,1)S(1)} %bitcast.98), channel_id=1, source_target_pairs={{0,4},{1,5},{2,6},{3,7},{4,8},{5,9},{6,10},{7,11},{8,12},{9,13},{1... | collective-permute-start | bytes 3145736 | tf_op jit(solution)/shard_map/ppermute | solution.py:201
  172.8 15.6 %collective-permute-start.13 = (bf16[8,4,128,128]{3,2,1,0:T(8,128)(2,1)S(1)}, bf16[8,4,128,128]{3,2,1,0:T(8,128)(2,1)S(1)}, u32[]{:S(2)}, u32[]{:S(2)}) collective-permute-start(bf16[8,4,128,128]{3,2,1,0:T(8,128)(2,1)S(1)} %bitcast.99), channel_id=1, source_target_pairs={{0,12},{1,13},{2,14},{3,15},{4,0},{5,1},{6,2},{7,3},{8,4},{9,5},{1... | collective-permute-start | bytes 3145736 | tf_op jit(solution)/shard_map/ppermute | solution.py:202
  188.3 10.5 %collective-permute-start.14 = (bf16[4,4,128,128]{3,2,1,0:T(8,128)(2,1)S(1)}, bf16[4,4,128,128]{3,2,1,0:T(8,128)(2,1)S(1)}, u32[]{:S(2)}, u32[]{:S(2)}) collective-permute-start(bf16[4,4,128,128]{3,2,1,0:T(8,128)(2,1)S(1)} %slice.18), channel_id=1, source_target_pairs={{0,4},{1,5},{2,6},{3,7},{4,8},{5,9},{6,10},{7,11},{8,12},{9,13},{1... | collective-permute-start | bytes 1572872 | tf_op jit(solution)/shard_map/ppermute | solution.py:203
  188.4 10.4 %collective-permute-start.15 = (bf16[4,4,128,128]{3,2,1,0:T(8,128)(2,1)S(1)}, bf16[4,4,128,128]{3,2,1,0:T(8,128)(2,1)S(1)}, u32[]{:S(2)}, u32[]{:S(2)}) collective-permute-start(bf16[4,4,128,128]{3,2,1,0:T(8,128)(2,1)S(1)} %slice.19), channel_id=1, source_target_pairs={{0,12},{1,13},{2,14},{3,15},{4,0},{5,1},{6,2},{7,3},{8,4},{9,5},{1... | collective-permute-start | bytes 1572872 | tf_op jit(solution)/shard_map/ppermute | solution.py:204

commit v2 on v1

v2 whole, which is shorter than its diff:
```python
import functools

import jax
import jax.numpy as jnp
from jax import lax
from jax.experimental import pallas as pl
from jax.experimental.pallas import tpu as pltpu
from jax.sharding import Mesh
from jax.sharding import PartitionSpec as P

step_rate = 0.3
epsilon = 1e-06
bf = jnp.bfloat16
f32 = jnp.float32
NX, NC, NZ, NY = 4, 2, 4, 4
CZY = ("c", "z", "y")
NT = (((1,), (1,)), ((), ()))


def ring(n, s):
    return [(i, (i + s) % n) for i in range(n)]


def spot(c, z, y):
    return (c * NZ + z) * NY + y


def turn_pairs(s, flip):
    out = []
    for c in range(NC):
        for z in range(NZ):
            for y in range(NY):
                if (c == 0) != flip:
                    to = spot(c, (z + s) % NZ, y)
                else:
                    to = spot(c, z, (y + s) % NY)
                out.append((spot(c, z, y), to))
    return out


def turn_groups(flip):
    out = []
    for c in range(NC):
        if (c == 0) != flip:
            out += [[spot(c, z, y) for z in range(NZ)] for y in range(NY)]
        else:
            out += [[spot(c, z, y) for y in range(NY)] for z in range(NZ)]
    return out


def pooled_kernel(rank_ref, cot_ref, co_ref, ci_ref, bias_ref, pos_ref, dig_ref, out_ref, key_ref):
    rank = co_ref.shape[1]
    dests, tables, cap, width = out_ref.shape
    samples = cot_ref.shape[0]
    here = pos_ref.shape[0]
    step = pl.program_id(0)
    gate = (
        lax.dot_general(rank_ref[:, :rank], co_ref[...], NT, preferred_element_type=f32)
        + bias_ref[...]
    )
    back = lax.dot_general(rank_ref[:, rank:], ci_ref[...], NT, preferred_element_type=f32)
    pooled = (cot_ref[...].astype(f32) * (gate + 1.0) + back).astype(bf)
    slot = lax.broadcasted_iota(jnp.int32, (dests * cap, samples), 0)
    owner = lax.broadcasted_iota(jnp.int32, (samples, width), 1) // DIGITS
    keys = jnp.zeros((dests * cap, width), f32)
    for k in range(here):
        t = step * here + k
        placed = jnp.where(slot == pos_ref[k], 1.0, 0.0).astype(bf)
        digits = jnp.where(owner == t, dig_ref[...].astype(f32), 0.0).astype(bf)
        both = jnp.concatenate([pooled[:, k * width : (k + 1) * width], digits], axis=1)
        rows = jnp.dot(placed, both, preferred_element_type=f32)
        out_ref[:, t] = rows[:, :width].astype(bf).reshape(dests, cap, width)
        keys = keys + rows[:, width:]

    @pl.when(step == 0)
    def _():
        key_ref[...] = keys

    @pl.when(step > 0)
    def _():
        key_ref[...] += keys

    @pl.when(step == pl.num_programs(0) - 1)
    def _():
        out_ref[:, tables - 1] = key_ref[...].astype(bf).reshape(dests, cap, width)


def pooled_dispatch(rank, cot, co, ci, bias, pos, digits, dests, cap, width):
    samples = cot.shape[0]
    tables = pos.shape[0]
    pair = 2
    out = (dests, tables + 1, cap, width)
    return pl.pallas_call(
        pooled_kernel,
        grid=(tables // pair,),
        out_shape=jax.ShapeDtypeStruct(out, bf),
        in_specs=[
            pl.BlockSpec(rank.shape, lambda i: (0, 0)),
            pl.BlockSpec((samples, pair * width), lambda i: (0, i)),
            pl.BlockSpec((pair * width, co.shape[1]), lambda i: (i, 0)),
            pl.BlockSpec((pair * width, co.shape[1]), lambda i: (i, 0)),
            pl.BlockSpec((1, pair * width), lambda i: (0, i)),
            pl.BlockSpec((pair, 1, samples), lambda i: (i, 0, 0)),
            pl.BlockSpec(digits.shape, lambda i: (0, 0)),
        ],
        out_specs=pl.BlockSpec(out, lambda i: (0, 0, 0, 0)),
        scratch_shapes=[pltpu.VMEM((dests * cap, width), f32)],
        name="pooled_dispatch",
    )(rank, cot, co, ci, bias, pos, digits)


DIGITS, QB, MB = 4, 32, 64


def digit_lanes(q, m, width):
    parts = jnp.stack([q // QB, q % QB, m // MB, m % MB], axis=1)
    parts = parts.reshape(-1, q.shape[1])
    parts = jnp.pad(parts, ((0, width - parts.shape[0]), (0, 0)))
    return parts.T.astype(bf)


def key_rows(keys, tables):
    width = keys.shape[1]
    lane = lax.broadcasted_iota(jnp.int32, (width, width), 0)
    col = lax.broadcasted_iota(jnp.int32, (width, width), 1)
    t = col % tables
    base = DIGITS * t + jnp.where(col >= tables, 2, 0)
    high = jnp.where(col >= tables, MB, QB).astype(f32)
    comb = jnp.where(lane == base, high, jnp.where(lane == base + 1, 1.0, 0.0))
    comb = jnp.where(col < 2 * tables, comb, 0.0).astype(bf)
    return jnp.dot(keys, comb, preferred_element_type=f32).T


def key_lanes(keys, t):
    width = keys.shape[1]
    lane = lax.broadcasted_iota(jnp.int32, (width, 2 * width), 0) - DIGITS * t
    side = lax.broadcasted_iota(jnp.int32, (width, 2 * width), 1) >= width
    lane = jnp.where(side, lane - 2, lane)
    high = jnp.where(side, float(MB), float(QB))
    comb = jnp.where(lane == 0, high, jnp.where(lane == 1, 1.0, 0.0)).astype(bf)
    out = jnp.dot(keys, comb, preferred_element_type=f32)
    return out[:, :width], out[:, width:]


def pick(key, tab):
    slots, width = key.shape
    half = tab.shape[0] // 2
    high = key >= half
    low = jnp.where(high, key - half, key)
    lane = lax.broadcasted_iota(jnp.int32, (slots, width), 1).astype(f32)
    hot = jnp.concatenate(
        [jnp.where(low - j == lane, 1.0, 0.0).astype(bf) for j in range(0, half, width)], axis=1
    )
    both = jnp.concatenate([tab[:half], tab[half:]], axis=1)
    got = jnp.dot(hot, both, preferred_element_type=f32)
    return jnp.where(high, got[:, width:], got[:, :width])


def spread(row, key, rows, val):
    slots = row.shape[1]
    half = rows // 2
    low = jnp.where(row >= half, row - half, row)
    at = lax.broadcasted_iota(jnp.int32, (half, slots), 0).astype(f32)
    hot = jnp.where(at == low, 1.0, 0.0).astype(bf)
    high = key >= half
    both = jnp.concatenate(
        [jnp.where(high, 0.0, val).astype(bf), jnp.where(high, val, 0.0).astype(bf)], axis=1
    )
    return jnp.dot(hot, both, preferred_element_type=f32)


def rem_kernel(first, tables, where_ref, g_ref, key_ref, slab_ref, r0, r1, r2, r3, row_ref, sum_ref):
    sources, _, cap, width = g_ref.shape
    slots = sources * cap
    rem_rows = sum_ref.shape[0]
    step = pl.program_id(0)
    keys = key_ref[:, 0].reshape(slots, width)

    @pl.when(step == 0)
    def _():
        row_ref[...] = key_rows(keys, tables)

    t = first + step
    g = g_ref[:, 0].reshape(slots, width).astype(f32)
    q, m = key_lanes(keys, t)
    val = g * pick(q, slab_ref[0])
    both = spread(row_ref[pl.ds(tables + t, 1), :], m, rem_rows, val)
    sum_ref[: rem_rows // 2] = both[:, :width].astype(bf)
    sum_ref[rem_rows // 2 :] = both[:, width:].astype(bf)
    sub_rows = r0.shape[2]
    at = where_ref[1]
    along_z = where_ref[0] == 0
    for rel, ref in enumerate((r0, r1, r2, r3)):
        far = (at + rel) % 4
        for sub in range(4):
            block = jnp.where(along_z, far * NY + sub, sub * NY + far)
            start = pl.multiple_of(block * sub_rows, sub_rows)
            ref[0, sub] = sum_ref[pl.ds(start, sub_rows), :]


def rem_parts(first, count, where, got, slab, rem_rows):
    sources, tables, cap, width = got.shape
    tables -= 1
    slots = sources * cap
    quot_rows = slab.shape[1]
    sub = rem_rows // (NZ * NY)
    piece = jax.ShapeDtypeStruct((count, 4, sub, width), bf)
    return pl.pallas_call(
        functools.partial(rem_kernel, first, tables),
        out_shape=(piece,) * 4,
        grid_spec=pltpu.PrefetchScalarGridSpec(
            num_scalar_prefetch=1,
            grid=(count,),
            in_specs=[
                pl.BlockSpec((sources, 1, cap, width), lambda t, c: (0, first + t, 0, 0)),
                pl.BlockSpec((sources, 1, cap, width), lambda t, c: (0, tables, 0, 0)),
                pl.BlockSpec((1, quot_rows, width), lambda t, c: (first + t, 0, 0)),
            ],
            out_specs=[pl.BlockSpec((1, 4, sub, width), lambda t, c: (t, 0, 0, 0))] * 4,
            scratch_shapes=[pltpu.VMEM((width, slots), f32), pltpu.VMEM((rem_rows, width), bf)],
        ),
        cost_estimate=pl.CostEstimate(
            flops=count * 4 * slots * rem_rows * width, bytes_accessed=1 << 22, transcendentals=0
        ),
        name="rem_parts",
    )(where, got, got, slab)


def quot_kernel(tables, g_ref, key_ref, rtab_ref, quot_ref, row_ref):
    sources, _, cap, width = g_ref.shape
    slots = sources * cap
    quot_rows = quot_ref.shape[1]
    t = pl.program_id(0)
    keys = key_ref[:, 0].reshape(slots, width)

    @pl.when(t == 0)
    def _():
        row_ref[...] = key_rows(keys, tables)

    g = g_ref[:, 0].reshape(slots, width).astype(f32)
    q, m = key_lanes(keys, t)
    val = g * pick(m, rtab_ref[0])
    both = spread(row_ref[pl.ds(t, 1), :], q, quot_rows, val)
    quot_ref[0, : quot_rows // 2] = both[:, :width]
    quot_ref[0, quot_rows // 2 :] = both[:, width:]


def quot_grads(got, rtab, quot_rows):
    sources, tables, cap, width = got.shape
    tables -= 1
    slots = sources * cap
    rem_rows = rtab.shape[1]
    return pl.pallas_call(
        functools.partial(quot_kernel, tables),
        out_shape=jax.ShapeDtypeStruct((tables, quot_rows, width), f32),
        grid=(tables,),
        in_specs=[
            pl.BlockSpec((sources, 1, cap, width), lambda t: (0, t, 0, 0)),
            pl.BlockSpec((sources, 1, cap, width), lambda t: (0, tables, 0, 0)),
            pl.BlockSpec((1, rem_rows, width), lambda t: (t, 0, 0)),
        ],
        out_specs=pl.BlockSpec((1, quot_rows, width), lambda t: (t, 0, 0)),
        scratch_shapes=[pltpu.VMEM((width, slots), f32)],
        cost_estimate=pl.CostEstimate(
            flops=tables * 4 * slots * rem_rows * width, bytes_accessed=1 << 23, transcendentals=0
        ),
        name="quot_grads",
    )(got, got, rtab)


def turn(a, s, flip):
    return lax.ppermute(a, CZY, turn_pairs(s, flip))


def add(*parts):
    total = parts[0].astype(f32)
    for p in parts[1:]:
        total = total + p.astype(f32)
    return total


def ring_scatter(low, high, flip):
    far_low = turn(low[2], 1, flip)
    far_high = turn(high[2], -1, flip)
    near_low = turn(low[3], -1, flip)
    near_high = turn(high[1], 1, flip)
    sum_low = turn(add(low[1], far_low).astype(bf), 1, flip)
    sum_high = turn(add(high[3], far_high).astype(bf), -1, flip)
    return add(low[0], near_low, sum_low), add(high[0], near_high, sum_high)


def ring_gather(low, high, flip):
    prev_low = turn(low, 1, flip)
    next_high = turn(high, -1, flip)
    prev_high = turn(high, 1, flip)
    next_low = turn(low, -1, flip)
    far_low = turn(prev_low, 1, flip)
    far_high = turn(next_high, -1, flip)
    return [low, next_low, far_low, prev_low], [high, next_high, far_high, prev_high]


def place_kernel(rels, where_ref, *refs):
    out_ref = refs[-1]
    half = out_ref.shape[0] // 2
    for k in range(len(rels)):

        @pl.when(pl.program_id(0) == k)
        def _():
            out_ref[:half, 0, 0] = refs[2 * k][:, 0]
            out_ref[half:, 0, 0] = refs[2 * k + 1][:, 0]


def place(rels, where, pieces, shape, old=None):
    tables, _, _, sub, width = shape
    half = tables // 2

    def out_map(k, s, w):
        rel = sum(jnp.where(k == i, r, 0) for i, r in enumerate(rels))
        far = (w[2] + rel) % 4
        along_z = w[0] == 0
        return 0, jnp.where(along_z, far, s), jnp.where(along_z, s, far), 0, 0

    ins = [x for lh in pieces for x in lh]
    specs = [
        pl.BlockSpec(
            (half, 1, sub, width),
            lambda k, s, w, i=i: (0, jnp.where(k < i, 0, jnp.where(k > i, 3, s)), 0, 0),
        )
        for i in range(len(rels))
        for _ in range(2)
    ]
    alias = {}
    if old is not None:
        ins.append(old)
        specs.append(pl.BlockSpec(memory_space=pl.ANY))
        alias = {len(ins): 0}
    return pl.pallas_call(
        functools.partial(place_kernel, rels),
        out_shape=jax.ShapeDtypeStruct(shape, bf),
        grid_spec=pltpu.PrefetchScalarGridSpec(
            num_scalar_prefetch=1,
            grid=(len(rels), 4),
            in_specs=specs,
            out_specs=pl.BlockSpec((tables, 1, 1, sub, width), out_map),
        ),
        input_output_aliases=alias,
        cost_estimate=pl.CostEstimate(flops=0, bytes_accessed=len(rels) << 21, transcendentals=0),
        name="place",
    )(where, *ins)


def rank_sums(part):
    ci = lax.axis_index("c")
    xi = lax.axis_index("x")
    swap = [(0, 1), (1, 0)]
    half = part.shape[0] // NC
    size = half // NX
    keep = lax.dynamic_slice_in_dim(part, ci * half, half, 0)
    give = lax.dynamic_slice_in_dim(part, (1 - ci) * half, half, 0).astype(bf)
    got = lax.ppermute(give, "c", swap)
    both = (keep + got.astype(f32)).astype(bf).reshape(NX, size, -1)
    take = lambda k: lax.dynamic_index_in_dim(both, (xi + k) % NX, 0, keepdims=False)
    total = take(0).astype(f32)
    for k in (2, 1, 3):
        total = total + lax.ppermute(take(k), "x", ring(NX, k)).astype(f32)
    mine = total.astype(bf)
    parts = jnp.zeros_like(both)
    parts = lax.dynamic_update_index_in_dim(parts, mine, xi, 0)
    for k in (2, 1, 3):
        parts = lax.dynamic_update_index_in_dim(
            parts, lax.ppermute(mine, "x", ring(NX, k)), (xi - k) % NX, 0
        )
    own = parts.reshape(half, -1)
    other = lax.ppermute(own, "c", swap)
    low = jnp.where(ci == 0, own, other)
    high = jnp.where(ci == 0, other, own)
    return jnp.concatenate([low, high], axis=0)


def per_device(
    features, cotangent, cross_in, cross_out, bias, dest_shard, quot_row, rem_row,
    quot_slab, quot_accum, rem_table, rem_accum,
):
    samples = features.shape[0]
    tables = quot_slab.shape[0]
    width = quot_slab.shape[2]
    rem_rows = rem_table.shape[1]
    rows = NZ * NY
    cap = 3 * samples // (2 * rows)
    slots = rows * cap
    ci, zi, yi = lax.axis_index("c"), lax.axis_index("z"), lax.axis_index("y")

    target = dest_shard[:, :, 0]
    onehot = target[:, :, None] == jnp.arange(rows, dtype=jnp.int32)[None, None, :]
    lower = (
        jnp.arange(samples, dtype=jnp.int32)[:, None]
        >= jnp.arange(samples, dtype=jnp.int32)[None, :]
    ).astype(bf)
    running = jnp.einsum("ij,tjn->tin", lower, onehot.astype(bf), preferred_element_type=f32)
    slot_index = jnp.sum(jnp.where(onehot, running, 0.0), axis=2).astype(jnp.int32) - 1
    position = target * cap + slot_index
    digits = digit_lanes(quot_row, rem_row, width)

    product = (cotangent.astype(f32) * features.astype(f32)).astype(bf)
    part = jnp.concatenate(
        [
            jnp.dot(features, cross_in, preferred_element_type=f32),
            jnp.dot(product, cross_out, preferred_element_type=f32),
        ],
        axis=1,
    )
    rank = rank_sums(part)

    send = pooled_dispatch(
        rank, cotangent, cross_out, cross_in, bias.reshape(1, -1),
        position.reshape(tables, 1, samples), digits, rows, cap, width,
    )
    got = lax.all_to_all(send, ("z", "y"), split_axis=0, concat_axis=0, tiled=True)
    along_z = ci == 0
    at_one = jnp.where(along_z, zi, yi)
    at_two = jnp.where(along_z, yi, zi)
    where = jnp.stack([ci, at_one, at_one]).astype(jnp.int32)
    half = tables // 2
    low = rem_parts(0, half, where, got, quot_slab, rem_rows)
    high = rem_parts(half, half, where, got, quot_slab, rem_rows)

    one_low, one_high = ring_scatter(low, high, False)
    ring_low, ring_high = ring_gather(one_low.astype(bf), one_high.astype(bf), True)
    share = rem_rows // rows
    view = (tables, NZ, NY, share)

    def quarter(a):
        a = a.reshape(view + a.shape[2:])
        return jnp.where(
            along_z,
            lax.dynamic_index_in_dim(a, zi, 1, keepdims=False),
            lax.dynamic_index_in_dim(a, yi, 2, keepdims=False),
        )

    def update(ring, acc_in, tab_in):
        grad = (ring[0].astype(f32) + ring[2].astype(f32)) + (
            ring[1].astype(f32) + ring[3].astype(f32)
        )
        acc = acc_in + jnp.mean(grad * grad, axis=-1)
        new = tab_in.astype(f32) - step_rate * grad * lax.rsqrt(acc + epsilon)[..., None]
        return acc, new.astype(bf)

    acc_in, tab_in = quarter(rem_accum), quarter(rem_table)
    acc_low, new_low = update(ring_low, acc_in[:half], tab_in[:half])
    acc_high, new_high = update(ring_high, acc_in[half:], tab_in[half:])
    acc = jnp.concatenate([acc_low, acc_high], axis=0)
    rem_acc_out = lax.dynamic_index_in_dim(acc, at_two, 1, keepdims=False)
    all_low, all_high = ring_gather(new_low, new_high, False)
    shape = (tables, NZ, NY, share, width)
    near = [(all_low[k], all_high[k]) for k in (0, 1, 3)]
    rem_out = place((0, 1, 3), where, near, shape)
    rem_out = place((2,), where, [(all_low[2], all_high[2])], shape, rem_out)
    rem_out = rem_out.reshape(tables, rem_rows, width)

    quot_grad = quot_grads(got, rem_table, quot_slab.shape[1])
    quot_acc_out = quot_accum + jnp.mean(quot_grad * quot_grad, axis=-1)
    quot_out = (
        quot_slab.astype(f32)
        - step_rate * quot_grad * lax.rsqrt(quot_acc_out + epsilon)[..., None]
    ).astype(bf)
    return (quot_out, quot_acc_out, rem_out, rem_acc_out)


def solution(mesh):
    fine = Mesh(mesh.devices.reshape(NX, NC, NZ, NY), ("x", "c", "z", "y"))
    T, R = ("x", "c"), ("z", "y")
    return jax.shard_map(
        per_device,
        mesh=fine,
        in_specs=(
            P(R, T), P(R, T), P(T, None), P(T, None), P(T), P(T, R, None), P(T, R), P(T, R),
            P(T, R, None), P(T, R), P(T, None, None), P(T, None),
        ),
        out_specs=(P(T, R, None), P(T, R), P(T, None, None), P(T, R)),
        check_vma=False,
    )
```

time: 204 us -> 187 us (0.917)
  blocking collectives: 33.4 us -> 0 us
  Pallas kernels: 26.6 us -> 52.1 us
  waiting for transfers between devices: 58.7 us -> 73.1 us
  local copies, waits for them, and re-layouts: 11.9 us -> 4.05 us
  starting transfers between devices: 44.3 us -> 36.8 us
  other arithmetic: 20.9 us -> 15.8 us
    all_to_all x1 -> x0, blocking collectives: 33.4 us -> none  [per_device(): lax.all_to_all(rem_part, CZY, 0, 0, tiled=True, axis_index_groups=turn_gr...]
    pallas_call x1 -> x5, Pallas kernels: 19.9 us -> 45.1 us  [the longest x2 17.1 us: rem_parts(): pl.pallas_call(functools.partial(rem_kernel, first, tables), out_shape=(p...]
    ppermute x8 -> x18, waiting for transfers between devices: 19.5 us -> 34.8 us  [turn(): return lax.ppermute(a, CZY, turn_pairs(s, flip))]
    all_to_all x2 -> x0, starting transfers between devices: 11.8 us -> none  [the longest x1 8.1 us: per_device(): lax.all_to_all(send_keys, ('z', 'y'), split_axis=1, concat_axis=1, tiled=...]
    all_to_all x2 -> x0, waiting for transfers between devices: 10.7 us -> none  [the longest x1 10.7 us: per_device(): lax.all_to_all(one.transpose(1, 0, 2, 3), CZY, 0, 0, tiled=True, axis_ind...]
    all_to_all x1, waiting for transfers between devices: 19.3 us -> 27.3 us  [per_device(): lax.all_to_all(send, ('z', 'y'), split_axis=0, concat_axis=0, tiled=True)]
    reduce_sum x4 -> x2, other arithmetic: 5.15 us -> 0.79 us  [update(): acc = acc_in + jnp.mean(grad * grad, axis=-1)]
    ppermute x8 -> x18, starting transfers between devices: 13.3 us -> 17.5 us  [turn(): return lax.ppermute(a, CZY, turn_pairs(s, flip))]
  transfers between devices with their start and end apart: 19 -> 27, of which waited for: 12 -> 18; matrix products, arithmetic and copies ran while one was open for 10% -> 7% of each run, Pallas kernels for 3% -> 17%
where the time goes in v2:
time: 187 us
  waiting for transfers between devices  73.1 us (39%)
  Pallas kernels  52.1 us (28%)
  starting transfers between devices  36.8 us (20%)
  other arithmetic  15.8 us (8%)
  local copies, waits for them, and re-layouts  4.05 us (2%)
  matrix products  3.54 us (2%)
    ppermute x18, waiting for transfers between devices, turn(): return lax.ppermute(a, CZY, turn_pairs(s, flip))  34.8 us
    all_to_all x1, waiting for transfers between devices, per_device(): lax.all_to_all(send, ('z', 'y'), split_axis=0, concat_axis=0, tiled=True)  27.3 us
    ppermute x18, starting transfers between devices, turn(): return lax.ppermute(a, CZY, turn_pairs(s, flip))  17.5 us
    pallas_call x2, Pallas kernels, rem_parts(): pl.pallas_call(functools.partial(rem_kernel, first, tables), out_shape=(p...  17.1 us
    pallas_call x1, Pallas kernels, quot_grads(): pl.pallas_call(functools.partial(quot_kernel, tables), out_shape=jax.Shap...  14.7 us
    pallas_call x2, Pallas kernels, place(): pl.pallas_call(functools.partial(place_kernel, rels), out_shape=jax.Shape...  13.3 us
    all_to_all x1, starting transfers between devices, per_device(): lax.all_to_all(send, ('z', 'y'), split_axis=0, concat_axis=0, tiled=True)  8.1 us
    pallas_call x1, Pallas kernels, pooled_dispatch(): pl.pallas_call(pooled_kernel, grid=(tables // pair,), out_shape=jax.Shape...  7.04 us
  transfers between devices with their start and end apart: 27, of which 18 were waited for; matrix products, arithmetic and copies ran while one was open for 7% of the time, Pallas kernels for 17%

profile of v2, /device:TPU:0, one launch (start us, length us, event | category | flops | bytes accessed | tf_op | source)
XLA Modules:
  0.0 186.5 jit_solution(13392831704327064750)
XLA Ops:
  0.7 2.4 %fusion.28 = f32[512,512]{0,1:T(8,128)S(1)} fusion(bf16[512,1024]{1,0:T(8,128)(2,1)} %param.12, bf16[1024,512]{1,0:T(8,128)(2,1)} %ci_ref.1), kind=kOutput, calls=%fused_computation.87 | convolution fusion | flops 536870912 | bytes 3145728 | tf_op jit(solution)/shard_map/dot_general | solution.py:407
  4.2 1.8 collective-permute-done
  6.5 3.2 %collective-permute-start.1 = (bf16[64,1024]{1,0:T(8,128)(2,1)S(1)}, bf16[64,1024]{1,0:T(8,128)(2,1)S(1)}, u32[]{:S(2)}, u32[]{:S(2)}) collective-permute-start(bf16[64,1024]{1,0:T(8,128)(2,1)S(1)} %get-tuple-element.32), channel_id=1, source_target_pairs={{0,64},{32,96},{64,0},{96,32},{1,65},{33,97},{65,1},{97,33},{2,66}... | collective-permute-start | bytes 393224 | tf_op jit(solution)/shard_map/ppermute | solution.py:365
  12.1 2.4 %collective-permute-done.1 = bf16[64,1024]{1,0:T(8,128)(2,1)S(1)} collective-permute-done((bf16[64,1024]{1,0:T(8,128)(2,1)S(1)}, bf16[64,1024]{1,0:T(8,128)(2,1)S(1)}, u32[]{:S(2)}, u32[]{:S(2)}) %collective-permute-start.1) | collective-permute-done | bytes 131104 | tf_op jit(solution)/shard_map/ppermute | solution.py:365
  14.4 2.2 %collective-permute-done.3 = bf16[64,1024]{1,0:T(8,128)(2,1)S(1)} collective-permute-done((bf16[64,1024]{1,0:T(8,128)(2,1)S(1)}, bf16[64,1024]{1,0:T(8,128)(2,1)S(1)}, u32[]{:S(2)}, u32[]{:S(2)}) %collective-permute-start.3) | collective-permute-done | bytes 131104 | tf_op jit(solution)/shard_map/ppermute | solution.py:365
  17.3 2.5 %collective-permute-start.4 = (bf16[64,1024]{1,0:T(8,128)(2,1)S(1)}, bf16[64,1024]{1,0:T(8,128)(2,1)S(1)}, u32[]{:S(2)}, u32[]{:S(2)}) collective-permute-start(bf16[64,1024]{1,0:T(8,128)(2,1)S(1)} %get-tuple-element.27), channel_id=1, source_target_pairs={{0,64},{32,96},{64,0},{96,32},{1,65},{33,97},{65,1},{97,33},{2,66}... | collective-permute-start | bytes 393224 | tf_op jit(solution)/shard_map/ppermute | solution.py:371
  20.8 2.6 %collective-permute-start.6 = (bf16[64,1024]{1,0:T(8,128)(2,1)S(1)}, bf16[64,1024]{1,0:T(8,128)(2,1)S(1)}, u32[]{:S(2)}, u32[]{:S(2)}) collective-permute-start(bf16[64,1024]{1,0:T(8,128)(2,1)S(1)} %get-tuple-element.27), channel_id=1, source_target_pairs={{0,96},{32,0},{64,32},{96,64},{1,97},{33,1},{65,33},{97,65},{2,98}... | collective-permute-start | bytes 393224 | tf_op jit(solution)/shard_map/ppermute | solution.py:371
  24.6 2.3 %collective-permute-done.5 = bf16[64,1024]{1,0:T(8,128)(2,1)S(1)} collective-permute-done((bf16[64,1024]{1,0:T(8,128)(2,1)S(1)}, bf16[64,1024]{1,0:T(8,128)(2,1)S(1)}, u32[]{:S(2)}, u32[]{:S(2)}) %collective-permute-start.5) | collective-permute-done | bytes 131104 | tf_op jit(solution)/shard_map/ppermute | solution.py:371
  30.2 7.0 %pooled_dispatch.1 = bf16[16,9,48,128]{3,2,1,0:T(8,128)(2,1)} custom-call(bf16[512,1024]{1,0:T(8,128)(2,1)} %pad_maximum_fusion.rank_ref, bf16[512,1024]{1,0:T(8,128)(2,1)} %cot_ref.1, bf16[1024,512]{1,0:T(8,128)(2,1)} %co_ref.1, bf16[1024,512]{1,0:T(8,128)(2,1)} %ci_ref.1, f32[1,1024]{1,0:T(1,128)} %bitcast.77, s32[8,1,512]{2,1,0:T(1,128)} %bitcast_add_fusion.pos_ref, ...), custom_call_target="tpu_custom_call" | custom-call | tf_op jit(solution)/shard_map/pooled_dispatch/pallas_call | solution.py:93
  37.2 8.1 %all-to-all-start = ((bf16[16,9,48,128]{3,2,1,0:T(8,128)(2,1)}), bf16[16,9,48,128]{3,2,1,0:T(8,128)(2,1)S(1)}, u32[]{:S(2)}, u32[]{:S(2)}) async-start(bf16[16,9,48,128]{3,2,1,0:T(8,128)(2,1)} %pooled_dispatch.1), calls=%async_computation | async-start | bytes 3538944 | tf_op jit(solution)/shard_map/all_to_all | solution.py:418
  46.0 27.3 %all-to-all-done.g_ref.key_ref = bf16[16,9,48,128]{3,2,1,0:T(8,128)(2,1)S(1)} async-done(((bf16[16,9,48,128]{3,2,1,0:T(8,128)(2,1)}), bf16[16,9,48,128]{3,2,1,0:T(8,128)(2,1)S(1)}, u32[]{:S(2)}, u32[]{:S(2)}) %all-to-all-start) | async-done | bytes 1769504 | tf_op jit(solution)/shard_map/all_to_all | solution.py:418
  74.5 8.5 %rem_parts.3 = (bf16[4,4,128,128]{3,2,1,0:T(8,128)(2,1)}, bf16[4,4,128,128]{3,2,1,0:T(8,128)(2,1)}, bf16[4,4,128,128]{3,2,1,0:T(8,128)(2,1)}, bf16[4,4,128,128]{3,2,1,0:T(8,128)(2,1)}) custom-call(s32[3]{0:T(128)} %pad_add_fusion.where_ref, bf16[16,9,48,128]{3,2,1,0:T(8,128)(2,1)} %copy-done.5, bf16[16,9,48,128]{3,2,1,0:T(8,128)(2,1)} %copy-done.5, ...), custom_call_target="tpu_custom_call" | custom-call | flops 3221225472 | bytes 4194304 | tf_op jit(solution)/shard_map/rem_parts/pallas_call | solution.py:208
  83.0 1.8 collective-permute-start.17
  84.8 8.5 %rem_parts.2 = (bf16[4,4,128,128]{3,2,1,0:T(8,128)(2,1)}, bf16[4,4,128,128]{3,2,1,0:T(8,128)(2,1)}, bf16[4,4,128,128]{3,2,1,0:T(8,128)(2,1)}, bf16[4,4,128,128]{3,2,1,0:T(8,128)(2,1)}) custom-call(s32[3]{0:T(128)} %pad_add_fusion.where_ref, bf16[16,9,48,128]{3,2,1,0:T(8,128)(2,1)} %copy-done.5, bf16[16,9,48,128]{3,2,1,0:T(8,128)(2,1)} %copy-done.5, ...), custom_call_target="tpu_custom_call" | custom-call | flops 3221225472 | bytes 4194304 | tf_op jit(solution)/shard_map/rem_parts/pallas_call | solution.py:208
  94.4 2.7 %collective-permute-start.18 = (bf16[4,4,128,128]{3,2,1,0:T(8,128)(2,1)S(1)}, bf16[4,4,128,128]{3,2,1,0:T(8,128)(2,1)S(1)}, u32[]{:S(2)}, u32[]{:S(2)}) collective-permute-start(bf16[4,4,128,128]{3,2,1,0:T(8,128)(2,1)S(1)} %add_convert_fusion.1), channel_id=1, source_target_pairs={{0,12},{1,13},{2,14},{3,15},{4,0},{5,1},{6,2},{7,3},{8,4},{9,5},{1... | collective-permute-start | bytes 1572872 | tf_op jit(solution)/shard_map/ppermute | solution.py:272
  98.9 5.1 %collective-permute-done.9 = bf16[4,4,128,128]{3,2,1,0:T(8,128)(2,1)S(1)} collective-permute-done((bf16[4,4,128,128]{3,2,1,0:T(8,128)(2,1)}, bf16[4,4,128,128]{3,2,1,0:T(8,128)(2,1)S(1)}, u32[]{:S(2)}, u32[]{:S(2)}) %collective-permute-start.9) | collective-permute-done | bytes 524320 | tf_op jit(solution)/shard_map/ppermute | solution.py:272
  105.5 4.2 %collective-permute-done.16 = bf16[4,4,128,128]{3,2,1,0:T(8,128)(2,1)S(1)} collective-permute-done((bf16[4,4,128,128]{3,2,1,0:T(8,128)(2,1)S(1)}, bf16[4,4,128,128]{3,2,1,0:T(8,128)(2,1)S(1)}, u32[]{:S(2)}, u32[]{:S(2)}) %collective-permute-start.16) | collective-permute-done | bytes 524320 | tf_op jit(solution)/shard_map/ppermute | solution.py:272
  110.7 5.2 %collective-permute-done.10 = bf16[4,4,128,128]{3,2,1,0:T(8,128)(2,1)S(1)} collective-permute-done((bf16[4,4,128,128]{3,2,1,0:T(8,128)(2,1)S(1)}, bf16[4,4,128,128]{3,2,1,0:T(8,128)(2,1)S(1)}, u32[]{:S(2)}, u32[]{:S(2)}) %collective-permute-start.10) | collective-permute-done | bytes 524320 | tf_op jit(solution)/shard_map/ppermute | solution.py:272
  116.4 2.8 %collective-permute-done.19 = bf16[4,4,128,128]{3,2,1,0:T(8,128)(2,1)S(1)} collective-permute-done((bf16[4,4,128,128]{3,2,1,0:T(8,128)(2,1)S(1)}, bf16[4,4,128,128]{3,2,1,0:T(8,128)(2,1)S(1)}, u32[]{:S(2)}, u32[]{:S(2)}) %collective-permute-start.19) | collective-permute-done | bytes 524320 | tf_op jit(solution)/shard_map/ppermute | solution.py:272
  123.2 3.4 %collective-permute-done.11 = bf16[4,4,128,128]{3,2,1,0:T(8,128)(2,1)S(1)} collective-permute-done((bf16[4,4,128,128]{3,2,1,0:T(8,128)(2,1)S(1)}, bf16[4,4,128,128]{3,2,1,0:T(8,128)(2,1)S(1)}, u32[]{:S(2)}, u32[]{:S(2)}) %collective-permute-start.11) | collective-permute-done | bytes 524320 | tf_op jit(solution)/shard_map/ppermute | solution.py:272
  126.6 5.6 %collective-permute-done.21 = bf16[4,4,128,128]{3,2,1,0:T(8,128)(2,1)S(1)} collective-permute-done((bf16[4,4,128,128]{3,2,1,0:T(8,128)(2,1)S(1)}, bf16[4,4,128,128]{3,2,1,0:T(8,128)(2,1)S(1)}, u32[]{:S(2)}, u32[]{:S(2)}) %collective-permute-start.21) | collective-permute-done | bytes 524320 | tf_op jit(solution)/shard_map/ppermute | solution.py:272
  133.9 3.9 %collective-permute-done.12 = bf16[4,4,128,128]{3,2,1,0:T(8,128)(2,1)S(1)} collective-permute-done((bf16[4,4,128,128]{3,2,1,0:T(8,128)(2,1)S(1)}, bf16[4,4,128,128]{3,2,1,0:T(8,128)(2,1)S(1)}, u32[]{:S(2)}, u32[]{:S(2)}) %collective-permute-start.12) | collective-permute-done | bytes 524320 | tf_op jit(solution)/shard_map/ppermute | solution.py:272
  138.2 1.8 subtract_convert_fusion.1
  140.0 2.0 %collective-permute-start.14 = (bf16[4,4,128,128]{3,2,1,0:T(8,128)(2,1)}, bf16[4,4,128,128]{3,2,1,0:T(8,128)(2,1)}, u32[]{:S(2)}, u32[]{:S(2)}) collective-permute-start(bf16[4,4,128,128]{3,2,1,0:T(8,128)(2,1)} %get-tuple-element.29.refs_0_), channel_id=1, source_target_pairs={{0,4},{1,5},{2,6},{3,7},{4,8},{5,9},{6,10},{7,11},{8,12},{9,13},{1... | collective-permute-start | bytes 1572872 | tf_op jit(solution)/shard_map/ppermute | solution.py:272
  142.1 14.7 %quot_grads.1 = f32[8,1024,128]{2,1,0:T(8,128)} custom-call(bf16[16,9,48,128]{3,2,1,0:T(8,128)(2,1)} %copy-done.5, bf16[16,9,48,128]{3,2,1,0:T(8,128)(2,1)} %copy-done.5, bf16[8,2048,128]{2,1,0:T(8,128)(2,1)} %rtab_ref.1), custom_call_target="tpu_custom_call" | custom-call | flops 6442450944 | bytes 8388608 | tf_op jit(solution)/shard_map/quot_grads/pallas_call | solution.py:253
  156.8 3.5 %multiply_reduce_fusion = f32[8,1024]{1,0:T(8,128)S(1)} fusion(f32[8,1024,128]{2,1,0:T(8,128)} %quot_grads.1), kind=kLoop, calls=%fused_computation.1 | loop fusion | flops 2088960 | bytes 4227072 | tf_op jit(solution)/shard_map/reduce_sum | solution.py:461
  160.9 3.2 %collective-permute-start.24 = (bf16[4,4,128,128]{3,2,1,0:T(8,128)(2,1)}, bf16[4,4,128,128]{3,2,1,0:T(8,128)(2,1)}, u32[]{:S(2)}, u32[]{:S(2)}) collective-permute-start(bf16[4,4,128,128]{3,2,1,0:T(8,128)(2,1)} %get-tuple-element.29.refs_0_), channel_id=1, source_target_pairs={{0,12},{1,13},{2,14},{3,15},{4,0},{5,1},{6,2},{7,3},{8,4},{9,5},{1... | collective-permute-start | bytes 1572872 | tf_op jit(solution)/shard_map/ppermute | solution.py:272
  164.2 2.0 %collective-permute-start.15 = (bf16[4,4,128,128]{3,2,1,0:T(8,128)(2,1)}, bf16[4,4,128,128]{3,2,1,0:T(8,128)(2,1)S(1)}, u32[]{:S(2)}, u32[]{:S(2)}) collective-permute-start(bf16[4,4,128,128]{3,2,1,0:T(8,128)(2,1)} %collective-permute-done.14.refs_4_), channel_id=1, source_target_pairs={{0,4},{1,5},{2,6},{3,7},{4,8},{5,9},{6,10},{7,11},{8,12},{9,13},{1... | collective-permute-start | bytes 1572872 | tf_op jit(solution)/shard_map/ppermute | solution.py:272
  166.2 2.2 %subtract_convert_fusion = bf16[8,1024,128]{2,1,0:T(8,128)(2,1)} fusion(f32[8,1024,128]{2,1,0:T(8,128)S(1)} %copy-done.1, bf16[8,1024,128]{2,1,0:T(8,128)(2,1)S(1)} %copy-done.4, f32[8,1024]{1,0:T(8,128)S(1)} %get-tuple-element.24), kind=kLoop, calls=%fused_computation | loop fusion | flops 4194304 | bytes 8421376 | tf_op jit(solution)/shard_map/convert_element_type | solution.py:465
  169.0 2.6 %collective-permute-done.25.refs_5_ = bf16[4,4,128,128]{3,2,1,0:T(8,128)(2,1)} collective-permute-done((bf16[4,4,128,128]{3,2,1,0:T(8,128)(2,1)}, bf16[4,4,128,128]{3,2,1,0:T(8,128)(2,1)}, u32[]{:S(2)}, u32[]{:S(2)}) %collective-permute-start.25) | collective-permute-done | bytes 524320 | tf_op jit(solution)/shard_map/ppermute | solution.py:272
  171.6 9.2 %place.2.refs_2_ = bf16[8,4,4,128,128]{4,3,2,1,0:T(8,128)(2,1)} custom-call(s32[3]{0:T(128)} %pad_add_fusion.where_ref, bf16[4,4,128,128]{3,2,1,0:T(8,128)(2,1)} %get-tuple-element.29.refs_0_, bf16[4,4,128,128]{3,2,1,0:T(8,128)(2,1)} %get-tuple-element.28.refs_1_, bf16[4,4,128,128]{3,2,1,0:T(8,128)(2,1)} %collective-permute-done.24.refs_2_, ...), custom_call_target="tpu_custom_call" | custom-call | bytes 6291456 | tf_op jit(solution)/shard_map/place/pallas_call | solution.py:337
  182.4 4.1 %place.3 = bf16[8,4,4,128,128]{4,3,2,1,0:T(8,128)(2,1)} custom-call(s32[3]{0:T(128)} %pad_add_fusion.where_ref, bf16[4,4,128,128]{3,2,1,0:T(8,128)(2,1)} %copy-done.8, bf16[4,4,128,128]{3,2,1,0:T(8,128)(2,1)} %copy-done.7, bf16[8,4,4,128,128]{4,3,2,1,0:T(8,128)(2,1)} %place.2.refs_2_), custom_call_target="tpu_custom_call", output_to_operand_aliasing={{}: (3, {})} | custom-call | bytes 2097152 | tf_op jit(solution)/shard_map/place/pallas_call | solution.py:337
  (102 shorter events, 26.3 us)
Async XLA Ops:
  0.6 119.7 %copy-start = (f32[8,2048]{1,0:T(8,128)S(1)}, f32[8,2048]{1,0:T(8,128)}, u32[]{:S(2)}) copy-start(f32[8,2048]{1,0:T(8,128)} %param.23) | copy-start | bytes 196612
  4.1 2.0 %collective-permute-start = (bf16[256,1024]{0,1:T(8,128)(2,1)S(1)}, bf16[256,1024]{0,1:T(8,128)(2,1)S(1)}, u32[]{:S(2)}, u32[]{:S(2)}) collective-permute-start(bf16[256,1024]{0,1:T(8,128)(2,1)S(1)} %fusion.4), channel_id=1, source_target_pairs={{0,16},{16,0},{1,17},{17,1},{2,18},{18,2},{3,19},{19,3},{4,20},{20... | collective-permute-start | bytes 1572872 | tf_op jit(solution)/shard_map/ppermute | solution.py:360
  6.5 8.0 %collective-permute-start.1 = (bf16[64,1024]{1,0:T(8,128)(2,1)S(1)}, bf16[64,1024]{1,0:T(8,128)(2,1)S(1)}, u32[]{:S(2)}, u32[]{:S(2)}) collective-permute-start(bf16[64,1024]{1,0:T(8,128)(2,1)S(1)} %get-tuple-element.32), channel_id=1, source_target_pairs={{0,64},{32,96},{64,0},{96,32},{1,65},{33,97},{65,1},{97,33},{2,66}... | collective-permute-start | bytes 393224 | tf_op jit(solution)/shard_map/ppermute | solution.py:365
  9.7 6.9 %collective-permute-start.3 = (bf16[64,1024]{1,0:T(8,128)(2,1)S(1)}, bf16[64,1024]{1,0:T(8,128)(2,1)S(1)}, u32[]{:S(2)}, u32[]{:S(2)}) collective-permute-start(bf16[64,1024]{1,0:T(8,128)(2,1)S(1)} %get-tuple-element.33), channel_id=1, source_target_pairs={{0,96},{32,0},{64,32},{96,64},{1,97},{33,1},{65,33},{97,65},{2,98}... | collective-permute-start | bytes 393224 | tf_op jit(solution)/shard_map/ppermute | solution.py:365
  10.8 6.3 %collective-permute-start.2 = (bf16[64,1024]{1,0:T(8,128)(2,1)S(1)}, bf16[64,1024]{1,0:T(8,128)(2,1)S(1)}, u32[]{:S(2)}, u32[]{:S(2)}) collective-permute-start(bf16[64,1024]{1,0:T(8,128)(2,1)S(1)} %get-tuple-element.34), channel_id=1, source_target_pairs={{0,32},{32,64},{64,96},{96,0},{1,33},{33,65},{65,97},{97,1},{2,34}... | collective-permute-start | bytes 393224 | tf_op jit(solution)/shard_map/ppermute | solution.py:365
  17.3 7.3 %collective-permute-start.4 = (bf16[64,1024]{1,0:T(8,128)(2,1)S(1)}, bf16[64,1024]{1,0:T(8,128)(2,1)S(1)}, u32[]{:S(2)}, u32[]{:S(2)}) collective-permute-start(bf16[64,1024]{1,0:T(8,128)(2,1)S(1)} %get-tuple-element.27), channel_id=1, source_target_pairs={{0,64},{32,96},{64,0},{96,32},{1,65},{33,97},{65,1},{97,33},{2,66}... | collective-permute-start | bytes 393224 | tf_op jit(solution)/shard_map/ppermute | solution.py:371
  20.1 6.9 %collective-permute-start.5 = (bf16[64,1024]{1,0:T(8,128)(2,1)S(1)}, bf16[64,1024]{1,0:T(8,128)(2,1)S(1)}, u32[]{:S(2)}, u32[]{:S(2)}) collective-permute-start(bf16[64,1024]{1,0:T(8,128)(2,1)S(1)} %get-tuple-element.27), channel_id=1, source_target_pairs={{0,32},{32,64},{64,96},{96,0},{1,33},{33,65},{65,97},{97,1},{2,34}... | collective-permute-start | bytes 393224 | tf_op jit(solution)/shard_map/ppermute | solution.py:371
  20.8 6.2 %collective-permute-start.6 = (bf16[64,1024]{1,0:T(8,128)(2,1)S(1)}, bf16[64,1024]{1,0:T(8,128)(2,1)S(1)}, u32[]{:S(2)}, u32[]{:S(2)}) collective-permute-start(bf16[64,1024]{1,0:T(8,128)(2,1)S(1)} %get-tuple-element.27), channel_id=1, source_target_pairs={{0,96},{32,0},{64,32},{96,64},{1,97},{33,1},{65,33},{97,65},{2,98}... | collective-permute-start | bytes 393224 | tf_op jit(solution)/shard_map/ppermute | solution.py:371
  27.0 2.0 %collective-permute-start.7 = (bf16[256,1024]{1,0:T(8,128)(2,1)S(1)}, bf16[256,1024]{1,0:T(8,128)(2,1)S(1)}, u32[]{:S(2)}, u32[]{:S(2)}) collective-permute-start(bf16[256,1024]{1,0:T(8,128)(2,1)S(1)} %bitcast.71), channel_id=1, source_target_pairs={{0,16},{16,0},{1,17},{17,1},{2,18},{18,2},{3,19},{19,3},{4,20},{20... | collective-permute-start | bytes 1572872 | tf_op jit(solution)/shard_map/ppermute | solution.py:374
  37.2 36.1 %all-to-all-start = ((bf16[16,9,48,128]{3,2,1,0:T(8,128)(2,1)}), bf16[16,9,48,128]{3,2,1,0:T(8,128)(2,1)S(1)}, u32[]{:S(2)}, u32[]{:S(2)}) async-start(bf16[16,9,48,128]{3,2,1,0:T(8,128)(2,1)} %pooled_dispatch.1), calls=%async_computation | async-start | bytes 3538944 | tf_op jit(solution)/shard_map/all_to_all | solution.py:418
  83.0 11.3 %copy-start.9 = (bf16[4,4,128,128]{3,2,1,0:T(8,128)(2,1)S(1)}, bf16[4,4,128,128]{3,2,1,0:T(8,128)(2,1)}, u32[]{:S(2)}) copy-start(bf16[4,4,128,128]{3,2,1,0:T(8,128)(2,1)} %get-tuple-element.18) | copy-start | bytes 1572868
  83.0 11.3 %collective-permute-start.17 = (bf16[4,4,128,128]{3,2,1,0:T(8,128)(2,1)}, bf16[4,4,128,128]{3,2,1,0:T(8,128)(2,1)S(1)}, u32[]{:S(2)}, u32[]{:S(2)}) collective-permute-start(bf16[4,4,128,128]{3,2,1,0:T(8,128)(2,1)} %get-tuple-element.19), channel_id=1, source_target_pairs={{0,12},{1,13},{2,14},{3,15},{4,0},{5,1},{6,2},{7,3},{8,4},{9,5},{1... | collective-permute-start | bytes 1572872 | tf_op jit(solution)/shard_map/ppermute | solution.py:272
  93.4 16.3 %copy-start.11 = (bf16[4,4,128,128]{3,2,1,0:T(8,128)(2,1)S(1)}, bf16[4,4,128,128]{3,2,1,0:T(8,128)(2,1)}, u32[]{:S(2)}) copy-start(bf16[4,4,128,128]{3,2,1,0:T(8,128)(2,1)} %get-tuple-element.16) | copy-start | bytes 1572868
  93.4 10.7 %collective-permute-start.9 = (bf16[4,4,128,128]{3,2,1,0:T(8,128)(2,1)}, bf16[4,4,128,128]{3,2,1,0:T(8,128)(2,1)S(1)}, u32[]{:S(2)}, u32[]{:S(2)}) collective-permute-start(bf16[4,4,128,128]{3,2,1,0:T(8,128)(2,1)} %get-tuple-element.15), channel_id=1, source_target_pairs={{0,4},{1,5},{2,6},{3,7},{4,8},{5,9},{6,10},{7,11},{8,12},{9,13},{1... | collective-permute-start | bytes 1572872 | tf_op jit(solution)/shard_map/ppermute | solution.py:272
  93.7 15.9 %collective-permute-start.16 = (bf16[4,4,128,128]{3,2,1,0:T(8,128)(2,1)S(1)}, bf16[4,4,128,128]{3,2,1,0:T(8,128)(2,1)S(1)}, u32[]{:S(2)}, u32[]{:S(2)}) collective-permute-start(bf16[4,4,128,128]{3,2,1,0:T(8,128)(2,1)S(1)} %copy-done.16), channel_id=1, source_target_pairs={{0,4},{1,5},{2,6},{3,7},{4,8},{5,9},{6,10},{7,11},{8,12},{9,13},{1... | collective-permute-start | bytes 1572872 | tf_op jit(solution)/shard_map/ppermute | solution.py:272
  94.4 21.4 %copy-start.10 = (bf16[4,4,128,128]{3,2,1,0:T(8,128)(2,1)S(1)}, bf16[4,4,128,128]{3,2,1,0:T(8,128)(2,1)}, u32[]{:S(2)}) copy-start(bf16[4,4,128,128]{3,2,1,0:T(8,128)(2,1)} %get-tuple-element.12) | copy-start | bytes 1572868
  94.4 15.2 %collective-permute-start.18 = (bf16[4,4,128,128]{3,2,1,0:T(8,128)(2,1)S(1)}, bf16[4,4,128,128]{3,2,1,0:T(8,128)(2,1)S(1)}, u32[]{:S(2)}, u32[]{:S(2)}) collective-permute-start(bf16[4,4,128,128]{3,2,1,0:T(8,128)(2,1)S(1)} %add_convert_fusion.1), channel_id=1, source_target_pairs={{0,12},{1,13},{2,14},{3,15},{4,0},{5,1},{6,2},{7,3},{8,4},{9,5},{1... | collective-permute-start | bytes 1572872 | tf_op jit(solution)/shard_map/ppermute | solution.py:272
  97.2 13.5 %collective-permute-start.8 = (bf16[4,4,128,128]{3,2,1,0:T(8,128)(2,1)}, bf16[4,4,128,128]{3,2,1,0:T(8,128)(2,1)S(1)}, u32[]{:S(2)}, u32[]{:S(2)}) collective-permute-start(bf16[4,4,128,128]{3,2,1,0:T(8,128)(2,1)} %get-tuple-element.13), channel_id=1, source_target_pairs={{0,12},{1,13},{2,14},{3,15},{4,0},{5,1},{6,2},{7,3},{8,4},{9,5},{1... | collective-permute-start | bytes 1572872 | tf_op jit(solution)/shard_map/ppermute | solution.py:272
  105.2 10.6 %collective-permute-start.10 = (bf16[4,4,128,128]{3,2,1,0:T(8,128)(2,1)S(1)}, bf16[4,4,128,128]{3,2,1,0:T(8,128)(2,1)S(1)}, u32[]{:S(2)}, u32[]{:S(2)}) collective-permute-start(bf16[4,4,128,128]{3,2,1,0:T(8,128)(2,1)S(1)} %add_convert_fusion.3), channel_id=1, source_target_pairs={{0,4},{1,5},{2,6},{3,7},{4,8},{5,9},{6,10},{7,11},{8,12},{9,13},{1... | collective-permute-start | bytes 1572872 | tf_op jit(solution)/shard_map/ppermute | solution.py:272
  109.9 9.2 %collective-permute-start.19 = (bf16[4,4,128,128]{3,2,1,0:T(8,128)(2,1)S(1)}, bf16[4,4,128,128]{3,2,1,0:T(8,128)(2,1)S(1)}, u32[]{:S(2)}, u32[]{:S(2)}) collective-permute-start(bf16[4,4,128,128]{3,2,1,0:T(8,128)(2,1)S(1)} %add_convert_fusion), channel_id=1, source_target_pairs={{0,3},{1,0},{2,1},{3,2},{4,7},{5,4},{6,5},{7,6},{8,11},{9,8},{10,9... | collective-permute-start | bytes 1572872 | tf_op jit(solution)/shard_map/ppermute | solution.py:272
  116.1 10.5 %collective-permute-start.11 = (bf16[4,4,128,128]{3,2,1,0:T(8,128)(2,1)S(1)}, bf16[4,4,128,128]{3,2,1,0:T(8,128)(2,1)S(1)}, u32[]{:S(2)}, u32[]{:S(2)}) collective-permute-start(bf16[4,4,128,128]{3,2,1,0:T(8,128)(2,1)S(1)} %add_convert_fusion.2), channel_id=1, source_target_pairs={{0,1},{1,2},{2,3},{3,0},{4,5},{5,6},{6,7},{7,4},{8,9},{9,10},{10,1... | collective-permute-start | bytes 1572872 | tf_op jit(solution)/shard_map/ppermute | solution.py:272
  116.2 16.0 %collective-permute-start.21 = (bf16[4,4,128,128]{3,2,1,0:T(8,128)(2,1)S(1)}, bf16[4,4,128,128]{3,2,1,0:T(8,128)(2,1)S(1)}, u32[]{:S(2)}, u32[]{:S(2)}) collective-permute-start(bf16[4,4,128,128]{3,2,1,0:T(8,128)(2,1)S(1)} %add_convert_fusion), channel_id=1, source_target_pairs={{0,1},{1,2},{2,3},{3,0},{4,5},{5,6},{6,7},{7,4},{8,9},{9,10},{10,1... | collective-permute-start | bytes 1572872 | tf_op jit(solution)/shard_map/ppermute | solution.py:272
  119.1 13.0 %collective-permute-start.20 = (bf16[4,4,128,128]{3,2,1,0:T(8,128)(2,1)S(1)}, bf16[4,4,128,128]{3,2,1,0:T(8,128)(2,1)S(1)}, u32[]{:S(2)}, u32[]{:S(2)}) collective-permute-start(bf16[4,4,128,128]{3,2,1,0:T(8,128)(2,1)S(1)} %collective-permute-done.19), channel_id=1, source_target_pairs={{0,3},{1,0},{2,1},{3,2},{4,7},{5,4},{6,5},{7,6},{8,11},{9,8},{10,9... | collective-permute-start | bytes 1572872 | tf_op jit(solution)/shard_map/ppermute | solution.py:272
  122.0 11.9 %collective-permute-start.13 = (bf16[4,4,128,128]{3,2,1,0:T(8,128)(2,1)S(1)}, bf16[4,4,128,128]{3,2,1,0:T(8,128)(2,1)S(1)}, u32[]{:S(2)}, u32[]{:S(2)}) collective-permute-start(bf16[4,4,128,128]{3,2,1,0:T(8,128)(2,1)S(1)} %add_convert_fusion.2), channel_id=1, source_target_pairs={{0,3},{1,0},{2,1},{3,2},{4,7},{5,4},{6,5},{7,6},{8,11},{9,8},{10,9... | collective-permute-start | bytes 1572872 | tf_op jit(solution)/shard_map/ppermute | solution.py:272
  126.6 11.2 %collective-permute-start.12 = (bf16[4,4,128,128]{3,2,1,0:T(8,128)(2,1)S(1)}, bf16[4,4,128,128]{3,2,1,0:T(8,128)(2,1)S(1)}, u32[]{:S(2)}, u32[]{:S(2)}) collective-permute-start(bf16[4,4,128,128]{3,2,1,0:T(8,128)(2,1)S(1)} %collective-permute-done.11), channel_id=1, source_target_pairs={{0,1},{1,2},{2,3},{3,0},{4,5},{5,6},{6,7},{7,4},{8,9},{9,10},{10,1... | collective-permute-start | bytes 1572872 | tf_op jit(solution)/shard_map/ppermute | solution.py:272
  140.0 24.1 %collective-permute-start.22 = (bf16[4,4,128,128]{3,2,1,0:T(8,128)(2,1)}, bf16[4,4,128,128]{3,2,1,0:T(8,128)(2,1)}, u32[]{:S(2)}, u32[]{:S(2)}) collective-permute-start(bf16[4,4,128,128]{3,2,1,0:T(8,128)(2,1)} %get-tuple-element.28.refs_1_), channel_id=1, source_target_pairs={{0,12},{1,13},{2,14},{3,15},{4,0},{5,1},{6,2},{7,3},{8,4},{9,5},{1... | collective-permute-start | bytes 1572872 | tf_op jit(solution)/shard_map/ppermute | solution.py:272
  140.0 24.2 %collective-permute-start.14 = (bf16[4,4,128,128]{3,2,1,0:T(8,128)(2,1)}, bf16[4,4,128,128]{3,2,1,0:T(8,128)(2,1)}, u32[]{:S(2)}, u32[]{:S(2)}) collective-permute-start(bf16[4,4,128,128]{3,2,1,0:T(8,128)(2,1)} %get-tuple-element.29.refs_0_), channel_id=1, source_target_pairs={{0,4},{1,5},{2,6},{3,7},{4,8},{5,9},{6,10},{7,11},{8,12},{9,13},{1... | collective-permute-start | bytes 1572872 | tf_op jit(solution)/shard_map/ppermute | solution.py:272
  142.0 24.1 %copy-start.4 = (bf16[8,1024,128]{2,1,0:T(8,128)(2,1)S(1)}, bf16[8,1024,128]{2,1,0:T(8,128)(2,1)}, u32[]{:S(2)}) copy-start(bf16[8,1024,128]{2,1,0:T(8,128)(2,1)} %slab_ref.3) | copy-start | bytes 6291460
  160.9 10.7 %collective-permute-start.25 = (bf16[4,4,128,128]{3,2,1,0:T(8,128)(2,1)}, bf16[4,4,128,128]{3,2,1,0:T(8,128)(2,1)}, u32[]{:S(2)}, u32[]{:S(2)}) collective-permute-start(bf16[4,4,128,128]{3,2,1,0:T(8,128)(2,1)} %get-tuple-element.28.refs_1_), channel_id=1, source_target_pairs={{0,4},{1,5},{2,6},{3,7},{4,8},{5,9},{6,10},{7,11},{8,12},{9,13},{1... | collective-permute-start | bytes 1572872 | tf_op jit(solution)/shard_map/ppermute | solution.py:272
  160.9 10.7 %collective-permute-start.24 = (bf16[4,4,128,128]{3,2,1,0:T(8,128)(2,1)}, bf16[4,4,128,128]{3,2,1,0:T(8,128)(2,1)}, u32[]{:S(2)}, u32[]{:S(2)}) collective-permute-start(bf16[4,4,128,128]{3,2,1,0:T(8,128)(2,1)} %get-tuple-element.29.refs_0_), channel_id=1, source_target_pairs={{0,12},{1,13},{2,14},{3,15},{4,0},{5,1},{6,2},{7,3},{8,4},{9,5},{1... | collective-permute-start | bytes 1572872 | tf_op jit(solution)/shard_map/ppermute | solution.py:272
  164.2 16.6 %collective-permute-start.23 = (bf16[4,4,128,128]{3,2,1,0:T(8,128)(2,1)}, bf16[4,4,128,128]{3,2,1,0:T(8,128)(2,1)S(1)}, u32[]{:S(2)}, u32[]{:S(2)}) collective-permute-start(bf16[4,4,128,128]{3,2,1,0:T(8,128)(2,1)} %collective-permute-done.22.refs_3_), channel_id=1, source_target_pairs={{0,12},{1,13},{2,14},{3,15},{4,0},{5,1},{6,2},{7,3},{8,4},{9,5},{1... | collective-permute-start | bytes 1572872 | tf_op jit(solution)/shard_map/ppermute | solution.py:272
  164.2 16.6 %collective-permute-start.15 = (bf16[4,4,128,128]{3,2,1,0:T(8,128)(2,1)}, bf16[4,4,128,128]{3,2,1,0:T(8,128)(2,1)S(1)}, u32[]{:S(2)}, u32[]{:S(2)}) collective-permute-start(bf16[4,4,128,128]{3,2,1,0:T(8,128)(2,1)} %collective-permute-done.14.refs_4_), channel_id=1, source_target_pairs={{0,4},{1,5},{2,6},{3,7},{4,8},{5,9},{6,10},{7,11},{8,12},{9,13},{1... | collective-permute-start | bytes 1572872 | tf_op jit(solution)/shard_map/ppermute | solution.py:272
  (12 other events, 56.6 us)

commit v3 on v2

v3 whole, which is shorter than its diff:
```python
import functools

import jax
import jax.numpy as jnp
from jax import lax
from jax.experimental import pallas as pl
from jax.experimental.pallas import tpu as pltpu
from jax.sharding import Mesh
from jax.sharding import PartitionSpec as P


step_rate = 0.3
epsilon = 1e-06
bf = jnp.bfloat16
f32 = jnp.float32
NX, NC, NZ, NY = 4, 2, 4, 4
CZY = ("c", "z", "y")
NT = (((1,), (1,)), ((), ()))


def ring(n, s):
    return [(i, (i + s) % n) for i in range(n)]


def spot(c, z, y):
    return (c * NZ + z) * NY + y


def turn_pairs(s, flip):
    out = []
    for c in range(NC):
        for z in range(NZ):
            for y in range(NY):
                if (c == 0) != flip:
                    to = spot(c, (z + s) % NZ, y)
                else:
                    to = spot(c, z, (y + s) % NY)
                out.append((spot(c, z, y), to))
    return out


def rank_kernel(half_ref, feat_ref, cot_ref, ci_ref, co_ref, out_ref, acc_ref):
    step = pl.program_id(0)
    rank = ci_ref.shape[1]
    feat = feat_ref[...]
    product = (cot_ref[...].astype(f32) * feat.astype(f32)).astype(bf)

    @pl.when(step == 0)
    def _():
        acc_ref[...] = jnp.zeros_like(acc_ref)

    acc_ref[:, :rank] += jnp.dot(feat, ci_ref[...], preferred_element_type=f32)
    acc_ref[:, rank:] += jnp.dot(product, co_ref[...], preferred_element_type=f32)

    @pl.when(step == pl.num_programs(0) - 1)
    def _():
        out_ref[...] = acc_ref[...].astype(out_ref.dtype)


def rank_part(half, feat, cot, ci, co, dtype):
    size = feat.shape[0] // NC
    depth, rank = ci.shape
    tile = depth // 4
    return pl.pallas_call(
        rank_kernel,
        out_shape=jax.ShapeDtypeStruct((size, 2 * rank), dtype),
        grid_spec=pltpu.PrefetchScalarGridSpec(
            num_scalar_prefetch=1,
            grid=(depth // tile,),
            in_specs=[
                pl.BlockSpec((size, tile), lambda k, h: (h[0], k)),
                pl.BlockSpec((size, tile), lambda k, h: (h[0], k)),
                pl.BlockSpec((tile, rank), lambda k, h: (k, 0)),
                pl.BlockSpec((tile, rank), lambda k, h: (k, 0)),
            ],
            out_specs=pl.BlockSpec((size, 2 * rank), lambda k, h: (0, 0)),
            scratch_shapes=[pltpu.VMEM((size, 2 * rank), f32)],
        ),
        cost_estimate=pl.CostEstimate(
            flops=4 * size * depth * rank, bytes_accessed=4 << 20, transcendentals=0
        ),
        compiler_params=pltpu.CompilerParams(vmem_limit_bytes=16 << 20),
        name="rank_part",
    )(half, feat, cot, ci, co)


def mix_kernel(x_ref, keep_ref, got_ref, *outs):
    size = outs[0].shape[0]
    for k, out in enumerate(outs):
        at = pl.ds(pl.multiple_of((x_ref[0] + k) % NX * size, size), size)
        out[...] = (keep_ref[at, :] + got_ref[at, :].astype(f32)).astype(bf)


def mix(xi, keep, got):
    piece = jax.ShapeDtypeStruct((keep.shape[0] // NX, keep.shape[1]), bf)
    vmem = pl.BlockSpec(memory_space=pltpu.VMEM)
    return pl.pallas_call(
        mix_kernel,
        out_shape=(piece,) * NX,
        grid_spec=pltpu.PrefetchScalarGridSpec(
            num_scalar_prefetch=1, grid=(), in_specs=[vmem] * 2, out_specs=[vmem] * NX
        ),
        compiler_params=pltpu.CompilerParams(vmem_limit_bytes=8 << 20),
        name="mix",
    )(xi, keep, got)


def pooled_kernel(at_ref, *refs):
    pieces, (cot_ref, co_ref, ci_ref, bias_ref, pos_ref, dig_ref, out_ref, key_ref, rank_ref) = (
        refs[: NC * NX],
        refs[NC * NX :],
    )
    rank = co_ref.shape[1]
    width, cap = key_ref.shape[1], CAP

    @pl.when(pl.program_id(0) == 0)
    def _():
        size = pieces[0].shape[0]
        for i, piece in enumerate(pieces):
            c = at_ref[0] if i < NX else 1 - at_ref[0]
            row = (c * NX + (at_ref[1] + NX - i % NX) % NX) * size
            rank_ref[pl.ds(pl.multiple_of(row, size), size), :] = piece[...]

    dests = out_ref.shape[0]
    tables = (out_ref.shape[1] - KEY_ROWS) // cap
    samples = cot_ref.shape[0]
    here = pos_ref.shape[0]
    step = pl.program_id(0)
    gate = (
        lax.dot_general(rank_ref[:, :rank], co_ref[...], NT, preferred_element_type=f32)
        + bias_ref[...]
    )
    back = lax.dot_general(rank_ref[:, rank:], ci_ref[...], NT, preferred_element_type=f32)
    pooled = (cot_ref[...].astype(f32) * (gate + 1.0) + back).astype(bf)
    slot = lax.broadcasted_iota(jnp.int32, (dests * cap, samples), 0)
    owner = lax.broadcasted_iota(jnp.int32, (samples, width), 1) % LANES // DIGITS
    keys = jnp.zeros((dests * cap, width), f32)
    for k in range(here):
        t = step * here + k
        placed = jnp.where(slot == pos_ref[k], 1.0, 0.0).astype(bf)
        digits = jnp.where(owner == t, dig_ref[...].astype(f32), 0.0).astype(bf)
        both = jnp.concatenate([pooled[:, k * width : (k + 1) * width], digits], axis=1)
        rows = jnp.dot(placed, both, preferred_element_type=f32)
        spot = pl.ds(pl.multiple_of(t * cap, KEY_ROWS), cap)
        out_ref[:, spot] = rows[:, :width].astype(bf).reshape(dests, cap, width)
        keys = keys + rows[:, width:]

    @pl.when(step == 0)
    def _():
        key_ref[...] = keys

    @pl.when(step > 0)
    def _():
        key_ref[...] += keys

    @pl.when(step == pl.num_programs(0) - 1)
    def _():
        parts = key_ref[...].reshape(dests, cap // KEY_ROWS, KEY_ROWS, width)
        group = lax.broadcasted_iota(jnp.int32, (dests, KEY_ROWS, width), 2) // LANES
        packed = jnp.zeros((dests, KEY_ROWS, width), f32)
        for k in range(cap // KEY_ROWS):
            packed = jnp.where(group == k, parts[:, k], packed)
        out_ref[:, tables * cap :] = packed.astype(bf)


def pooled_dispatch(where, pieces, cot, co, ci, bias, pos, digits, dests, cap, width):
    samples = cot.shape[0]
    tables = pos.shape[0]
    pair = 2
    out = (dests, tables * cap + KEY_ROWS, width)
    return pl.pallas_call(
        pooled_kernel,
        out_shape=jax.ShapeDtypeStruct(out, bf),
        grid_spec=pltpu.PrefetchScalarGridSpec(
            num_scalar_prefetch=1,
            grid=(tables // pair,),
            in_specs=[pl.BlockSpec(memory_space=pltpu.VMEM)] * len(pieces)
            + [
                pl.BlockSpec((samples, pair * width), lambda i, w: (0, i)),
                pl.BlockSpec((pair * width, co.shape[1]), lambda i, w: (i, 0)),
                pl.BlockSpec((pair * width, co.shape[1]), lambda i, w: (i, 0)),
                pl.BlockSpec((1, pair * width), lambda i, w: (0, i)),
                pl.BlockSpec((pair, 1, samples), lambda i, w: (i, 0, 0)),
                pl.BlockSpec(digits.shape, lambda i, w: (0, 0)),
            ],
            out_specs=pl.BlockSpec(out, lambda i, w: (0, 0, 0)),
            scratch_shapes=[
                pltpu.VMEM((dests * cap, width), f32),
                pltpu.VMEM((samples, pieces[0].shape[1]), bf),
            ],
        ),
        compiler_params=pltpu.CompilerParams(vmem_limit_bytes=16 << 20),
        name="pooled_dispatch",
    )(where, *pieces, cot, co, ci, bias, pos, digits)


DIGITS, QB, MB, LANES, KEY_ROWS, CAP = 4, 32, 64, 32, 16, 48
PARTS = 2


def digit_lanes(q, m, width):
    parts = jnp.stack([q // QB, q % QB, m // MB, m % MB], axis=1)
    parts = parts.reshape(-1, q.shape[1])
    parts = jnp.concatenate([parts] * (CAP // KEY_ROWS), axis=0)
    parts = jnp.pad(parts, ((0, width - parts.shape[0]), (0, 0)))
    return parts.T.astype(bf)


def unpack_keys(packed):
    sources, _, width = packed.shape
    group = lax.broadcasted_iota(jnp.int32, packed.shape, 2) // LANES
    packed = packed.astype(f32)
    parts = [jnp.where(group == k, packed, 0.0)[:, None] for k in range(CAP // KEY_ROWS)]
    return jnp.concatenate(parts, axis=1).reshape(sources * CAP, width).astype(bf)


def key_rows(keys, tables):
    width = keys.shape[1]
    lane = lax.broadcasted_iota(jnp.int32, (width, width), 0) % LANES
    col = lax.broadcasted_iota(jnp.int32, (width, width), 1)
    t = col % tables
    base = DIGITS * t + jnp.where(col >= tables, 2, 0)
    high = jnp.where(col >= tables, MB, QB).astype(f32)
    comb = jnp.where(lane == base, high, jnp.where(lane == base + 1, 1.0, 0.0))
    comb = jnp.where(col < 2 * tables, comb, 0.0).astype(bf)
    return jnp.dot(keys, comb, preferred_element_type=f32).T


def key_lanes(keys, t):
    width = keys.shape[1]
    lane = lax.broadcasted_iota(jnp.int32, (width, 2 * width), 0) % LANES - DIGITS * t
    side = lax.broadcasted_iota(jnp.int32, (width, 2 * width), 1) >= width
    lane = jnp.where(side, lane - 2, lane)
    high = jnp.where(side, float(MB), float(QB))
    comb = jnp.where(lane == 0, high, jnp.where(lane == 1, 1.0, 0.0)).astype(bf)
    out = jnp.dot(keys, comb, preferred_element_type=f32)
    return out[:, :width], out[:, width:]


def pick(key, tab):
    slots, width = key.shape
    half = tab.shape[0] // 2
    both = jnp.concatenate([tab[:half], tab[half:]], axis=1)
    size = slots // PARTS
    out = []
    for p in range(PARTS):
        part = key[p * size : (p + 1) * size]
        high = part >= half
        low = jnp.where(high, part - half, part)
        lane = lax.broadcasted_iota(jnp.int32, (size, width), 1).astype(f32)
        hot = jnp.concatenate(
            [jnp.where(low - j == lane, 1.0, 0.0).astype(bf) for j in range(0, half, width)],
            axis=1,
        )
        got = jnp.dot(hot, both, preferred_element_type=f32)
        out.append(jnp.where(high, got[:, width:], got[:, :width]))
    return jnp.concatenate(out, axis=0)


def spread(row, key, rows, val, store):
    slots = row.shape[1]
    width = val.shape[1]
    half = rows // 2
    low = jnp.where(row >= half, row - half, row)
    high = key >= half
    both = jnp.concatenate(
        [jnp.where(high, 0.0, val).astype(bf), jnp.where(high, val, 0.0).astype(bf)], axis=1
    )
    size = half // PARTS
    at = lax.broadcasted_iota(jnp.int32, (size, slots), 0).astype(f32)
    for p in range(PARTS):
        hot = jnp.where(at == low - p * size, 1.0, 0.0).astype(bf)
        sums = jnp.dot(hot, both, preferred_element_type=f32)
        store(p * size, sums[:, :width])
        store(half + p * size, sums[:, width:])


def rem_kernel(
    first, tables, where_ref, got_ref, slab_ref, r0, r1, r2, r3,
    g_buf, pack_buf, slab_buf, sum_ref, sem, pack_sem,
):
    count, sources, cap, width = g_buf.shape
    slots = sources * cap
    rem_rows = sum_ref.shape[0]
    pack = pltpu.make_async_copy(
        got_ref.at[:, pl.ds(tables * cap, KEY_ROWS)], pack_buf, pack_sem
    )
    pack.start()

    def inputs(k):
        return (
            pltpu.make_async_copy(
                got_ref.at[:, pl.ds((first + k) * cap, cap)], g_buf.at[k], sem.at[0, k]
            ),
            pltpu.make_async_copy(slab_ref.at[first + k], slab_buf.at[k], sem.at[1, k]),
        )

    copies = [inputs(k) for k in range(count)]
    for pair in copies:
        for copy in pair:
            copy.start()
    pack.wait()
    keys = unpack_keys(pack_buf[...])
    rows = key_rows(keys, tables)
    sub_rows = r0.shape[2]
    at = where_ref[1]
    along_z = where_ref[0] == 0
    for k in range(count):
        for copy in copies[k]:
            copy.wait()
        t = first + k
        g = g_buf[k].reshape(slots, width).astype(f32)
        q, m = key_lanes(keys, t)
        val = g * pick(q, slab_buf[k])


        def store(at, sums):
            sum_ref[at : at + sums.shape[0]] = sums.astype(bf)

        spread(rows[tables + t : tables + t + 1], m, rem_rows, val, store)
        for rel, ref in enumerate((r0, r1, r2, r3)):
            far = (at + rel) % 4
            for sub in range(4):
                block = jnp.where(along_z, far * NY + sub, sub * NY + far)
                start = pl.multiple_of(block * sub_rows, sub_rows)
                ref[k, sub] = sum_ref[pl.ds(start, sub_rows), :]


def rem_parts(first, count, where, got, slab, rem_rows):
    sources, _, width = got.shape
    tables, quot_rows, _ = slab.shape
    slots = sources * CAP
    slab = pltpu.with_memory_space_constraint(slab, pltpu.HBM)
    sub = rem_rows // (NZ * NY)
    piece = jax.ShapeDtypeStruct((count, 4, sub, width), bf)
    return pl.pallas_call(
        functools.partial(rem_kernel, first, tables),
        out_shape=(piece,) * 4,
        grid_spec=pltpu.PrefetchScalarGridSpec(
            num_scalar_prefetch=1,
            grid=(),
            in_specs=[
                pl.BlockSpec(memory_space=pl.ANY),
                pl.BlockSpec(memory_space=pltpu.HBM),
            ],
            out_specs=[pl.BlockSpec(memory_space=pltpu.VMEM)] * 4,
            scratch_shapes=[
                pltpu.VMEM((count, sources, CAP, width), bf),
                pltpu.VMEM((sources, KEY_ROWS, width), bf),
                pltpu.VMEM((count, quot_rows, width), bf),
                pltpu.VMEM((rem_rows, width), bf),
                pltpu.SemaphoreType.DMA((2, count)),
                pltpu.SemaphoreType.DMA,
            ],
        ),
        cost_estimate=pl.CostEstimate(
            flops=count * 4 * slots * rem_rows * width, bytes_accessed=1 << 22, transcendentals=0
        ),
        compiler_params=pltpu.CompilerParams(vmem_limit_bytes=16 << 20),
        name="rem_parts",
    )(where, got, slab)


def quot_kernel(first, tables, g_ref, pack_ref, rtab_ref, *refs):
    quot_ref, key_ref, row_ref = refs[-3:]
    sources, cap, width = g_ref.shape
    slots = sources * cap
    quot_rows = quot_ref.shape[1]
    step = pl.program_id(0)
    t = first + step

    @pl.when(step == 0)
    def _():
        keys = unpack_keys(pack_ref[...])
        key_ref[...] = keys
        row_ref[...] = key_rows(keys, tables)

    g = g_ref[...].reshape(slots, width).astype(f32)
    q, m = key_lanes(key_ref[...], t)
    val = g * pick(m, rtab_ref[0])

    def store(at, sums):
        quot_ref[0, at : at + sums.shape[0]] = sums

    spread(row_ref[pl.ds(t, 1), :], q, quot_rows, val, store)


def quot_grads(first, count, got, rtab, quot_rows, old=None):
    sources, _, width = got.shape
    tables, rem_rows, _ = rtab.shape
    slots = sources * CAP
    rtab = pltpu.with_memory_space_constraint(rtab, pltpu.HBM)
    ins, extra, alias = [got, got, rtab], [], {}
    if old is not None:
        ins.append(old)
        extra = [pl.BlockSpec(memory_space=pltpu.HBM)]
        alias = {3: 0}
    return pl.pallas_call(
        functools.partial(quot_kernel, first, tables),
        out_shape=jax.ShapeDtypeStruct((tables, quot_rows, width), f32),
        grid=(count,),
        in_specs=[
            pl.BlockSpec((sources, CAP, width), lambda t: (0, first + t, 0)),
            pl.BlockSpec((sources, KEY_ROWS, width), lambda t: (0, tables * CAP // KEY_ROWS, 0)),
            pl.BlockSpec((1, rem_rows, width), lambda t: (first + t, 0, 0)),
        ]
        + extra,
        out_specs=pl.BlockSpec((1, quot_rows, width), lambda t: (first + t, 0, 0)),
        scratch_shapes=[pltpu.VMEM((slots, width), bf), pltpu.VMEM((width, slots), f32)],
        input_output_aliases=alias,
        cost_estimate=pl.CostEstimate(
            flops=count * 4 * slots * rem_rows * width, bytes_accessed=1 << 23, transcendentals=0
        ),
        compiler_params=pltpu.CompilerParams(vmem_limit_bytes=16 << 20),
        name="quot_grads",
    )(*ins)


def turn(a, s, flip):
    return lax.ppermute(a, CZY, turn_pairs(s, flip))


def add(*parts):
    total = parts[0].astype(f32)
    for p in parts[1:]:
        total = total + p.astype(f32)
    return total


def ring_scatter(low, high, flip):
    far_low = turn(low[2], 1, flip)
    near_low = turn(low[3], -1, flip)
    far_high = turn(high[2], -1, flip)
    near_high = turn(high[1], 1, flip)
    sum_low = turn(add(low[1], far_low).astype(bf), 1, flip)
    sum_high = turn(add(high[3], far_high).astype(bf), -1, flip)
    return add(low[0], near_low, sum_low), add(high[0], near_high, sum_high)


def ring_gather(low, high, flip):
    prev_low = turn(low, 1, flip)
    next_high = turn(high, -1, flip)
    next_low = turn(low, -1, flip)
    prev_high = turn(high, 1, flip)
    far_low = turn(prev_low, 1, flip)
    far_high = turn(next_high, -1, flip)
    return [low, next_low, far_low, prev_low], [high, next_high, far_high, prev_high]


def place_kernel(rels, where_ref, *refs):
    count = 2 * len(rels)
    ins = refs[:count]
    out_ref, buf, in_sem, out_sem = refs[-4:]
    half = out_ref.shape[0] // 2
    at = where_ref[1]

    def move(along_z):
        takes = [pltpu.make_async_copy(ins[i], buf.at[i], in_sem.at[i]) for i in range(count)]
        puts = []
        for i in range(count):
            far = (at + rels[i // 2]) % 4
            tabs = pl.ds(i % 2 * half, half)
            to = out_ref.at[tabs, far] if along_z else out_ref.at[tabs, :, far]
            puts.append(pltpu.make_async_copy(buf.at[i], to, out_sem.at[i]))
        for take in takes:
            take.start()
        for take, put in zip(takes, puts):
            take.wait()
            put.start()
        for put in puts:
            put.wait()

    pl.when(where_ref[0] == 0)(lambda: move(True))
    pl.when(where_ref[0] != 0)(lambda: move(False))


def place(rels, where, pieces, shape, old=None):
    ins = [x for lh in pieces for x in lh]
    count = len(ins)
    alias = {}
    if old is not None:
        ins.append(old)
        alias = {len(ins): 0}
    hbm = pl.BlockSpec(memory_space=pl.ANY)
    return pl.pallas_call(
        functools.partial(place_kernel, rels),
        out_shape=jax.ShapeDtypeStruct(shape, bf),
        grid_spec=pltpu.PrefetchScalarGridSpec(
            num_scalar_prefetch=1,
            grid=(),
            in_specs=[hbm] * len(ins),
            out_specs=hbm,
            scratch_shapes=[
                pltpu.VMEM((count,) + ins[0].shape, bf),
                pltpu.SemaphoreType.DMA((count,)),
                pltpu.SemaphoreType.DMA((count,)),
            ],
        ),
        input_output_aliases=alias,
        cost_estimate=pl.CostEstimate(flops=0, bytes_accessed=len(rels) << 21, transcendentals=0),
        compiler_params=pltpu.CompilerParams(vmem_limit_bytes=8 << 20),
        name="place",
    )(where, *ins)


def rank_sums(feat, cot, cross_in, cross_out):
    ci = lax.axis_index("c").astype(jnp.int32).reshape(1)
    xi = lax.axis_index("x").astype(jnp.int32).reshape(1)
    swap = lambda a: lax.ppermute(a, "c", [(0, 1), (1, 0)])
    got = swap(rank_part(1 - ci, feat, cot, cross_in, cross_out, bf))
    keep = rank_part(ci, feat, cot, cross_in, cross_out, f32)
    parts = mix(xi, keep, got)
    far = lax.ppermute(parts[2], "x", ring(NX, 2))
    nxt = lax.ppermute(parts[1], "x", ring(NX, 1))
    prev = lax.ppermute(parts[3], "x", ring(NX, 3))
    mine = add(parts[0], far, nxt, prev).astype(bf)
    far = lax.ppermute(mine, "x", ring(NX, 2))
    prev = lax.ppermute(mine, "x", ring(NX, 1))
    nxt = lax.ppermute(mine, "x", ring(NX, 3))
    own = (mine, prev, far, nxt)
    return own + tuple(swap(a) for a in own)


def update_kernel(own_ref, next_ref, far_ref, prev_ref, acc_ref, tab_ref, new_ref, out_ref):
    tables, subs, _, width = own_ref.shape
    accs = acc_ref[...].T
    lane = lax.broadcasted_iota(jnp.int32, accs.shape, 1)
    done = jnp.zeros_like(accs)
    for i in range(tables * subs):
        t, s = divmod(i, subs)
        grad = (own_ref[t, s].astype(f32) + far_ref[t, s].astype(f32)) + (
            next_ref[t, s].astype(f32) + prev_ref[t, s].astype(f32)
        )
        mean = jnp.sum(grad * grad, axis=1, keepdims=True) * (1.0 / width)
        acc = accs[:, i : i + 1] + mean
        new = tab_ref[t, s].astype(f32) - step_rate * grad * lax.rsqrt(acc + epsilon)
        new_ref[t, s] = new.astype(bf)
        done = jnp.where(lane == i, acc, done)
    out_ref[...] = done.T


def update(ring_parts, acc, tab):
    vmem = pl.BlockSpec(memory_space=pltpu.VMEM)
    tables, subs, rows, _ = tab.shape
    new, out = pl.pallas_call(
        update_kernel,
        out_shape=(
            jax.ShapeDtypeStruct(tab.shape, bf),
            jax.ShapeDtypeStruct((tables * subs, rows), f32),
        ),
        in_specs=[vmem] * 6,
        out_specs=(vmem, vmem),
        cost_estimate=pl.CostEstimate(flops=tab.size * 8, bytes_accessed=4 << 20, transcendentals=0),
        compiler_params=pltpu.CompilerParams(vmem_limit_bytes=12 << 20),
        name="update",
    )(*ring_parts, acc.reshape(tables * subs, rows), tab)
    return out.reshape(acc.shape), new


def device_step(
    features, cotangent, cross_in, cross_out, bias, dest_shard, quot_row, rem_row,
    quot_slab, quot_accum, rem_table, rem_accum,
):
    samples = features.shape[0]
    tables = quot_slab.shape[0]
    width = quot_slab.shape[2]
    rem_rows = rem_table.shape[1]
    rows = NZ * NY
    cap = CAP
    ci, zi, yi = lax.axis_index("c"), lax.axis_index("z"), lax.axis_index("y")

    target = dest_shard[:, :, 0]
    onehot = target[:, :, None] == jnp.arange(rows, dtype=jnp.int32)[None, None, :]
    lower = (
        jnp.arange(samples, dtype=jnp.int32)[:, None]
        >= jnp.arange(samples, dtype=jnp.int32)[None, :]
    ).astype(bf)
    running = jnp.einsum("ij,tjn->tin", lower, onehot.astype(bf), preferred_element_type=f32)
    slot_index = jnp.sum(jnp.where(onehot, running, 0.0), axis=2).astype(jnp.int32) - 1
    position = target * cap + slot_index
    digits = digit_lanes(quot_row, rem_row, width)

    pieces = rank_sums(features, cotangent, cross_in, cross_out)
    xi = lax.axis_index("x")
    send = pooled_dispatch(
        jnp.stack([ci, xi]).astype(jnp.int32), pieces, cotangent, cross_out, cross_in,
        bias.reshape(1, -1), position.reshape(tables, 1, samples), digits, rows, cap, width,
    )
    got = lax.all_to_all(send, ("z", "y"), split_axis=0, concat_axis=0, tiled=True)
    along_z = ci == 0
    at_one = jnp.where(along_z, zi, yi)
    at_two = jnp.where(along_z, yi, zi)
    where = jnp.stack([ci, at_one, at_one]).astype(jnp.int32)
    half = tables // 2
    low = rem_parts(0, half, where, got, quot_slab, rem_rows)
    high = rem_parts(half, half, where, got, quot_slab, rem_rows)

    one_low, one_high = ring_scatter(low, high, False)
    ring_low, ring_high = ring_gather(one_low.astype(bf), one_high.astype(bf), True)
    share = rem_rows // rows
    view = (tables, NZ, NY, share)

    def quarter(a):
        a = a.reshape(view + a.shape[2:])
        return jnp.where(
            along_z,
            lax.dynamic_index_in_dim(a, zi, 1, keepdims=False),
            lax.dynamic_index_in_dim(a, yi, 2, keepdims=False),
        )

    acc_in, tab_in = quarter(rem_accum), quarter(rem_table)
    acc_low, new_low = update(ring_low, acc_in[:half], tab_in[:half])
    acc_high, new_high = update(ring_high, acc_in[half:], tab_in[half:])
    acc = jnp.concatenate([acc_low, acc_high], axis=0)
    rem_acc_out = lax.dynamic_index_in_dim(acc, at_two, 1, keepdims=False)
    all_low, all_high = ring_gather(new_low, new_high, False)
    shape = (tables, NZ, NY, share, width)
    near = [(all_low[k], all_high[k]) for k in (0, 1, 3)]
    rem_out = place((0, 1, 3), where, near, shape)
    rem_out = place((2,), where, [(all_low[2], all_high[2])], shape, rem_out)
    rem_out = rem_out.reshape(tables, rem_rows, width)

    quot_rows = quot_slab.shape[1]
    quot_grad = quot_grads(0, half, got, rem_table, quot_rows)
    quot_grad = quot_grads(half, half, got, rem_table, quot_rows, quot_grad)
    quot_acc_out = quot_accum + jnp.mean(quot_grad * quot_grad, axis=-1)
    quot_out = (
        quot_slab.astype(f32)
        - step_rate * quot_grad * lax.rsqrt(quot_acc_out + epsilon)[..., None]
    ).astype(bf)
    return (quot_out, quot_acc_out, rem_out, rem_acc_out)


def solution(mesh):
    fine = Mesh(mesh.devices.reshape(NX, NC, NZ, NY), ("x", "c", "z", "y"))
    T, R = ("x", "c"), ("z", "y")
    return jax.shard_map(
        device_step,
        mesh=fine,
        in_specs=(
            P(R, T), P(R, T), P(T, None), P(T, None), P(T), P(T, R, None), P(T, R), P(T, R),
            P(T, R, None), P(T, R), P(T, None, None), P(T, None),
        ),
        out_specs=(P(T, R, None), P(T, R), P(T, None, None), P(T, R)),
        check_vma=False,
    )
```

time: 187 us -> 173 us (0.925)
  waiting for transfers between devices: 73.1 us -> 61.4 us
  local copies, waits for them, and re-layouts: 4.05 us -> 10.8 us
  Pallas kernels: 52.1 us -> 46.8 us
  matrix products: 3.54 us -> 0.3 us
  other arithmetic: 15.8 us -> 12.6 us
  starting transfers between devices: 36.8 us -> 39.4 us
    ppermute x18, waiting for transfers between devices: 34.8 us -> 21.1 us  [turn(): return lax.ppermute(a, CZY, turn_pairs(s, flip))]
    pallas_call x2, Pallas kernels: 13.3 us -> 4.15 us  [place(): pl.pallas_call(functools.partial(place_kernel, rels), out_shape=jax.Shape...]
    pallas_call x2 -> x8, Pallas kernels: 21.8 us -> 30.2 us  [the longest x2 11.8 us: quot_grads(): pl.pallas_call(functools.partial(quot_kernel, first, tables), out_shape=j...]
    ppermute x18, starting transfers between devices: 17.5 us -> 22.3 us  [turn(): return lax.ppermute(a, CZY, turn_pairs(s, flip))]
    pallas_call x2, Pallas kernels: 17.1 us -> 12.5 us  [rem_parts(): pl.pallas_call(functools.partial(rem_kernel, first, tables), out_shape=(p...]
    unnamed x35 -> x37, local copies, waits for them, and re-layouts: 2.89 us -> 7.36 us
    dot_general x3 -> x1, matrix products: 3.54 us -> 0.3 us  [device_step(): jnp.einsum('ij,tjn->tin', lower, onehot.astype(bf), preferred_element_typ...]
    reduce_sum x3 -> x1, other arithmetic: 4.27 us -> 1.15 us  [device_step(): quot_acc_out = quot_accum + jnp.mean(quot_grad * quot_grad, axis=-1)]
  transfers between devices with their start and end apart: 27 -> 30, of which waited for: 18 -> 14; matrix products, arithmetic and copies ran while one was open for 7% -> 9% of each run, Pallas kernels for 17% -> 17%
where the time goes in v3:
time: 173 us
  waiting for transfers between devices  61.4 us (35%)
  Pallas kernels  46.8 us (27%)
  starting transfers between devices  39.4 us (23%)
  other arithmetic  12.6 us (7%)
  local copies, waits for them, and re-layouts  10.8 us (6%)
    all_to_all x1, waiting for transfers between devices, device_step(): lax.all_to_all(send, ('z', 'y'), split_axis=0, concat_axis=0, tiled=True)  27.3 us
    ppermute x18, starting transfers between devices, turn(): return lax.ppermute(a, CZY, turn_pairs(s, flip))  22.3 us
    ppermute x18, waiting for transfers between devices, turn(): return lax.ppermute(a, CZY, turn_pairs(s, flip))  21.1 us
    pallas_call x2, Pallas kernels, rem_parts(): pl.pallas_call(functools.partial(rem_kernel, first, tables), out_shape=(p...  12.5 us
    pallas_call x2, Pallas kernels, quot_grads(): pl.pallas_call(functools.partial(quot_kernel, first, tables), out_shape=j...  11.8 us
    all_to_all x1, starting transfers between devices, device_step(): lax.all_to_all(send, ('z', 'y'), split_axis=0, concat_axis=0, tiled=True)  8.06 us
    unnamed x37, local copies, waits for them, and re-layouts  7.36 us
    pallas_call x2, Pallas kernels, update(): pl.pallas_call(update_kernel, out_shape=(jax.ShapeDtypeStruct(tab.shape,...  6.7 us
  transfers between devices with their start and end apart: 30, of which 14 were waited for; matrix products, arithmetic and copies ran while one was open for 9% of the time, Pallas kernels for 17%

profile of v3, /device:TPU:0, one launch (start us, length us, event | category | flops | bytes accessed | tf_op | source)
XLA Modules:
  0.0 172.6 jit_solution(11522357457608113854)
XLA Ops:
  5.6 2.6 %rank_part.3 = bf16[256,1024]{1,0:T(8,128)(2,1)} custom-call(s32[1]{0:T(128)S(6)} %sub.22.half_ref, bf16[512,1024]{1,0:T(8,128)(2,1)S(1)} %copy-done.8, bf16[512,1024]{1,0:T(8,128)(2,1)S(1)} %copy-done.1, bf16[1024,512]{1,0:T(8,128)(2,1)S(1)} %copy-done.3, bf16[1024,512]{1,0:T(8,128)(2,1)S(1)} %copy-done.5), custom_call_target="tpu_custom_call" | custom-call | flops 536870912 | bytes 4194304 | tf_op jit(solution)/shard_map/rank_part/pallas_call | solution.py:64
  9.5 1.8 %rank_part.2.keep_ref = f32[256,1024]{1,0:T(8,128)S(1)} custom-call(s32[1]{0:T(128)} %bitcast.half_ref, bf16[512,1024]{1,0:T(8,128)(2,1)S(1)} %copy-done.9, bf16[512,1024]{1,0:T(8,128)(2,1)S(1)} %copy-done.2, bf16[1024,512]{1,0:T(8,128)(2,1)S(1)} %copy-done.4, bf16[1024,512]{1,0:T(8,128)(2,1)S(1)} %copy-done.6), custom_call_target="tpu_custom_call" | custom-call | flops 536870912 | bytes 4194304 | tf_op jit(solution)/shard_map/rank_part/pallas_call | solution.py:64
  12.8 2.9 %collective-permute-start.3 = (bf16[64,1024]{1,0:T(8,128)(2,1)S(1)}, bf16[64,1024]{1,0:T(8,128)(2,1)S(1)}, u32[]{:S(2)}, u32[]{:S(2)}) collective-permute-start(bf16[64,1024]{1,0:T(8,128)(2,1)S(1)} %get-tuple-element.23), channel_id=1, source_target_pairs={{0,96},{32,0},{64,32},{96,64},{1,97},{33,1},{65,33},{97,65},{2,98}... | collective-permute-start | bytes 393224 | tf_op jit(solution)/shard_map/ppermute | solution.py:515
  15.7 2.3 %collective-permute-start.1 = (bf16[64,1024]{1,0:T(8,128)(2,1)S(1)}, bf16[64,1024]{1,0:T(8,128)(2,1)S(1)}, u32[]{:S(2)}, u32[]{:S(2)}) collective-permute-start(bf16[64,1024]{1,0:T(8,128)(2,1)S(1)} %get-tuple-element.21), channel_id=1, source_target_pairs={{0,64},{32,96},{64,0},{96,32},{1,65},{33,97},{65,1},{97,33},{2,66}... | collective-permute-start | bytes 393224 | tf_op jit(solution)/shard_map/ppermute | solution.py:513
  19.2 6.2 %collective-permute-done.2 = bf16[64,1024]{1,0:T(8,128)(2,1)S(1)} collective-permute-done((bf16[64,1024]{1,0:T(8,128)(2,1)S(1)}, bf16[64,1024]{1,0:T(8,128)(2,1)S(1)}, u32[]{:S(2)}, u32[]{:S(2)}) %collective-permute-start.2) | collective-permute-done | bytes 131104 | tf_op jit(solution)/shard_map/ppermute | solution.py:514
  25.5 1.9 %collective-permute-start.5 = (bf16[64,1024]{1,0:T(8,128)(2,1)S(1)}, bf16[64,1024]{1,0:T(8,128)(2,1)}, u32[]{:S(2)}, u32[]{:S(2)}) collective-permute-start(bf16[64,1024]{1,0:T(8,128)(2,1)S(1)} %add_convert_fusion.4.refs_0_), channel_id=1, source_target_pairs={{0,64},{32,96},{64,0},{96,32},{1,65},{33,97},{65,1},{97,33},{2,66}... | collective-permute-start | bytes 393224 | tf_op jit(solution)/shard_map/ppermute | solution.py:517
  28.9 5.4 %collective-permute-done.4.refs_1_ = bf16[64,1024]{1,0:T(8,128)(2,1)S(1)} collective-permute-done((bf16[64,1024]{1,0:T(8,128)(2,1)S(1)}, bf16[64,1024]{1,0:T(8,128)(2,1)S(1)}, u32[]{:S(2)}, u32[]{:S(2)}) %collective-permute-start.4) | collective-permute-done | bytes 131104 | tf_op jit(solution)/shard_map/ppermute | solution.py:518
  38.6 6.2 %pooled_dispatch.1 = bf16[16,400,128]{2,1,0:T(8,128)(2,1)S(1)} custom-call(s32[2]{0:T(128)S(1)} %pad_add_fusion.at_ref, bf16[64,1024]{1,0:T(8,128)(2,1)S(1)} %add_convert_fusion.4.refs_0_, bf16[64,1024]{1,0:T(8,128)(2,1)S(1)} %collective-permute-done.4.refs_1_, bf16[64,1024]{1,0:T(8,128)(2,1)} %collective-permute-done.5.refs_2_, ...), custom_call_target="tpu_custom_call" | custom-call | tf_op jit(solution)/shard_map/pooled_dispatch/pallas_call | solution.py:171
  45.9 8.1 %all-to-all-start = ((bf16[16,400,128]{2,1,0:T(8,128)(2,1)}), bf16[16,400,128]{2,1,0:T(8,128)(2,1)S(1)}, u32[]{:S(2)}, u32[]{:S(2)}) async-start(bf16[16,400,128]{2,1,0:T(8,128)(2,1)} %copy-done.7), calls=%async_computation | async-start | bytes 3276800 | tf_op jit(solution)/shard_map/all_to_all | solution.py:589
  54.1 27.3 %all-to-all-done.g_ref.pack_ref.got_ref = bf16[16,400,128]{2,1,0:T(8,128)(2,1)S(1)} async-done(((bf16[16,400,128]{2,1,0:T(8,128)(2,1)}), bf16[16,400,128]{2,1,0:T(8,128)(2,1)S(1)}, u32[]{:S(2)}, u32[]{:S(2)}) %all-to-all-start) | async-done | bytes 1638432 | tf_op jit(solution)/shard_map/all_to_all | solution.py:589
  81.4 5.8 %rem_parts.2 = (bf16[4,4,128,128]{3,2,1,0:T(8,128)(2,1)S(1)}, bf16[4,4,128,128]{3,2,1,0:T(8,128)(2,1)S(1)}, bf16[4,4,128,128]{3,2,1,0:T(8,128)(2,1)S(1)}, bf16[4,4,128,128]{3,2,1,0:T(8,128)(2,1)S(1)}) custom-call(s32[3]{0:T(128)S(1)} %pad_add_fusion.1.where_ref, bf16[16,400,128]{2,1,0:T(8,128)(2,1)S(1)} %all-to-all-done.g_ref.pack_ref.got_ref, ...), custom_call_target="tpu_custom_call" | custom-call | flops 3221225472 | bytes 4194304 | tf_op jit(solution)/shard_map/rem_parts/pallas_call | solution.py:336
  87.7 6.7 %rem_parts.3 = (bf16[4,4,128,128]{3,2,1,0:T(8,128)(2,1)S(1)}, bf16[4,4,128,128]{3,2,1,0:T(8,128)(2,1)}, bf16[4,4,128,128]{3,2,1,0:T(8,128)(2,1)}, bf16[4,4,128,128]{3,2,1,0:T(8,128)(2,1)S(1)}) custom-call(s32[3]{0:T(128)S(1)} %pad_add_fusion.1.where_ref, bf16[16,400,128]{2,1,0:T(8,128)(2,1)S(1)} %all-to-all-done.g_ref.pack_ref.got_ref, ...), custom_call_target="tpu_custom_call" | custom-call | flops 3221225472 | bytes 4194304 | tf_op jit(solution)/shard_map/rem_parts/pallas_call | solution.py:336
  94.5 3.0 %collective-permute-start.20 = (bf16[4,4,128,128]{3,2,1,0:T(8,128)(2,1)}, bf16[4,4,128,128]{3,2,1,0:T(8,128)(2,1)}, u32[]{:S(2)}, u32[]{:S(2)}) collective-permute-start(bf16[4,4,128,128]{3,2,1,0:T(8,128)(2,1)} %get-tuple-element.32), channel_id=1, source_target_pairs={{0,12},{1,13},{2,14},{3,15},{4,0},{5,1},{6,2},{7,3},{8,4},{9,5},{1... | collective-permute-start | bytes 1572872 | tf_op jit(solution)/shard_map/ppermute | solution.py:420
  98.8 1.6 collective-permute-start.13
  100.4 4.0 %collective-permute-done.20 = bf16[4,4,128,128]{3,2,1,0:T(8,128)(2,1)} collective-permute-done((bf16[4,4,128,128]{3,2,1,0:T(8,128)(2,1)}, bf16[4,4,128,128]{3,2,1,0:T(8,128)(2,1)}, u32[]{:S(2)}, u32[]{:S(2)}) %collective-permute-start.20) | collective-permute-done | bytes 524320 | tf_op jit(solution)/shard_map/ppermute | solution.py:420
  105.7 3.8 %collective-permute-start.21 = (bf16[4,4,128,128]{3,2,1,0:T(8,128)(2,1)S(1)}, bf16[4,4,128,128]{3,2,1,0:T(8,128)(2,1)S(1)}, u32[]{:S(2)}, u32[]{:S(2)}) collective-permute-start(bf16[4,4,128,128]{3,2,1,0:T(8,128)(2,1)S(1)} %add_convert_fusion.1), channel_id=1, source_target_pairs={{0,12},{1,13},{2,14},{3,15},{4,0},{5,1},{6,2},{7,3},{8,4},{9,5},{1... | collective-permute-start | bytes 1572872 | tf_op jit(solution)/shard_map/ppermute | solution.py:420
  109.5 2.6 %bitcast_select_fusion = bf16[8,4,128,128]{3,2,1,0:T(8,128)(2,1)} fusion(bf16[8,4,4,128,128]{4,3,2,1,0:T(8,128)(2,1)} %bitcast.56, s32[]{:T(128)S(6)} %select_n.69, s32[]{:T(128)S(6)} %select_n.68, pred[]{:T(512)S(6)} %eq.25), kind=kLoop, calls=%fused_computation.5 | loop fusion | flops 524288 | bytes 3145737 | tf_op jit(solution)/shard_map/jit(_where)/select_n | solution.py:605
  118.6 2.0 %collective-permute-start.24 = (bf16[4,4,128,128]{3,2,1,0:T(8,128)(2,1)S(1)}, bf16[4,4,128,128]{3,2,1,0:T(8,128)(2,1)S(1)}, u32[]{:S(2)}, u32[]{:S(2)}) collective-permute-start(bf16[4,4,128,128]{3,2,1,0:T(8,128)(2,1)S(1)} %add_convert_fusion.own_ref), channel_id=1, source_target_pairs={{0,1},{1,2},{2,3},{3,0},{4,5},{5,6},{6,7},{7,4},{8,9},{9,10},{10,1... | collective-permute-start | bytes 1572872 | tf_op jit(solution)/shard_map/ppermute | solution.py:420
  120.5 3.5 %collective-permute-done.15.prev_ref = bf16[4,4,128,128]{3,2,1,0:T(8,128)(2,1)} collective-permute-done((bf16[4,4,128,128]{3,2,1,0:T(8,128)(2,1)S(1)}, bf16[4,4,128,128]{3,2,1,0:T(8,128)(2,1)}, u32[]{:S(2)}, u32[]{:S(2)}) %collective-permute-start.15) | collective-permute-done | bytes 524320 | tf_op jit(solution)/shard_map/ppermute | solution.py:420
  124.1 1.9 %collective-permute-done.22.next_ref = bf16[4,4,128,128]{3,2,1,0:T(8,128)(2,1)S(1)} collective-permute-done((bf16[4,4,128,128]{3,2,1,0:T(8,128)(2,1)S(1)}, bf16[4,4,128,128]{3,2,1,0:T(8,128)(2,1)S(1)}, u32[]{:S(2)}, u32[]{:S(2)}) %collective-permute-start.22) | collective-permute-done | bytes 524320 | tf_op jit(solution)/shard_map/ppermute | solution.py:420
  127.5 5.9 %quot_grads.2.refs_0_ = f32[8,1024,128]{2,1,0:T(8,128)S(1)} custom-call(bf16[16,400,128]{2,1,0:T(8,128)(2,1)S(1)} %all-to-all-done.g_ref.pack_ref.got_ref, bf16[16,400,128]{2,1,0:T(8,128)(2,1)S(1)} %all-to-all-done.g_ref.pack_ref.got_ref, bf16[8,2048,128]{2,1,0:T(8,128)(2,1)} %rtab_ref.3), custom_call_target="tpu_custom_call" | custom-call | flops 3221225472 | bytes 8388608 | tf_op jit(solution)/shard_map/quot_grads/pallas_call | solution.py:398
  133.4 1.8 %collective-permute-done.16.far_ref = bf16[4,4,128,128]{3,2,1,0:T(8,128)(2,1)S(1)} collective-permute-done((bf16[4,4,128,128]{3,2,1,0:T(8,128)(2,1)}, bf16[4,4,128,128]{3,2,1,0:T(8,128)(2,1)S(1)}, u32[]{:S(2)}, u32[]{:S(2)}) %collective-permute-start.16) | collective-permute-done | bytes 524320 | tf_op jit(solution)/shard_map/ppermute | solution.py:420
  135.2 3.8 %update.2 = (bf16[4,4,128,128]{3,2,1,0:T(8,128)(2,1)S(1)}, f32[16,128]{1,0:T(8,128)S(1)}) custom-call(bf16[4,4,128,128]{3,2,1,0:T(8,128)(2,1)S(1)} %add_convert_fusion.2.own_ref, bf16[4,4,128,128]{3,2,1,0:T(8,128)(2,1)S(1)} %collective-permute-done.14.next_ref, bf16[4,4,128,128]{3,2,1,0:T(8,128)(2,1)S(1)} %collective-permute-done.16.far_ref, ...), custom_call_target="tpu_custom_call" | custom-call | flops 2097152 | bytes 4194304 | tf_op jit(solution)/shard_map/update/pallas_call | solution.py:545
  139.4 2.9 %update.3 = (bf16[4,4,128,128]{3,2,1,0:T(8,128)(2,1)S(1)}, f32[16,128]{1,0:T(8,128)S(1)}) custom-call(bf16[4,4,128,128]{3,2,1,0:T(8,128)(2,1)S(1)} %add_convert_fusion.own_ref, bf16[4,4,128,128]{3,2,1,0:T(8,128)(2,1)S(1)} %collective-permute-done.22.next_ref, bf16[4,4,128,128]{3,2,1,0:T(8,128)(2,1)S(1)} %collective-permute-done.23.far_ref, ...), custom_call_target="tpu_custom_call" | custom-call | flops 2097152 | bytes 4194304 | tf_op jit(solution)/shard_map/update/pallas_call | solution.py:545
  142.2 3.2 %collective-permute-start.25 = (bf16[4,4,128,128]{3,2,1,0:T(8,128)(2,1)S(1)}, bf16[4,4,128,128]{3,2,1,0:T(8,128)(2,1)S(1)}, u32[]{:S(2)}, u32[]{:S(2)}) collective-permute-start(bf16[4,4,128,128]{3,2,1,0:T(8,128)(2,1)S(1)} %get-tuple-element.33.refs_1_), channel_id=1, source_target_pairs={{0,12},{1,13},{2,14},{3,15},{4,0},{5,1},{6,2},{7,3},{8,4},{9,5},{1... | collective-permute-start | bytes 1572872 | tf_op jit(solution)/shard_map/ppermute | solution.py:420
  145.5 5.9 %quot_grads.3 = f32[8,1024,128]{2,1,0:T(8,128)S(1)} custom-call(bf16[16,400,128]{2,1,0:T(8,128)(2,1)S(1)} %all-to-all-done.g_ref.pack_ref.got_ref, bf16[16,400,128]{2,1,0:T(8,128)(2,1)S(1)} %all-to-all-done.g_ref.pack_ref.got_ref, bf16[8,2048,128]{2,1,0:T(8,128)(2,1)} %rtab_ref.3, f32[8,1024,128]{2,1,0:T(8,128)S(1)} %quot_grads.2.refs_0_), custom_call_target="tpu_custom_call", output_to_operand_aliasing={{}: (3, {})} | custom-call | flops 3221225472 | bytes 8388608 | tf_op jit(solution)/shard_map/quot_grads/pallas_call | solution.py:398
  155.2 3.2 %collective-permute-start.26 = (bf16[4,4,128,128]{3,2,1,0:T(8,128)(2,1)S(1)}, bf16[4,4,128,128]{3,2,1,0:T(8,128)(2,1)S(1)}, u32[]{:S(2)}, u32[]{:S(2)}) collective-permute-start(bf16[4,4,128,128]{3,2,1,0:T(8,128)(2,1)S(1)} %collective-permute-done.25.refs_3_), channel_id=1, source_target_pairs={{0,12},{1,13},{2,14},{3,15},{4,0},{5,1},{6,2},{7,3},{8,4},{9,5},{1... | collective-permute-start | bytes 1572872 | tf_op jit(solution)/shard_map/ppermute | solution.py:420
  158.4 2.2 %subtract_convert_fusion = bf16[8,1024,128]{2,1,0:T(8,128)(2,1)} fusion(f32[8,1024,128]{2,1,0:T(8,128)S(1)} %quot_grads.3, bf16[8,1024,128]{2,1,0:T(8,128)(2,1)S(1)} %copy-done.13, f32[8,1024]{1,0:T(8,128)S(1)} %get-tuple-element.36), kind=kLoop, calls=%fused_computation | loop fusion | flops 4194304 | bytes 8421376 | tf_op jit(solution)/shard_map/convert_element_type | solution.py:630
  162.3 2.8 %collective-permute-done.28.refs_5_ = bf16[4,4,128,128]{3,2,1,0:T(8,128)(2,1)S(1)} collective-permute-done((bf16[4,4,128,128]{3,2,1,0:T(8,128)(2,1)S(1)}, bf16[4,4,128,128]{3,2,1,0:T(8,128)(2,1)S(1)}, u32[]{:S(2)}, u32[]{:S(2)}) %collective-permute-start.28) | collective-permute-done | bytes 524320 | tf_op jit(solution)/shard_map/ppermute | solution.py:420
  165.1 2.5 %place.2.refs_2_ = bf16[8,4,4,128,128]{4,3,2,1,0:T(8,128)(2,1)} custom-call(s32[3]{0:T(128)S(1)} %pad_add_fusion.1.where_ref, bf16[4,4,128,128]{3,2,1,0:T(8,128)(2,1)S(1)} %get-tuple-element.28.refs_0_, bf16[4,4,128,128]{3,2,1,0:T(8,128)(2,1)S(1)} %get-tuple-element.33.refs_1_, bf16[4,4,128,128]{3,2,1,0:T(8,128)(2,1)S(1)} %collective-permute-done.27.refs_2_, ...), custom_call_target="tpu_custom_call" | custom-call | bytes 6291456 | tf_op jit(solution)/shard_map/place/pallas_call | solution.py:485
  167.7 3.1 %collective-permute-done.18.refs_0_ = bf16[4,4,128,128]{3,2,1,0:T(8,128)(2,1)S(1)} collective-permute-done((bf16[4,4,128,128]{3,2,1,0:T(8,128)(2,1)S(1)}, bf16[4,4,128,128]{3,2,1,0:T(8,128)(2,1)S(1)}, u32[]{:S(2)}, u32[]{:S(2)}) %collective-permute-start.18) | collective-permute-done | bytes 524320 | tf_op jit(solution)/shard_map/ppermute | solution.py:420
  170.8 1.6 place.3
  (103 shorter events, 32.8 us)
Async XLA Ops:
  0.6 108.8 %copy-start = (f32[8,2048]{1,0:T(8,128)S(1)}, f32[8,2048]{1,0:T(8,128)}, u32[]{:S(2)}) copy-start(f32[8,2048]{1,0:T(8,128)} %param.23) | copy-start | bytes 196612
  8.2 3.5 %collective-permute-start = (bf16[256,1024]{1,0:T(8,128)(2,1)}, bf16[256,1024]{1,0:T(8,128)(2,1)}, u32[]{:S(2)}, u32[]{:S(2)}) collective-permute-start(bf16[256,1024]{1,0:T(8,128)(2,1)} %rank_part.3), channel_id=1, source_target_pairs={{0,16},{16,0},{1,17},{17,1},{2,18},{18,2},{3,19},{19,3},{4,20},{20... | collective-permute-start | bytes 1572872 | tf_op jit(solution)/shard_map/ppermute | solution.py:509
  9.5 29.1 %copy-start.12 = (f32[1024]{0:T(1024)S(1)}, f32[1024]{0:T(1024)}, u32[]{:S(2)}) copy-start(f32[1024]{0:T(1024)} %param.16) | copy-start | bytes 12292
  12.8 6.3 %collective-permute-start.3 = (bf16[64,1024]{1,0:T(8,128)(2,1)S(1)}, bf16[64,1024]{1,0:T(8,128)(2,1)S(1)}, u32[]{:S(2)}, u32[]{:S(2)}) collective-permute-start(bf16[64,1024]{1,0:T(8,128)(2,1)S(1)} %get-tuple-element.23), channel_id=1, source_target_pairs={{0,96},{32,0},{64,32},{96,64},{1,97},{33,1},{65,33},{97,65},{2,98}... | collective-permute-start | bytes 393224 | tf_op jit(solution)/shard_map/ppermute | solution.py:515
  15.7 9.6 %collective-permute-start.2 = (bf16[64,1024]{1,0:T(8,128)(2,1)S(1)}, bf16[64,1024]{1,0:T(8,128)(2,1)S(1)}, u32[]{:S(2)}, u32[]{:S(2)}) collective-permute-start(bf16[64,1024]{1,0:T(8,128)(2,1)S(1)} %get-tuple-element.22), channel_id=1, source_target_pairs={{0,32},{32,64},{64,96},{96,0},{1,33},{33,65},{65,97},{97,1},{2,34}... | collective-permute-start | bytes 393224 | tf_op jit(solution)/shard_map/ppermute | solution.py:514
  15.7 9.6 %collective-permute-start.1 = (bf16[64,1024]{1,0:T(8,128)(2,1)S(1)}, bf16[64,1024]{1,0:T(8,128)(2,1)S(1)}, u32[]{:S(2)}, u32[]{:S(2)}) collective-permute-start(bf16[64,1024]{1,0:T(8,128)(2,1)S(1)} %get-tuple-element.21), channel_id=1, source_target_pairs={{0,64},{32,96},{64,0},{96,32},{1,65},{33,97},{65,1},{97,33},{2,66}... | collective-permute-start | bytes 393224 | tf_op jit(solution)/shard_map/ppermute | solution.py:513
  25.4 8.8 %collective-permute-start.4 = (bf16[64,1024]{1,0:T(8,128)(2,1)S(1)}, bf16[64,1024]{1,0:T(8,128)(2,1)S(1)}, u32[]{:S(2)}, u32[]{:S(2)}) collective-permute-start(bf16[64,1024]{1,0:T(8,128)(2,1)S(1)} %add_convert_fusion.4.refs_0_), channel_id=1, source_target_pairs={{0,32},{32,64},{64,96},{96,0},{1,33},{33,65},{65,97},{97,1},{2,34}... | collective-permute-start | bytes 393224 | tf_op jit(solution)/shard_map/ppermute | solution.py:518
  25.5 8.8 %collective-permute-start.5 = (bf16[64,1024]{1,0:T(8,128)(2,1)S(1)}, bf16[64,1024]{1,0:T(8,128)(2,1)}, u32[]{:S(2)}, u32[]{:S(2)}) collective-permute-start(bf16[64,1024]{1,0:T(8,128)(2,1)S(1)} %add_convert_fusion.4.refs_0_), channel_id=1, source_target_pairs={{0,64},{32,96},{64,0},{96,32},{1,65},{33,97},{65,1},{97,33},{2,66}... | collective-permute-start | bytes 393224 | tf_op jit(solution)/shard_map/ppermute | solution.py:517
  27.4 7.6 %collective-permute-start.6 = (bf16[64,1024]{1,0:T(8,128)(2,1)S(1)}, bf16[64,1024]{1,0:T(8,128)(2,1)}, u32[]{:S(2)}, u32[]{:S(2)}) collective-permute-start(bf16[64,1024]{1,0:T(8,128)(2,1)S(1)} %add_convert_fusion.4.refs_0_), channel_id=1, source_target_pairs={{0,96},{32,0},{64,32},{96,64},{1,97},{33,1},{65,33},{97,65},{2,98}... | collective-permute-start | bytes 393224 | tf_op jit(solution)/shard_map/ppermute | solution.py:519
  28.8 9.7 %collective-permute-start.7 = (bf16[64,1024]{1,0:T(8,128)(2,1)S(1)}, bf16[64,1024]{1,0:T(8,128)(2,1)}, u32[]{:S(2)}, u32[]{:S(2)}) collective-permute-start(bf16[64,1024]{1,0:T(8,128)(2,1)S(1)} %add_convert_fusion.4.refs_0_), channel_id=1, source_target_pairs={{0,16},{16,0},{1,17},{17,1},{2,18},{18,2},{3,19},{19,3},{4,20},{20... | collective-permute-start | bytes 393224 | tf_op jit(solution)/shard_map/ppermute | solution.py:509
  34.3 4.2 %collective-permute-start.8 = (bf16[64,1024]{1,0:T(8,128)(2,1)S(1)}, bf16[64,1024]{1,0:T(8,128)(2,1)}, u32[]{:S(2)}, u32[]{:S(2)}) collective-permute-start(bf16[64,1024]{1,0:T(8,128)(2,1)S(1)} %collective-permute-done.4.refs_1_), channel_id=1, source_target_pairs={{0,16},{16,0},{1,17},{17,1},{2,18},{18,2},{3,19},{19,3},{4,20},{20... | collective-permute-start | bytes 393224 | tf_op jit(solution)/shard_map/ppermute | solution.py:509
  34.3 4.2 %collective-permute-start.9 = (bf16[64,1024]{1,0:T(8,128)(2,1)}, bf16[64,1024]{1,0:T(8,128)(2,1)}, u32[]{:S(2)}, u32[]{:S(2)}) collective-permute-start(bf16[64,1024]{1,0:T(8,128)(2,1)} %collective-permute-done.5.refs_2_), channel_id=1, source_target_pairs={{0,16},{16,0},{1,17},{17,1},{2,18},{18,2},{3,19},{19,3},{4,20},{20... | collective-permute-start | bytes 393224 | tf_op jit(solution)/shard_map/ppermute | solution.py:509
  35.0 3.5 %collective-permute-start.10 = (bf16[64,1024]{1,0:T(8,128)(2,1)}, bf16[64,1024]{1,0:T(8,128)(2,1)}, u32[]{:S(2)}, u32[]{:S(2)}) collective-permute-start(bf16[64,1024]{1,0:T(8,128)(2,1)} %collective-permute-done.6.refs_3_), channel_id=1, source_target_pairs={{0,16},{16,0},{1,17},{17,1},{2,18},{18,2},{3,19},{19,3},{4,20},{20... | collective-permute-start | bytes 393224 | tf_op jit(solution)/shard_map/ppermute | solution.py:509
  45.9 35.4 %all-to-all-start = ((bf16[16,400,128]{2,1,0:T(8,128)(2,1)}), bf16[16,400,128]{2,1,0:T(8,128)(2,1)S(1)}, u32[]{:S(2)}, u32[]{:S(2)}) async-start(bf16[16,400,128]{2,1,0:T(8,128)(2,1)} %copy-done.7), calls=%async_computation | async-start | bytes 3276800 | tf_op jit(solution)/shard_map/all_to_all | solution.py:589
  87.1 10.7 %collective-permute-start.12 = (bf16[4,4,128,128]{3,2,1,0:T(8,128)(2,1)S(1)}, bf16[4,4,128,128]{3,2,1,0:T(8,128)(2,1)S(1)}, u32[]{:S(2)}, u32[]{:S(2)}) collective-permute-start(bf16[4,4,128,128]{3,2,1,0:T(8,128)(2,1)S(1)} %get-tuple-element.27), channel_id=1, source_target_pairs={{0,4},{1,5},{2,6},{3,7},{4,8},{5,9},{6,10},{7,11},{8,12},{9,13},{1... | collective-permute-start | bytes 1572872 | tf_op jit(solution)/shard_map/ppermute | solution.py:420
  94.5 10.0 %collective-permute-start.20 = (bf16[4,4,128,128]{3,2,1,0:T(8,128)(2,1)}, bf16[4,4,128,128]{3,2,1,0:T(8,128)(2,1)}, u32[]{:S(2)}, u32[]{:S(2)}) collective-permute-start(bf16[4,4,128,128]{3,2,1,0:T(8,128)(2,1)} %get-tuple-element.32), channel_id=1, source_target_pairs={{0,12},{1,13},{2,14},{3,15},{4,0},{5,1},{6,2},{7,3},{8,4},{9,5},{1... | collective-permute-start | bytes 1572872 | tf_op jit(solution)/shard_map/ppermute | solution.py:420
  97.5 14.7 %collective-permute-start.11 = (bf16[4,4,128,128]{3,2,1,0:T(8,128)(2,1)S(1)}, bf16[4,4,128,128]{3,2,1,0:T(8,128)(2,1)}, u32[]{:S(2)}, u32[]{:S(2)}) collective-permute-start(bf16[4,4,128,128]{3,2,1,0:T(8,128)(2,1)S(1)} %get-tuple-element.25), channel_id=1, source_target_pairs={{0,12},{1,13},{2,14},{3,15},{4,0},{5,1},{6,2},{7,3},{8,4},{9,5},{1... | collective-permute-start | bytes 1572872 | tf_op jit(solution)/shard_map/ppermute | solution.py:420
  98.8 13.3 %collective-permute-start.13 = (bf16[4,4,128,128]{3,2,1,0:T(8,128)(2,1)}, bf16[4,4,128,128]{3,2,1,0:T(8,128)(2,1)}, u32[]{:S(2)}, u32[]{:S(2)}) collective-permute-start(bf16[4,4,128,128]{3,2,1,0:T(8,128)(2,1)} %add_convert_fusion.3), channel_id=1, source_target_pairs={{0,4},{1,5},{2,6},{3,7},{4,8},{5,9},{6,10},{7,11},{8,12},{9,13},{1... | collective-permute-start | bytes 1572872 | tf_op jit(solution)/shard_map/ppermute | solution.py:420
  100.4 14.6 %collective-permute-start.19 = (bf16[4,4,128,128]{3,2,1,0:T(8,128)(2,1)}, bf16[4,4,128,128]{3,2,1,0:T(8,128)(2,1)S(1)}, u32[]{:S(2)}, u32[]{:S(2)}) collective-permute-start(bf16[4,4,128,128]{3,2,1,0:T(8,128)(2,1)} %get-tuple-element.30), channel_id=1, source_target_pairs={{0,4},{1,5},{2,6},{3,7},{4,8},{5,9},{6,10},{7,11},{8,12},{9,13},{1... | collective-permute-start | bytes 1572872 | tf_op jit(solution)/shard_map/ppermute | solution.py:420
  105.7 10.8 %collective-permute-start.21 = (bf16[4,4,128,128]{3,2,1,0:T(8,128)(2,1)S(1)}, bf16[4,4,128,128]{3,2,1,0:T(8,128)(2,1)S(1)}, u32[]{:S(2)}, u32[]{:S(2)}) collective-permute-start(bf16[4,4,128,128]{3,2,1,0:T(8,128)(2,1)S(1)} %add_convert_fusion.1), channel_id=1, source_target_pairs={{0,12},{1,13},{2,14},{3,15},{4,0},{5,1},{6,2},{7,3},{8,4},{9,5},{1... | collective-permute-start | bytes 1572872 | tf_op jit(solution)/shard_map/ppermute | solution.py:420
  113.5 10.6 %collective-permute-start.15 = (bf16[4,4,128,128]{3,2,1,0:T(8,128)(2,1)S(1)}, bf16[4,4,128,128]{3,2,1,0:T(8,128)(2,1)}, u32[]{:S(2)}, u32[]{:S(2)}) collective-permute-start(bf16[4,4,128,128]{3,2,1,0:T(8,128)(2,1)S(1)} %add_convert_fusion.2.own_ref), channel_id=1, source_target_pairs={{0,1},{1,2},{2,3},{3,0},{4,5},{5,6},{6,7},{7,4},{8,9},{9,10},{10,1... | collective-permute-start | bytes 1572872 | tf_op jit(solution)/shard_map/ppermute | solution.py:420
  116.7 9.2 %collective-permute-start.22 = (bf16[4,4,128,128]{3,2,1,0:T(8,128)(2,1)S(1)}, bf16[4,4,128,128]{3,2,1,0:T(8,128)(2,1)S(1)}, u32[]{:S(2)}, u32[]{:S(2)}) collective-permute-start(bf16[4,4,128,128]{3,2,1,0:T(8,128)(2,1)S(1)} %add_convert_fusion.own_ref), channel_id=1, source_target_pairs={{0,3},{1,0},{2,1},{3,2},{4,7},{5,4},{6,5},{7,6},{8,11},{9,8},{10,9... | collective-permute-start | bytes 1572872 | tf_op jit(solution)/shard_map/ppermute | solution.py:420
  118.4 15.0 %collective-permute-start.14 = (bf16[4,4,128,128]{3,2,1,0:T(8,128)(2,1)S(1)}, bf16[4,4,128,128]{3,2,1,0:T(8,128)(2,1)S(1)}, u32[]{:S(2)}, u32[]{:S(2)}) collective-permute-start(bf16[4,4,128,128]{3,2,1,0:T(8,128)(2,1)S(1)} %add_convert_fusion.2.own_ref), channel_id=1, source_target_pairs={{0,3},{1,0},{2,1},{3,2},{4,7},{5,4},{6,5},{7,6},{8,11},{9,8},{10,9... | collective-permute-start | bytes 1572872 | tf_op jit(solution)/shard_map/ppermute | solution.py:420
  118.6 20.8 %collective-permute-start.24 = (bf16[4,4,128,128]{3,2,1,0:T(8,128)(2,1)S(1)}, bf16[4,4,128,128]{3,2,1,0:T(8,128)(2,1)S(1)}, u32[]{:S(2)}, u32[]{:S(2)}) collective-permute-start(bf16[4,4,128,128]{3,2,1,0:T(8,128)(2,1)S(1)} %add_convert_fusion.own_ref), channel_id=1, source_target_pairs={{0,1},{1,2},{2,3},{3,0},{4,5},{5,6},{6,7},{7,4},{8,9},{9,10},{10,1... | collective-permute-start | bytes 1572872 | tf_op jit(solution)/shard_map/ppermute | solution.py:420
  124.1 11.1 %collective-permute-start.16 = (bf16[4,4,128,128]{3,2,1,0:T(8,128)(2,1)}, bf16[4,4,128,128]{3,2,1,0:T(8,128)(2,1)S(1)}, u32[]{:S(2)}, u32[]{:S(2)}) collective-permute-start(bf16[4,4,128,128]{3,2,1,0:T(8,128)(2,1)} %collective-permute-done.15.prev_ref), channel_id=1, source_target_pairs={{0,1},{1,2},{2,3},{3,0},{4,5},{5,6},{6,7},{7,4},{8,9},{9,10},{10,1... | collective-permute-start | bytes 1572872 | tf_op jit(solution)/shard_map/ppermute | solution.py:420
  126.0 13.4 %collective-permute-start.23 = (bf16[4,4,128,128]{3,2,1,0:T(8,128)(2,1)S(1)}, bf16[4,4,128,128]{3,2,1,0:T(8,128)(2,1)S(1)}, u32[]{:S(2)}, u32[]{:S(2)}) collective-permute-start(bf16[4,4,128,128]{3,2,1,0:T(8,128)(2,1)S(1)} %collective-permute-done.22.next_ref), channel_id=1, source_target_pairs={{0,3},{1,0},{2,1},{3,2},{4,7},{5,4},{6,5},{7,6},{8,11},{9,8},{10,9... | collective-permute-start | bytes 1572872 | tf_op jit(solution)/shard_map/ppermute | solution.py:420
  139.1 16.1 %collective-permute-start.17 = (bf16[4,4,128,128]{3,2,1,0:T(8,128)(2,1)S(1)}, bf16[4,4,128,128]{3,2,1,0:T(8,128)(2,1)S(1)}, u32[]{:S(2)}, u32[]{:S(2)}) collective-permute-start(bf16[4,4,128,128]{3,2,1,0:T(8,128)(2,1)S(1)} %get-tuple-element.28.refs_0_), channel_id=1, source_target_pairs={{0,4},{1,5},{2,6},{3,7},{4,8},{5,9},{6,10},{7,11},{8,12},{9,13},{1... | collective-permute-start | bytes 1572872 | tf_op jit(solution)/shard_map/ppermute | solution.py:420
  142.2 13.0 %collective-permute-start.25 = (bf16[4,4,128,128]{3,2,1,0:T(8,128)(2,1)S(1)}, bf16[4,4,128,128]{3,2,1,0:T(8,128)(2,1)S(1)}, u32[]{:S(2)}, u32[]{:S(2)}) collective-permute-start(bf16[4,4,128,128]{3,2,1,0:T(8,128)(2,1)S(1)} %get-tuple-element.33.refs_1_), channel_id=1, source_target_pairs={{0,12},{1,13},{2,14},{3,15},{4,0},{5,1},{6,2},{7,3},{8,4},{9,5},{1... | collective-permute-start | bytes 1572872 | tf_op jit(solution)/shard_map/ppermute | solution.py:420
  153.2 9.2 %collective-permute-start.27 = (bf16[4,4,128,128]{3,2,1,0:T(8,128)(2,1)S(1)}, bf16[4,4,128,128]{3,2,1,0:T(8,128)(2,1)S(1)}, u32[]{:S(2)}, u32[]{:S(2)}) collective-permute-start(bf16[4,4,128,128]{3,2,1,0:T(8,128)(2,1)S(1)} %get-tuple-element.28.refs_0_), channel_id=1, source_target_pairs={{0,12},{1,13},{2,14},{3,15},{4,0},{5,1},{6,2},{7,3},{8,4},{9,5},{1... | collective-permute-start | bytes 1572872 | tf_op jit(solution)/shard_map/ppermute | solution.py:420
  154.7 10.4 %collective-permute-start.28 = (bf16[4,4,128,128]{3,2,1,0:T(8,128)(2,1)S(1)}, bf16[4,4,128,128]{3,2,1,0:T(8,128)(2,1)S(1)}, u32[]{:S(2)}, u32[]{:S(2)}) collective-permute-start(bf16[4,4,128,128]{3,2,1,0:T(8,128)(2,1)S(1)} %get-tuple-element.33.refs_1_), channel_id=1, source_target_pairs={{0,4},{1,5},{2,6},{3,7},{4,8},{5,9},{6,10},{7,11},{8,12},{9,13},{1... | collective-permute-start | bytes 1572872 | tf_op jit(solution)/shard_map/ppermute | solution.py:420
  155.2 15.6 %collective-permute-start.18 = (bf16[4,4,128,128]{3,2,1,0:T(8,128)(2,1)S(1)}, bf16[4,4,128,128]{3,2,1,0:T(8,128)(2,1)S(1)}, u32[]{:S(2)}, u32[]{:S(2)}) collective-permute-start(bf16[4,4,128,128]{3,2,1,0:T(8,128)(2,1)S(1)} %collective-permute-done.17.refs_4_), channel_id=1, source_target_pairs={{0,4},{1,5},{2,6},{3,7},{4,8},{5,9},{6,10},{7,11},{8,12},{9,13},{1... | collective-permute-start | bytes 1572872 | tf_op jit(solution)/shard_map/ppermute | solution.py:420
  155.2 15.5 %collective-permute-start.26 = (bf16[4,4,128,128]{3,2,1,0:T(8,128)(2,1)S(1)}, bf16[4,4,128,128]{3,2,1,0:T(8,128)(2,1)S(1)}, u32[]{:S(2)}, u32[]{:S(2)}) collective-permute-start(bf16[4,4,128,128]{3,2,1,0:T(8,128)(2,1)S(1)} %collective-permute-done.25.refs_3_), channel_id=1, source_target_pairs={{0,12},{1,13},{2,14},{3,15},{4,0},{5,1},{6,2},{7,3},{8,4},{9,5},{1... | collective-permute-start | bytes 1572872 | tf_op jit(solution)/shard_map/ppermute | solution.py:420
  (16 other events, 57.1 us)

commit v4 on v3

--- a/solution.py
+++ b/solution.py
@@ -60,6 +60,9 @@
 def rank_part(half, feat, cot, ci, co, dtype):
     size = feat.shape[0] // NC
     depth, rank = ci.shape
+    feat, cot, ci, co = (
+        pltpu.with_memory_space_constraint(a, pltpu.HBM) for a in (feat, cot, ci, co)
+    )
     tile = depth // 4
     return pl.pallas_call(
         rank_kernel,
@@ -79,7 +82,7 @@
         cost_estimate=pl.CostEstimate(
             flops=4 * size * depth * rank, bytes_accessed=4 << 20, transcendentals=0
         ),
-        compiler_params=pltpu.CompilerParams(vmem_limit_bytes=16 << 20),
+        compiler_params=pltpu.CompilerParams(vmem_limit_bytes=12 << 20),
         name="rank_part",
     )(half, feat, cot, ci, co)
 
@@ -170,7 +173,7 @@
     out = (dests, tables * cap + KEY_ROWS, width)
     return pl.pallas_call(
         pooled_kernel,
-        out_shape=jax.ShapeDtypeStruct(out, bf),
+        out_shape=pltpu.HBM(out, bf),
         grid_spec=pltpu.PrefetchScalarGridSpec(
             num_scalar_prefetch=1,
             grid=(tables // pair,),
@@ -189,7 +192,7 @@
                 pltpu.VMEM((samples, pieces[0].shape[1]), bf),
             ],
         ),
-        compiler_params=pltpu.CompilerParams(vmem_limit_bytes=16 << 20),
+        compiler_params=pltpu.CompilerParams(vmem_limit_bytes=12 << 20),
         name="pooled_dispatch",
     )(where, *pieces, cot, co, ci, bias, pos, digits)
 
@@ -356,13 +359,24 @@
         cost_estimate=pl.CostEstimate(
             flops=count * 4 * slots * rem_rows * width, bytes_accessed=1 << 22, transcendentals=0
         ),
-        compiler_params=pltpu.CompilerParams(vmem_limit_bytes=16 << 20),
+        compiler_params=pltpu.CompilerParams(vmem_limit_bytes=12 << 20),
         name="rem_parts",
     )(where, got, slab)
 
 
-def quot_kernel(first, tables, g_ref, pack_ref, rtab_ref, *refs):
-    quot_ref, key_ref, row_ref = refs[-3:]
+def lane_mean(x):
+    width = x.shape[1]
+    square = x * x
+    high = square.astype(bf)
+    low = (square - high.astype(f32)).astype(bf)
+    ones = jnp.full((width, width), 1.0 / width, bf)
+    return jnp.dot(high, ones, preferred_element_type=f32) + jnp.dot(
+        low, ones, preferred_element_type=f32
+    )
+
+
+def quot_kernel(first, tables, g_ref, pack_ref, rtab_ref, slab_ref, acc_ref, *refs):
+    quot_ref, out_ref, key_ref, row_ref, sum_ref, col_ref, done_ref = refs[-7:]
     sources, cap, width = g_ref.shape
     slots = sources * cap
     quot_rows = quot_ref.shape[1]
@@ -374,45 +388,77 @@
         keys = unpack_keys(pack_ref[...])
         key_ref[...] = keys
         row_ref[...] = key_rows(keys, tables)
+        col_ref[...] = acc_ref[...].T
 
     g = g_ref[...].reshape(slots, width).astype(f32)
     q, m = key_lanes(key_ref[...], t)
     val = g * pick(m, rtab_ref[0])
 
     def store(at, sums):
-        quot_ref[0, at : at + sums.shape[0]] = sums
+        sum_ref[at : at + sums.shape[0]] = sums
 
     spread(row_ref[pl.ds(t, 1), :], q, quot_rows, val, store)
-
-
-def quot_grads(first, count, got, rtab, quot_rows, old=None):
+    size = quot_rows // 4
+    for at in range(0, quot_rows, size):
+        part = slice(at, at + size)
+        grad = sum_ref[part]
+        col = lax.broadcasted_iota(jnp.int32, (size, tables), 1)
+        old = jnp.sum(jnp.where(col == t, col_ref[part], 0.0), axis=1, keepdims=True)
+        acc = old + lane_mean(grad)
+        new = slab_ref[0, part].astype(f32) - step_rate * grad * lax.rsqrt(acc + epsilon)
+        quot_ref[0, part] = new.astype(bf)
+        lane = lax.broadcasted_iota(jnp.int32, (size, width), 1)
+        done_ref[part] = jnp.where(lane == step, acc, done_ref[part])
+
+    @pl.when(step == pl.num_programs(0) - 1)
+    def _():
+        out_ref[...] = done_ref[...].T[: out_ref.shape[0]]
+
+
+def quot_update(first, count, got, rtab, slab, accum, old=None):
     sources, _, width = got.shape
     tables, rem_rows, _ = rtab.shape
+    quot_rows = slab.shape[1]
     slots = sources * CAP
     rtab = pltpu.with_memory_space_constraint(rtab, pltpu.HBM)
-    ins, extra, alias = [got, got, rtab], [], {}
+    slab = pltpu.with_memory_space_constraint(slab, pltpu.HBM)
+    ins, extra, alias = [got, got, rtab, slab, accum], [], {}
     if old is not None:
         ins.append(old)
         extra = [pl.BlockSpec(memory_space=pltpu.HBM)]
-        alias = {3: 0}
+        alias = {len(ins) - 1: 0}
     return pl.pallas_call(
         functools.partial(quot_kernel, first, tables),
-        out_shape=jax.ShapeDtypeStruct((tables, quot_rows, width), f32),
+        out_shape=(
+            pltpu.HBM(slab.shape, bf),
+            jax.ShapeDtypeStruct((tables, quot_rows), f32),
+        ),
         grid=(count,),
         in_specs=[
             pl.BlockSpec((sources, CAP, width), lambda t: (0, first + t, 0)),
             pl.BlockSpec((sources, KEY_ROWS, width), lambda t: (0, tables * CAP // KEY_ROWS, 0)),
             pl.BlockSpec((1, rem_rows, width), lambda t: (first + t, 0, 0)),
+            pl.BlockSpec((1, quot_rows, width), lambda t: (first + t, 0, 0)),
+            pl.BlockSpec((tables, quot_rows), lambda t: (0, 0)),
         ]
         + extra,
-        out_specs=pl.BlockSpec((1, quot_rows, width), lambda t: (first + t, 0, 0)),
-        scratch_shapes=[pltpu.VMEM((slots, width), bf), pltpu.VMEM((width, slots), f32)],
+        out_specs=(
+            pl.BlockSpec((1, quot_rows, width), lambda t: (first + t, 0, 0)),
+            pl.BlockSpec((tables, quot_rows), lambda t: (0, 0)),
+        ),
+        scratch_shapes=[
+            pltpu.VMEM((slots, width), bf),
+            pltpu.VMEM((width, slots), f32),
+            pltpu.VMEM((quot_rows, width), f32),
+            pltpu.VMEM((quot_rows, tables), f32),
+            pltpu.VMEM((quot_rows, width), f32),
+        ],
         input_output_aliases=alias,
         cost_estimate=pl.CostEstimate(
             flops=count * 4 * slots * rem_rows * width, bytes_accessed=1 << 23, transcendentals=0
         ),
-        compiler_params=pltpu.CompilerParams(vmem_limit_bytes=16 << 20),
-        name="quot_grads",
+        compiler_params=pltpu.CompilerParams(vmem_limit_bytes=14 << 20),
+        name="quot_update",
     )(*ins)
 
 
@@ -503,7 +549,7 @@
     )(where, *ins)
 
 
-def rank_sums(feat, cot, cross_in, cross_out):
+def rank_sums(feat, cot, cross_in, cross_out, ready):
     ci = lax.axis_index("c").astype(jnp.int32).reshape(1)
     xi = lax.axis_index("x").astype(jnp.int32).reshape(1)
     swap = lambda a: lax.ppermute(a, "c", [(0, 1), (1, 0)])
@@ -514,29 +560,29 @@
     nxt = lax.ppermute(parts[1], "x", ring(NX, 1))
     prev = lax.ppermute(parts[3], "x", ring(NX, 3))
     mine = add(parts[0], far, nxt, prev).astype(bf)
+    mine, ready = lax.optimization_barrier((mine, ready))
     far = lax.ppermute(mine, "x", ring(NX, 2))
     prev = lax.ppermute(mine, "x", ring(NX, 1))
     nxt = lax.ppermute(mine, "x", ring(NX, 3))
     own = (mine, prev, far, nxt)
-    return own + tuple(swap(a) for a in own)
+    return own + tuple(swap(a) for a in own), ready
 
 
 def update_kernel(own_ref, next_ref, far_ref, prev_ref, acc_ref, tab_ref, new_ref, out_ref):
-    tables, subs, _, width = own_ref.shape
+    tables, subs, rows, width = own_ref.shape
     accs = acc_ref[...].T
-    lane = lax.broadcasted_iota(jnp.int32, accs.shape, 1)
-    done = jnp.zeros_like(accs)
+    lane = lax.broadcasted_iota(jnp.int32, (rows, width), 1)
+    done = jnp.zeros((rows, width), f32)
     for i in range(tables * subs):
         t, s = divmod(i, subs)
         grad = (own_ref[t, s].astype(f32) + far_ref[t, s].astype(f32)) + (
             next_ref[t, s].astype(f32) + prev_ref[t, s].astype(f32)
         )
-        mean = jnp.sum(grad * grad, axis=1, keepdims=True) * (1.0 / width)
-        acc = accs[:, i : i + 1] + mean
+        acc = accs[:, i : i + 1] + lane_mean(grad)
         new = tab_ref[t, s].astype(f32) - step_rate * grad * lax.rsqrt(acc + epsilon)
         new_ref[t, s] = new.astype(bf)
         done = jnp.where(lane == i, acc, done)
-    out_ref[...] = done.T
+    out_ref[...] = done.T[: tables * subs]
 
 
 def update(ring_parts, acc, tab):
@@ -580,11 +626,14 @@
     position = target * cap + slot_index
     digits = digit_lanes(quot_row, rem_row, width)
 
-    pieces = rank_sums(features, cotangent, cross_in, cross_out)
+    position = position.reshape(tables, 1, samples)
+    pieces, (position, digits) = rank_sums(
+        features, cotangent, cross_in, cross_out, (position, digits)
+    )
     xi = lax.axis_index("x")
     send = pooled_dispatch(
         jnp.stack([ci, xi]).astype(jnp.int32), pieces, cotangent, cross_out, cross_in,
-        bias.reshape(1, -1), position.reshape(tables, 1, samples), digits, rows, cap, width,
+        bias.reshape(1, -1), position, digits, rows, cap, width,
     )
     got = lax.all_to_all(send, ("z", "y"), split_axis=0, concat_axis=0, tiled=True)
     along_z = ci == 0
@@ -620,14 +669,9 @@
     rem_out = place((2,), where, [(all_low[2], all_high[2])], shape, rem_out)
     rem_out = rem_out.reshape(tables, rem_rows, width)
 
-    quot_rows = quot_slab.shape[1]
-    quot_grad = quot_grads(0, half, got, rem_table, quot_rows)
-    quot_grad = quot_grads(half, half, got, rem_table, quot_rows, quot_grad)
-    quot_acc_out = quot_accum + jnp.mean(quot_grad * quot_grad, axis=-1)
-    quot_out = (
-        quot_slab.astype(f32)
-        - step_rate * quot_grad * lax.rsqrt(quot_acc_out + epsilon)[..., None]
-    ).astype(bf)
+    quot_out, acc_low = quot_update(0, half, got, rem_table, quot_slab, quot_accum)
+    quot_out, acc_high = quot_update(half, half, got, rem_table, quot_slab, quot_accum, quot_out)
+    quot_acc_out = jnp.concatenate([acc_low[:half], acc_high[:half]], axis=0)
     return (quot_out, quot_acc_out, rem_out, rem_acc_out)
 
 

time: 173 us -> 164 us (0.948)
  local copies, waits for them, and re-layouts: 10.8 us -> 2.32 us
  other arithmetic: 12.6 us -> 6.17 us
  Pallas kernels: 46.8 us -> 52.7 us
  starting transfers between devices: 39.4 us -> 36.6 us
  waiting for transfers between devices: 61.4 us -> 63.3 us
    unnamed x37 -> x19, local copies, waits for them, and re-layouts: 7.36 us -> 0.06 us
    ppermute x18, waiting for transfers between devices: 21.1 us -> 27.1 us  [turn(): return lax.ppermute(a, CZY, turn_pairs(s, flip))]
    ppermute x1, waiting for transfers between devices: 6.22 us -> 0.87 us  [rank_sums(): nxt = lax.ppermute(parts[1], 'x', ring(NX, 1))]
    ppermute x1, waiting for transfers between devices: 0.21 us -> 4.31 us  [rank_sums(): nxt = lax.ppermute(mine, 'x', ring(NX, 3))]
    ppermute x1, waiting for transfers between devices: 5.39 us -> 1.4 us  [rank_sums(): prev = lax.ppermute(mine, 'x', ring(NX, 1))]
    pallas_call x3, Pallas kernels: 17.9 us -> 21.8 us  [the longest x2 15.7 us: quot_update(): pl.pallas_call(functools.partial(quot_kernel, first, tables), out_shape=(...]
    ppermute x18, starting transfers between devices: 22.3 us -> 18.4 us  [turn(): return lax.ppermute(a, CZY, turn_pairs(s, flip))]
    pallas_call x2, Pallas kernels: 4.38 us -> 8.12 us  [rank_part(): pl.pallas_call(rank_kernel, out_shape=jax.ShapeDtypeStruct((size, 2 * ran...]
  transfers between devices with their start and end apart: 30 -> 30, of which waited for: 14 -> 17; matrix products, arithmetic and copies ran while one was open for 9% -> 5% of each run, Pallas kernels for 17% -> 20%
where the time goes in v4:
time: 164 us; the launch traced here: 162 us
  waiting for transfers between devices  63.3 us (39%)
  Pallas kernels  52.7 us (32%)
  starting transfers between devices  36.6 us (22%)
  other arithmetic  6.17 us (4%)
  local copies, waits for them, and re-layouts  2.32 us (1%)
    ppermute x18, waiting for transfers between devices, turn(): return lax.ppermute(a, CZY, turn_pairs(s, flip))  27.1 us
    all_to_all x1, waiting for transfers between devices, device_step(): lax.all_to_all(send, ('z', 'y'), split_axis=0, concat_axis=0, tiled=True)  25.9 us
    ppermute x18, starting transfers between devices, turn(): return lax.ppermute(a, CZY, turn_pairs(s, flip))  18.4 us
    pallas_call x2, Pallas kernels, quot_update(): pl.pallas_call(functools.partial(quot_kernel, first, tables), out_shape=(...  15.7 us
    pallas_call x2, Pallas kernels, rem_parts(): pl.pallas_call(functools.partial(rem_kernel, first, tables), out_shape=(p...  11.6 us
    pallas_call x2, Pallas kernels, rank_part(): pl.pallas_call(rank_kernel, out_shape=jax.ShapeDtypeStruct((size, 2 * ran...  8.12 us
    all_to_all x1, starting transfers between devices, device_step(): lax.all_to_all(send, ('z', 'y'), split_axis=0, concat_axis=0, tiled=True)  8.05 us
    pallas_call x1, Pallas kernels, pooled_dispatch(): pl.pallas_call(pooled_kernel, out_shape=pltpu.HBM(out, bf), grid_spec=plt...  6.15 us
  transfers between devices with their start and end apart: 30, of which 17 were waited for; matrix products, arithmetic and copies ran while one was open for 5% of the time, Pallas kernels for 20%

profile of v4, /device:TPU:0, one launch (start us, length us, event | category | flops | bytes accessed | tf_op | source)
XLA Modules:
  0.0 162.5 jit_solution(15380450951915584804)
XLA Ops:
  0.7 4.4 %rank_part.3 = bf16[256,1024]{1,0:T(8,128)(2,1)} custom-call(s32[1]{0:T(128)S(6)} %sub.19.half_ref, bf16[512,1024]{1,0:T(8,128)(2,1)} %feat_ref.3, bf16[512,1024]{1,0:T(8,128)(2,1)} %refs_8_.1, bf16[1024,512]{1,0:T(8,128)(2,1)} %refs_10_.1, bf16[1024,512]{1,0:T(8,128)(2,1)} %refs_9_.1), custom_call_target="tpu_custom_call" | custom-call | flops 536870912 | bytes 4194304 | tf_op jit(solution)/shard_map/rank_part/pallas_call | solution.py:67
  5.4 3.7 %rank_part.2.keep_ref = f32[256,1024]{1,0:T(8,128)S(1)} custom-call(s32[1]{0:T(128)} %bitcast.half_ref, bf16[512,1024]{1,0:T(8,128)(2,1)} %feat_ref.3, bf16[512,1024]{1,0:T(8,128)(2,1)} %refs_8_.1, bf16[1024,512]{1,0:T(8,128)(2,1)} %refs_10_.1, bf16[1024,512]{1,0:T(8,128)(2,1)} %refs_9_.1), custom_call_target="tpu_custom_call" | custom-call | flops 536870912 | bytes 4194304 | tf_op jit(solution)/shard_map/rank_part/pallas_call | solution.py:67
  9.3 1.9 %mix.1 = (bf16[64,1024]{1,0:T(8,128)(2,1)S(1)}, bf16[64,1024]{1,0:T(8,128)(2,1)}, bf16[64,1024]{1,0:T(8,128)(2,1)}, bf16[64,1024]{1,0:T(8,128)(2,1)S(1)}) custom-call(s32[1]{0:T(128)} %bitcast.1.x_ref, f32[256,1024]{1,0:T(8,128)S(1)} %rank_part.2.keep_ref, bf16[256,1024]{1,0:T(8,128)(2,1)} %collective-permute-done.got_ref), custom_call_target="tpu_custom_call" | custom-call | tf_op jit(solution)/shard_map/mix/pallas_call | solution.py:100
  11.2 3.1 %collective-permute-start.1 = (bf16[64,1024]{1,0:T(8,128)(2,1)}, bf16[64,1024]{1,0:T(8,128)(2,1)}, u32[]{:S(2)}, u32[]{:S(2)}) collective-permute-start(bf16[64,1024]{1,0:T(8,128)(2,1)} %get-tuple-element.28), channel_id=1, source_target_pairs={{0,64},{32,96},{64,0},{96,32},{1,65},{33,97},{65,1},{97,33},{2,66}... | collective-permute-start | bytes 393224 | tf_op jit(solution)/shard_map/ppermute | solution.py:559
  15.0 2.6 %collective-permute-start.3 = (bf16[64,1024]{1,0:T(8,128)(2,1)S(1)}, bf16[64,1024]{1,0:T(8,128)(2,1)}, u32[]{:S(2)}, u32[]{:S(2)}) collective-permute-start(bf16[64,1024]{1,0:T(8,128)(2,1)S(1)} %get-tuple-element.30), channel_id=1, source_target_pairs={{0,96},{32,0},{64,32},{96,64},{1,97},{33,1},{65,33},{97,65},{2,98}... | collective-permute-start | bytes 393224 | tf_op jit(solution)/shard_map/ppermute | solution.py:561
  23.1 2.8 %collective-permute-start.6 = (bf16[64,1024]{1,0:T(8,128)(2,1)S(1)}, bf16[64,1024]{1,0:T(8,128)(2,1)S(1)}, u32[]{:S(2)}, u32[]{:S(2)}) collective-permute-start(bf16[64,1024]{1,0:T(8,128)(2,1)S(1)} %add_convert_fusion.4.refs_0_), channel_id=1, source_target_pairs={{0,96},{32,0},{64,32},{96,64},{1,97},{33,1},{65,33},{97,65},{2,98}... | collective-permute-start | bytes 393224 | tf_op jit(solution)/shard_map/ppermute | solution.py:566
  26.8 4.3 %collective-permute-done.6.refs_3_ = bf16[64,1024]{1,0:T(8,128)(2,1)S(1)} collective-permute-done((bf16[64,1024]{1,0:T(8,128)(2,1)S(1)}, bf16[64,1024]{1,0:T(8,128)(2,1)S(1)}, u32[]{:S(2)}, u32[]{:S(2)}) %collective-permute-start.6) | collective-permute-done | bytes 131104 | tf_op jit(solution)/shard_map/ppermute | solution.py:566
  31.1 2.3 %collective-permute-done.5.refs_2_ = bf16[64,1024]{1,0:T(8,128)(2,1)S(1)} collective-permute-done((bf16[64,1024]{1,0:T(8,128)(2,1)S(1)}, bf16[64,1024]{1,0:T(8,128)(2,1)S(1)}, u32[]{:S(2)}, u32[]{:S(2)}) %collective-permute-start.5) | collective-permute-done | bytes 131104 | tf_op jit(solution)/shard_map/ppermute | solution.py:564
  36.2 6.2 %pooled_dispatch.1 = bf16[16,400,128]{2,1,0:T(8,128)(2,1)} custom-call(s32[2]{0:T(128)S(1)} %pad_add_fusion.at_ref, bf16[64,1024]{1,0:T(8,128)(2,1)S(1)} %add_convert_fusion.4.refs_0_, bf16[64,1024]{1,0:T(8,128)(2,1)S(1)} %collective-permute-done.4.refs_1_, bf16[64,1024]{1,0:T(8,128)(2,1)S(1)} %collective-permute-done.5.refs_2_, ...), custom_call_target="tpu_custom_call" | custom-call | tf_op jit(solution)/shard_map/pooled_dispatch/pallas_call | solution.py:174
  42.3 8.0 %all-to-all-start = ((bf16[16,400,128]{2,1,0:T(8,128)(2,1)}), bf16[16,400,128]{2,1,0:T(8,128)(2,1)S(1)}, u32[]{:S(2)}, u32[]{:S(2)}) async-start(bf16[16,400,128]{2,1,0:T(8,128)(2,1)} %pooled_dispatch.1), calls=%async_computation | async-start | bytes 3276800 | tf_op jit(solution)/shard_map/all_to_all | solution.py:638
  50.5 25.9 %all-to-all-done.g_ref.pack_ref.got_ref = bf16[16,400,128]{2,1,0:T(8,128)(2,1)S(1)} async-done(((bf16[16,400,128]{2,1,0:T(8,128)(2,1)}), bf16[16,400,128]{2,1,0:T(8,128)(2,1)S(1)}, u32[]{:S(2)}, u32[]{:S(2)}) %all-to-all-start) | async-done | bytes 1638432 | tf_op jit(solution)/shard_map/all_to_all | solution.py:638
  76.4 5.8 %rem_parts.3 = (bf16[4,4,128,128]{3,2,1,0:T(8,128)(2,1)S(1)}, bf16[4,4,128,128]{3,2,1,0:T(8,128)(2,1)S(1)}, bf16[4,4,128,128]{3,2,1,0:T(8,128)(2,1)S(1)}, bf16[4,4,128,128]{3,2,1,0:T(8,128)(2,1)S(1)}) custom-call(s32[3]{0:T(128)S(1)} %pad_add_fusion.1.where_ref, bf16[16,400,128]{2,1,0:T(8,128)(2,1)S(1)} %all-to-all-done.g_ref.pack_ref.got_ref, ...), custom_call_target="tpu_custom_call" | custom-call | flops 3221225472 | bytes 4194304 | tf_op jit(solution)/shard_map/rem_parts/pallas_call | solution.py:339
  82.2 1.8 %collective-permute-start.20 = (bf16[4,4,128,128]{3,2,1,0:T(8,128)(2,1)S(1)}, bf16[4,4,128,128]{3,2,1,0:T(8,128)(2,1)S(1)}, u32[]{:S(2)}, u32[]{:S(2)}) collective-permute-start(bf16[4,4,128,128]{3,2,1,0:T(8,128)(2,1)S(1)} %get-tuple-element.46), channel_id=1, source_target_pairs={{0,12},{1,13},{2,14},{3,15},{4,0},{5,1},{6,2},{7,3},{8,4},{9,5},{1... | collective-permute-start | bytes 1572872 | tf_op jit(solution)/shard_map/ppermute | solution.py:466
  84.1 5.8 %rem_parts.2 = (bf16[4,4,128,128]{3,2,1,0:T(8,128)(2,1)S(1)}, bf16[4,4,128,128]{3,2,1,0:T(8,128)(2,1)S(1)}, bf16[4,4,128,128]{3,2,1,0:T(8,128)(2,1)S(1)}, bf16[4,4,128,128]{3,2,1,0:T(8,128)(2,1)S(1)}) custom-call(s32[3]{0:T(128)S(1)} %pad_add_fusion.1.where_ref, bf16[16,400,128]{2,1,0:T(8,128)(2,1)S(1)} %all-to-all-done.g_ref.pack_ref.got_ref, ...), custom_call_target="tpu_custom_call" | custom-call | flops 3221225472 | bytes 4194304 | tf_op jit(solution)/shard_map/rem_parts/pallas_call | solution.py:339
  91.8 2.9 %collective-permute-start.21 = (bf16[4,4,128,128]{3,2,1,0:T(8,128)(2,1)S(1)}, bf16[4,4,128,128]{3,2,1,0:T(8,128)(2,1)S(1)}, u32[]{:S(2)}, u32[]{:S(2)}) collective-permute-start(bf16[4,4,128,128]{3,2,1,0:T(8,128)(2,1)S(1)} %add_convert_fusion.1), channel_id=1, source_target_pairs={{0,12},{1,13},{2,14},{3,15},{4,0},{5,1},{6,2},{7,3},{8,4},{9,5},{1... | collective-permute-start | bytes 1572872 | tf_op jit(solution)/shard_map/ppermute | solution.py:466
  95.4 4.9 %collective-permute-done.12 = bf16[4,4,128,128]{3,2,1,0:T(8,128)(2,1)S(1)} collective-permute-done((bf16[4,4,128,128]{3,2,1,0:T(8,128)(2,1)S(1)}, bf16[4,4,128,128]{3,2,1,0:T(8,128)(2,1)S(1)}, u32[]{:S(2)}, u32[]{:S(2)}) %collective-permute-start.12) | collective-permute-done | bytes 524320 | tf_op jit(solution)/shard_map/ppermute | solution.py:466
  100.5 5.4 %collective-permute-done.19 = bf16[4,4,128,128]{3,2,1,0:T(8,128)(2,1)S(1)} collective-permute-done((bf16[4,4,128,128]{3,2,1,0:T(8,128)(2,1)S(1)}, bf16[4,4,128,128]{3,2,1,0:T(8,128)(2,1)S(1)}, u32[]{:S(2)}, u32[]{:S(2)}) %collective-permute-start.19) | collective-permute-done | bytes 524320 | tf_op jit(solution)/shard_map/ppermute | solution.py:466
  106.2 3.2 %collective-permute-done.11 = bf16[4,4,128,128]{3,2,1,0:T(8,128)(2,1)S(1)} collective-permute-done((bf16[4,4,128,128]{3,2,1,0:T(8,128)(2,1)S(1)}, bf16[4,4,128,128]{3,2,1,0:T(8,128)(2,1)S(1)}, u32[]{:S(2)}, u32[]{:S(2)}) %collective-permute-start.11) | collective-permute-done | bytes 524320 | tf_op jit(solution)/shard_map/ppermute | solution.py:466
  109.4 2.1 %collective-permute-done.13 = bf16[4,4,128,128]{3,2,1,0:T(8,128)(2,1)S(1)} collective-permute-done((bf16[4,4,128,128]{3,2,1,0:T(8,128)(2,1)S(1)}, bf16[4,4,128,128]{3,2,1,0:T(8,128)(2,1)S(1)}, u32[]{:S(2)}, u32[]{:S(2)}) %collective-permute-start.13) | collective-permute-done | bytes 524320 | tf_op jit(solution)/shard_map/ppermute | solution.py:466
  112.4 2.9 %collective-permute-start.14 = (bf16[4,4,128,128]{3,2,1,0:T(8,128)(2,1)S(1)}, bf16[4,4,128,128]{3,2,1,0:T(8,128)(2,1)S(1)}, u32[]{:S(2)}, u32[]{:S(2)}) collective-permute-start(bf16[4,4,128,128]{3,2,1,0:T(8,128)(2,1)S(1)} %add_convert_fusion.2.own_ref), channel_id=1, source_target_pairs={{0,3},{1,0},{2,1},{3,2},{4,7},{5,4},{6,5},{7,6},{8,11},{9,8},{10,9... | collective-permute-start | bytes 1572872 | tf_op jit(solution)/shard_map/ppermute | solution.py:466
  115.5 1.7 %collective-permute-start.23 = (bf16[4,4,128,128]{3,2,1,0:T(8,128)(2,1)}, bf16[4,4,128,128]{3,2,1,0:T(8,128)(2,1)S(1)}, u32[]{:S(2)}, u32[]{:S(2)}) collective-permute-start(bf16[4,4,128,128]{3,2,1,0:T(8,128)(2,1)} %collective-permute-done.22.next_ref), channel_id=1, source_target_pairs={{0,3},{1,0},{2,1},{3,2},{4,7},{5,4},{6,5},{7,6},{8,11},{9,8},{10,9... | collective-permute-start | bytes 1572872 | tf_op jit(solution)/shard_map/ppermute | solution.py:466
  117.2 5.0 %collective-permute-done.15.prev_ref = bf16[4,4,128,128]{3,2,1,0:T(8,128)(2,1)S(1)} collective-permute-done((bf16[4,4,128,128]{3,2,1,0:T(8,128)(2,1)S(1)}, bf16[4,4,128,128]{3,2,1,0:T(8,128)(2,1)S(1)}, u32[]{:S(2)}, u32[]{:S(2)}) %collective-permute-start.15) | collective-permute-done | bytes 524320 | tf_op jit(solution)/shard_map/ppermute | solution.py:466
  122.2 1.7 %bitcast_select_fusion = bf16[8,4,128,128]{3,2,1,0:T(8,128)(2,1)S(1)} fusion(bf16[8,4,4,128,128]{4,3,2,1,0:T(8,128)(2,1)} %bitcast.56, s32[]{:T(128)S(6)} %select_n.69, s32[]{:T(128)S(6)} %select_n.68, pred[]{:T(512)S(6)} %eq.25), kind=kLoop, calls=%fused_computation.3 | loop fusion | flops 524288 | bytes 3145737 | tf_op jit(solution)/shard_map/jit(_where)/select_n | solution.py:654
  124.0 3.9 %collective-permute-done.24.prev_ref = bf16[4,4,128,128]{3,2,1,0:T(8,128)(2,1)S(1)} collective-permute-done((bf16[4,4,128,128]{3,2,1,0:T(8,128)(2,1)S(1)}, bf16[4,4,128,128]{3,2,1,0:T(8,128)(2,1)S(1)}, u32[]{:S(2)}, u32[]{:S(2)}) %collective-permute-start.24) | collective-permute-done | bytes 524320 | tf_op jit(solution)/shard_map/ppermute | solution.py:466
  128.0 2.6 %update.3 = (bf16[4,4,128,128]{3,2,1,0:T(8,128)(2,1)}, f32[16,128]{1,0:T(8,128)S(1)}) custom-call(bf16[4,4,128,128]{3,2,1,0:T(8,128)(2,1)S(1)} %add_convert_fusion.own_ref, bf16[4,4,128,128]{3,2,1,0:T(8,128)(2,1)} %collective-permute-done.22.next_ref, bf16[4,4,128,128]{3,2,1,0:T(8,128)(2,1)S(1)} %collective-permute-done.23.far_ref, ...), custom_call_target="tpu_custom_call" | custom-call | flops 2097152 | bytes 4194304 | tf_op jit(solution)/shard_map/update/pallas_call | solution.py:591
  133.5 1.6 update.2
  135.1 7.8 %quot_update.2 = (bf16[8,1024,128]{2,1,0:T(8,128)(2,1)}, f32[8,1024]{1,0:T(8,128)S(1)}) custom-call(bf16[16,400,128]{2,1,0:T(8,128)(2,1)S(1)} %all-to-all-done.g_ref.pack_ref.got_ref, bf16[16,400,128]{2,1,0:T(8,128)(2,1)S(1)} %all-to-all-done.g_ref.pack_ref.got_ref, bf16[8,2048,128]{2,1,0:T(8,128)(2,1)} %rtab_ref.3, bf16[8,1024,128]{2,1,0:T(8,128)(2,1)} %slab_ref.7, ...), custom_call_target="tpu_custom_call" | custom-call | flops 3221225472 | bytes 8388608 | tf_op jit(solution)/shard_map/quot_update/pallas_call | solution.py:430
  143.9 2.3 %collective-permute-start.27 = (bf16[4,4,128,128]{3,2,1,0:T(8,128)(2,1)}, bf16[4,4,128,128]{3,2,1,0:T(8,128)(2,1)S(1)}, u32[]{:S(2)}, u32[]{:S(2)}) collective-permute-start(bf16[4,4,128,128]{3,2,1,0:T(8,128)(2,1)} %get-tuple-element.42.refs_0_), channel_id=1, source_target_pairs={{0,12},{1,13},{2,14},{3,15},{4,0},{5,1},{6,2},{7,3},{8,4},{9,5},{1... | collective-permute-start | bytes 1572872 | tf_op jit(solution)/shard_map/ppermute | solution.py:466
  146.2 2.0 %collective-permute-start.26 = (bf16[4,4,128,128]{3,2,1,0:T(8,128)(2,1)}, bf16[4,4,128,128]{3,2,1,0:T(8,128)(2,1)S(1)}, u32[]{:S(2)}, u32[]{:S(2)}) collective-permute-start(bf16[4,4,128,128]{3,2,1,0:T(8,128)(2,1)} %collective-permute-done.25.refs_3_), channel_id=1, source_target_pairs={{0,12},{1,13},{2,14},{3,15},{4,0},{5,1},{6,2},{7,3},{8,4},{9,5},{1... | collective-permute-start | bytes 1572872 | tf_op jit(solution)/shard_map/ppermute | solution.py:466
  148.2 7.8 %quot_update.3 = (bf16[8,1024,128]{2,1,0:T(8,128)(2,1)}, f32[8,1024]{1,0:T(8,128)S(1)}) custom-call(bf16[16,400,128]{2,1,0:T(8,128)(2,1)S(1)} %all-to-all-done.g_ref.pack_ref.got_ref, bf16[16,400,128]{2,1,0:T(8,128)(2,1)S(1)} %all-to-all-done.g_ref.pack_ref.got_ref, bf16[8,2048,128]{2,1,0:T(8,128)(2,1)} %rtab_ref.3, ...), custom_call_target="tpu_custom_call", output_to_operand_aliasing={{0}: (5, {})} | custom-call | flops 3221225472 | bytes 8388608 | tf_op jit(solution)/shard_map/quot_update/pallas_call | solution.py:430
  157.3 3.4 %place.2.refs_2_ = bf16[8,4,4,128,128]{4,3,2,1,0:T(8,128)(2,1)} custom-call(s32[3]{0:T(128)S(1)} %pad_add_fusion.1.where_ref, bf16[4,4,128,128]{3,2,1,0:T(8,128)(2,1)} %get-tuple-element.42.refs_0_, bf16[4,4,128,128]{3,2,1,0:T(8,128)(2,1)} %get-tuple-element.47.refs_1_, bf16[4,4,128,128]{3,2,1,0:T(8,128)(2,1)S(1)} %collective-permute-done.27.refs_2_, ...), custom_call_target="tpu_custom_call" | custom-call | bytes 6291456 | tf_op jit(solution)/shard_map/place/pallas_call | solution.py:531
  160.7 1.6 %place.3 = bf16[8,4,4,128,128]{4,3,2,1,0:T(8,128)(2,1)} custom-call(s32[3]{0:T(128)S(1)} %pad_add_fusion.1.where_ref, bf16[4,4,128,128]{3,2,1,0:T(8,128)(2,1)S(1)} %collective-permute-done.18.refs_0_, bf16[4,4,128,128]{3,2,1,0:T(8,128)(2,1)S(1)} %collective-permute-done.26.refs_1_, ...), custom_call_target="tpu_custom_call", output_to_operand_aliasing={{}: (3, {})} | custom-call | bytes 2097152 | tf_op jit(solution)/shard_map/place/pallas_call | solution.py:531
  (85 shorter events, 19.7 us)
Async XLA Ops:
  0.6 111.2 %copy-start = (f32[8,2048]{1,0:T(8,128)S(1)}, f32[8,2048]{1,0:T(8,128)}, u32[]{:S(2)}) copy-start(f32[8,2048]{1,0:T(8,128)} %param.23) | copy-start | bytes 196612
  5.1 4.2 %collective-permute-start = (bf16[256,1024]{1,0:T(8,128)(2,1)}, bf16[256,1024]{1,0:T(8,128)(2,1)}, u32[]{:S(2)}, u32[]{:S(2)}) collective-permute-start(bf16[256,1024]{1,0:T(8,128)(2,1)} %rank_part.3), channel_id=1, source_target_pairs={{0,16},{16,0},{1,17},{17,1},{2,18},{18,2},{3,19},{19,3},{4,20},{20... | collective-permute-start | bytes 1572872 | tf_op jit(solution)/shard_map/ppermute | solution.py:555
  5.4 30.7 %copy-start.3 = (bf16[1024,512]{1,0:T(8,128)(2,1)S(1)}, bf16[1024,512]{1,0:T(8,128)(2,1)}, u32[]{:S(2)}) copy-start(bf16[1024,512]{1,0:T(8,128)(2,1)} %refs_9_.1) | copy-start | bytes 3145732
  11.2 9.8 %collective-permute-start.1 = (bf16[64,1024]{1,0:T(8,128)(2,1)}, bf16[64,1024]{1,0:T(8,128)(2,1)}, u32[]{:S(2)}, u32[]{:S(2)}) collective-permute-start(bf16[64,1024]{1,0:T(8,128)(2,1)} %get-tuple-element.28), channel_id=1, source_target_pairs={{0,64},{32,96},{64,0},{96,32},{1,65},{33,97},{65,1},{97,33},{2,66}... | collective-permute-start | bytes 393224 | tf_op jit(solution)/shard_map/ppermute | solution.py:559
  14.4 7.5 %collective-permute-start.2 = (bf16[64,1024]{1,0:T(8,128)(2,1)}, bf16[64,1024]{1,0:T(8,128)(2,1)}, u32[]{:S(2)}, u32[]{:S(2)}) collective-permute-start(bf16[64,1024]{1,0:T(8,128)(2,1)} %get-tuple-element.29), channel_id=1, source_target_pairs={{0,32},{32,64},{64,96},{96,0},{1,33},{33,65},{65,97},{97,1},{2,34}... | collective-permute-start | bytes 393224 | tf_op jit(solution)/shard_map/ppermute | solution.py:560
  15.0 7.0 %collective-permute-start.3 = (bf16[64,1024]{1,0:T(8,128)(2,1)S(1)}, bf16[64,1024]{1,0:T(8,128)(2,1)}, u32[]{:S(2)}, u32[]{:S(2)}) collective-permute-start(bf16[64,1024]{1,0:T(8,128)(2,1)S(1)} %get-tuple-element.30), channel_id=1, source_target_pairs={{0,96},{32,0},{64,32},{96,64},{1,97},{33,1},{65,33},{97,65},{2,98}... | collective-permute-start | bytes 393224 | tf_op jit(solution)/shard_map/ppermute | solution.py:561
  23.1 8.1 %collective-permute-start.6 = (bf16[64,1024]{1,0:T(8,128)(2,1)S(1)}, bf16[64,1024]{1,0:T(8,128)(2,1)S(1)}, u32[]{:S(2)}, u32[]{:S(2)}) collective-permute-start(bf16[64,1024]{1,0:T(8,128)(2,1)S(1)} %add_convert_fusion.4.refs_0_), channel_id=1, source_target_pairs={{0,96},{32,0},{64,32},{96,64},{1,97},{33,1},{65,33},{97,65},{2,98}... | collective-permute-start | bytes 393224 | tf_op jit(solution)/shard_map/ppermute | solution.py:566
  25.9 7.5 %collective-permute-start.5 = (bf16[64,1024]{1,0:T(8,128)(2,1)S(1)}, bf16[64,1024]{1,0:T(8,128)(2,1)S(1)}, u32[]{:S(2)}, u32[]{:S(2)}) collective-permute-start(bf16[64,1024]{1,0:T(8,128)(2,1)S(1)} %add_convert_fusion.4.refs_0_), channel_id=1, source_target_pairs={{0,64},{32,96},{64,0},{96,32},{1,65},{33,97},{65,1},{97,33},{2,66}... | collective-permute-start | bytes 393224 | tf_op jit(solution)/shard_map/ppermute | solution.py:564
  26.7 8.1 %collective-permute-start.4 = (bf16[64,1024]{1,0:T(8,128)(2,1)S(1)}, bf16[64,1024]{1,0:T(8,128)(2,1)S(1)}, u32[]{:S(2)}, u32[]{:S(2)}) collective-permute-start(bf16[64,1024]{1,0:T(8,128)(2,1)S(1)} %add_convert_fusion.4.refs_0_), channel_id=1, source_target_pairs={{0,32},{32,64},{64,96},{96,0},{1,33},{33,65},{65,97},{97,1},{2,34}... | collective-permute-start | bytes 393224 | tf_op jit(solution)/shard_map/ppermute | solution.py:565
  26.8 8.1 %collective-permute-start.7 = (bf16[64,1024]{1,0:T(8,128)(2,1)S(1)}, bf16[64,1024]{1,0:T(8,128)(2,1)S(1)}, u32[]{:S(2)}, u32[]{:S(2)}) collective-permute-start(bf16[64,1024]{1,0:T(8,128)(2,1)S(1)} %add_convert_fusion.4.refs_0_), channel_id=1, source_target_pairs={{0,16},{16,0},{1,17},{17,1},{2,18},{18,2},{3,19},{19,3},{4,20},{20... | collective-permute-start | bytes 393224 | tf_op jit(solution)/shard_map/ppermute | solution.py:555
  31.1 3.8 %collective-permute-start.10 = (bf16[64,1024]{1,0:T(8,128)(2,1)S(1)}, bf16[64,1024]{1,0:T(8,128)(2,1)S(1)}, u32[]{:S(2)}, u32[]{:S(2)}) collective-permute-start(bf16[64,1024]{1,0:T(8,128)(2,1)S(1)} %collective-permute-done.6.refs_3_), channel_id=1, source_target_pairs={{0,16},{16,0},{1,17},{17,1},{2,18},{18,2},{3,19},{19,3},{4,20},{20... | collective-permute-start | bytes 393224 | tf_op jit(solution)/shard_map/ppermute | solution.py:555
  33.4 1.5 collective-permute-start.9
  34.8 1.3 collective-permute-start.8
  42.3 34.1 %all-to-all-start = ((bf16[16,400,128]{2,1,0:T(8,128)(2,1)}), bf16[16,400,128]{2,1,0:T(8,128)(2,1)S(1)}, u32[]{:S(2)}, u32[]{:S(2)}) async-start(bf16[16,400,128]{2,1,0:T(8,128)(2,1)} %pooled_dispatch.1), calls=%async_computation | async-start | bytes 3276800 | tf_op jit(solution)/shard_map/all_to_all | solution.py:638
  82.2 9.4 %collective-permute-start.20 = (bf16[4,4,128,128]{3,2,1,0:T(8,128)(2,1)S(1)}, bf16[4,4,128,128]{3,2,1,0:T(8,128)(2,1)S(1)}, u32[]{:S(2)}, u32[]{:S(2)}) collective-permute-start(bf16[4,4,128,128]{3,2,1,0:T(8,128)(2,1)S(1)} %get-tuple-element.46), channel_id=1, source_target_pairs={{0,12},{1,13},{2,14},{3,15},{4,0},{5,1},{6,2},{7,3},{8,4},{9,5},{1... | collective-permute-start | bytes 1572872 | tf_op jit(solution)/shard_map/ppermute | solution.py:466
  89.9 10.5 %collective-permute-start.12 = (bf16[4,4,128,128]{3,2,1,0:T(8,128)(2,1)S(1)}, bf16[4,4,128,128]{3,2,1,0:T(8,128)(2,1)S(1)}, u32[]{:S(2)}, u32[]{:S(2)}) collective-permute-start(bf16[4,4,128,128]{3,2,1,0:T(8,128)(2,1)S(1)} %get-tuple-element.41), channel_id=1, source_target_pairs={{0,4},{1,5},{2,6},{3,7},{4,8},{5,9},{6,10},{7,11},{8,12},{9,13},{1... | collective-permute-start | bytes 1572872 | tf_op jit(solution)/shard_map/ppermute | solution.py:466
  90.4 15.6 %collective-permute-start.19 = (bf16[4,4,128,128]{3,2,1,0:T(8,128)(2,1)S(1)}, bf16[4,4,128,128]{3,2,1,0:T(8,128)(2,1)S(1)}, u32[]{:S(2)}, u32[]{:S(2)}) collective-permute-start(bf16[4,4,128,128]{3,2,1,0:T(8,128)(2,1)S(1)} %get-tuple-element.44), channel_id=1, source_target_pairs={{0,4},{1,5},{2,6},{3,7},{4,8},{5,9},{6,10},{7,11},{8,12},{9,13},{1... | collective-permute-start | bytes 1572872 | tf_op jit(solution)/shard_map/ppermute | solution.py:466
  91.8 14.1 %collective-permute-start.21 = (bf16[4,4,128,128]{3,2,1,0:T(8,128)(2,1)S(1)}, bf16[4,4,128,128]{3,2,1,0:T(8,128)(2,1)S(1)}, u32[]{:S(2)}, u32[]{:S(2)}) collective-permute-start(bf16[4,4,128,128]{3,2,1,0:T(8,128)(2,1)S(1)} %add_convert_fusion.1), channel_id=1, source_target_pairs={{0,12},{1,13},{2,14},{3,15},{4,0},{5,1},{6,2},{7,3},{8,4},{9,5},{1... | collective-permute-start | bytes 1572872 | tf_op jit(solution)/shard_map/ppermute | solution.py:466
  94.7 14.8 %collective-permute-start.11 = (bf16[4,4,128,128]{3,2,1,0:T(8,128)(2,1)S(1)}, bf16[4,4,128,128]{3,2,1,0:T(8,128)(2,1)S(1)}, u32[]{:S(2)}, u32[]{:S(2)}) collective-permute-start(bf16[4,4,128,128]{3,2,1,0:T(8,128)(2,1)S(1)} %get-tuple-element.39), channel_id=1, source_target_pairs={{0,12},{1,13},{2,14},{3,15},{4,0},{5,1},{6,2},{7,3},{8,4},{9,5},{1... | collective-permute-start | bytes 1572872 | tf_op jit(solution)/shard_map/ppermute | solution.py:466
  100.5 11.1 %collective-permute-start.13 = (bf16[4,4,128,128]{3,2,1,0:T(8,128)(2,1)S(1)}, bf16[4,4,128,128]{3,2,1,0:T(8,128)(2,1)S(1)}, u32[]{:S(2)}, u32[]{:S(2)}) collective-permute-start(bf16[4,4,128,128]{3,2,1,0:T(8,128)(2,1)S(1)} %add_convert_fusion.3), channel_id=1, source_target_pairs={{0,4},{1,5},{2,6},{3,7},{4,8},{5,9},{6,10},{7,11},{8,12},{9,13},{1... | collective-permute-start | bytes 1572872 | tf_op jit(solution)/shard_map/ppermute | solution.py:466
  106.2 9.4 %collective-permute-start.22 = (bf16[4,4,128,128]{3,2,1,0:T(8,128)(2,1)S(1)}, bf16[4,4,128,128]{3,2,1,0:T(8,128)(2,1)}, u32[]{:S(2)}, u32[]{:S(2)}) collective-permute-start(bf16[4,4,128,128]{3,2,1,0:T(8,128)(2,1)S(1)} %add_convert_fusion.own_ref), channel_id=1, source_target_pairs={{0,3},{1,0},{2,1},{3,2},{4,7},{5,4},{6,5},{7,6},{8,11},{9,8},{10,9... | collective-permute-start | bytes 1572872 | tf_op jit(solution)/shard_map/ppermute | solution.py:466
  111.8 10.5 %collective-permute-start.15 = (bf16[4,4,128,128]{3,2,1,0:T(8,128)(2,1)S(1)}, bf16[4,4,128,128]{3,2,1,0:T(8,128)(2,1)S(1)}, u32[]{:S(2)}, u32[]{:S(2)}) collective-permute-start(bf16[4,4,128,128]{3,2,1,0:T(8,128)(2,1)S(1)} %add_convert_fusion.2.own_ref), channel_id=1, source_target_pairs={{0,1},{1,2},{2,3},{3,0},{4,5},{5,6},{6,7},{7,4},{8,9},{9,10},{10,1... | collective-permute-start | bytes 1572872 | tf_op jit(solution)/shard_map/ppermute | solution.py:466
  111.9 15.9 %collective-permute-start.24 = (bf16[4,4,128,128]{3,2,1,0:T(8,128)(2,1)S(1)}, bf16[4,4,128,128]{3,2,1,0:T(8,128)(2,1)S(1)}, u32[]{:S(2)}, u32[]{:S(2)}) collective-permute-start(bf16[4,4,128,128]{3,2,1,0:T(8,128)(2,1)S(1)} %add_convert_fusion.own_ref), channel_id=1, source_target_pairs={{0,1},{1,2},{2,3},{3,0},{4,5},{5,6},{6,7},{7,4},{8,9},{9,10},{10,1... | collective-permute-start | bytes 1572872 | tf_op jit(solution)/shard_map/ppermute | solution.py:466
  112.4 19.7 %collective-permute-start.14 = (bf16[4,4,128,128]{3,2,1,0:T(8,128)(2,1)S(1)}, bf16[4,4,128,128]{3,2,1,0:T(8,128)(2,1)S(1)}, u32[]{:S(2)}, u32[]{:S(2)}) collective-permute-start(bf16[4,4,128,128]{3,2,1,0:T(8,128)(2,1)S(1)} %add_convert_fusion.2.own_ref), channel_id=1, source_target_pairs={{0,3},{1,0},{2,1},{3,2},{4,7},{5,4},{6,5},{7,6},{8,11},{9,8},{10,9... | collective-permute-start | bytes 1572872 | tf_op jit(solution)/shard_map/ppermute | solution.py:466
  115.5 12.4 %collective-permute-start.23 = (bf16[4,4,128,128]{3,2,1,0:T(8,128)(2,1)}, bf16[4,4,128,128]{3,2,1,0:T(8,128)(2,1)S(1)}, u32[]{:S(2)}, u32[]{:S(2)}) collective-permute-start(bf16[4,4,128,128]{3,2,1,0:T(8,128)(2,1)} %collective-permute-done.22.next_ref), channel_id=1, source_target_pairs={{0,3},{1,0},{2,1},{3,2},{4,7},{5,4},{6,5},{7,6},{8,11},{9,8},{10,9... | collective-permute-start | bytes 1572872 | tf_op jit(solution)/shard_map/ppermute | solution.py:466
  122.2 11.2 %collective-permute-start.16 = (bf16[4,4,128,128]{3,2,1,0:T(8,128)(2,1)S(1)}, bf16[4,4,128,128]{3,2,1,0:T(8,128)(2,1)S(1)}, u32[]{:S(2)}, u32[]{:S(2)}) collective-permute-start(bf16[4,4,128,128]{3,2,1,0:T(8,128)(2,1)S(1)} %collective-permute-done.15.prev_ref), channel_id=1, source_target_pairs={{0,1},{1,2},{2,3},{3,0},{4,5},{5,6},{6,7},{7,4},{8,9},{9,10},{10,1... | collective-permute-start | bytes 1572872 | tf_op jit(solution)/shard_map/ppermute | solution.py:466
  130.6 15.6 %collective-permute-start.25 = (bf16[4,4,128,128]{3,2,1,0:T(8,128)(2,1)}, bf16[4,4,128,128]{3,2,1,0:T(8,128)(2,1)}, u32[]{:S(2)}, u32[]{:S(2)}) collective-permute-start(bf16[4,4,128,128]{3,2,1,0:T(8,128)(2,1)} %get-tuple-element.47.refs_1_), channel_id=1, source_target_pairs={{0,12},{1,13},{2,14},{3,15},{4,0},{5,1},{6,2},{7,3},{8,4},{9,5},{1... | collective-permute-start | bytes 1572872 | tf_op jit(solution)/shard_map/ppermute | solution.py:466
  135.1 13.1 %collective-permute-start.17 = (bf16[4,4,128,128]{3,2,1,0:T(8,128)(2,1)}, bf16[4,4,128,128]{3,2,1,0:T(8,128)(2,1)S(1)}, u32[]{:S(2)}, u32[]{:S(2)}) collective-permute-start(bf16[4,4,128,128]{3,2,1,0:T(8,128)(2,1)} %get-tuple-element.42.refs_0_), channel_id=1, source_target_pairs={{0,4},{1,5},{2,6},{3,7},{4,8},{5,9},{6,10},{7,11},{8,12},{9,13},{1... | collective-permute-start | bytes 1572872 | tf_op jit(solution)/shard_map/ppermute | solution.py:466
  142.9 14.3 %collective-permute-start.28 = (bf16[4,4,128,128]{3,2,1,0:T(8,128)(2,1)}, bf16[4,4,128,128]{3,2,1,0:T(8,128)(2,1)S(1)}, u32[]{:S(2)}, u32[]{:S(2)}) collective-permute-start(bf16[4,4,128,128]{3,2,1,0:T(8,128)(2,1)} %get-tuple-element.47.refs_1_), channel_id=1, source_target_pairs={{0,4},{1,5},{2,6},{3,7},{4,8},{5,9},{6,10},{7,11},{8,12},{9,13},{1... | collective-permute-start | bytes 1572872 | tf_op jit(solution)/shard_map/ppermute | solution.py:466
  143.9 13.4 %collective-permute-start.27 = (bf16[4,4,128,128]{3,2,1,0:T(8,128)(2,1)}, bf16[4,4,128,128]{3,2,1,0:T(8,128)(2,1)S(1)}, u32[]{:S(2)}, u32[]{:S(2)}) collective-permute-start(bf16[4,4,128,128]{3,2,1,0:T(8,128)(2,1)} %get-tuple-element.42.refs_0_), channel_id=1, source_target_pairs={{0,12},{1,13},{2,14},{3,15},{4,0},{5,1},{6,2},{7,3},{8,4},{9,5},{1... | collective-permute-start | bytes 1572872 | tf_op jit(solution)/shard_map/ppermute | solution.py:466
  146.2 14.5 %collective-permute-start.26 = (bf16[4,4,128,128]{3,2,1,0:T(8,128)(2,1)}, bf16[4,4,128,128]{3,2,1,0:T(8,128)(2,1)S(1)}, u32[]{:S(2)}, u32[]{:S(2)}) collective-permute-start(bf16[4,4,128,128]{3,2,1,0:T(8,128)(2,1)} %collective-permute-done.25.refs_3_), channel_id=1, source_target_pairs={{0,12},{1,13},{2,14},{3,15},{4,0},{5,1},{6,2},{7,3},{8,4},{9,5},{1... | collective-permute-start | bytes 1572872 | tf_op jit(solution)/shard_map/ppermute | solution.py:466
  148.2 12.5 %collective-permute-start.18 = (bf16[4,4,128,128]{3,2,1,0:T(8,128)(2,1)S(1)}, bf16[4,4,128,128]{3,2,1,0:T(8,128)(2,1)S(1)}, u32[]{:S(2)}, u32[]{:S(2)}) collective-permute-start(bf16[4,4,128,128]{3,2,1,0:T(8,128)(2,1)S(1)} %collective-permute-done.17.refs_4_), channel_id=1, source_target_pairs={{0,4},{1,5},{2,6},{3,7},{4,8},{5,9},{6,10},{7,11},{8,12},{9,13},{1... | collective-permute-start | bytes 1572872 | tf_op jit(solution)/shard_map/ppermute | solution.py:466
  (7 other events, 100.2 us)

commit v5 on v4

--- a/solution.py
+++ b/solution.py
@@ -39,73 +39,78 @@
     return out
 
 
-def rank_kernel(half_ref, feat_ref, cot_ref, ci_ref, co_ref, out_ref, acc_ref):
-    step = pl.program_id(0)
+def rank_kernel(at_ref, feat_ref, cot_ref, ci_ref, co_ref, *refs):
+    outs, (feat_buf, cot_buf, ci_buf, co_buf, acc_ref, sem) = refs[: 2 * NX], refs[2 * NX :]
+    chunks, samples, tile = feat_buf.shape
     rank = ci_ref.shape[1]
-    feat = feat_ref[...]
-    product = (cot_ref[...].astype(f32) * feat.astype(f32)).astype(bf)
-
-    @pl.when(step == 0)
-    def _():
-        acc_ref[...] = jnp.zeros_like(acc_ref)
-
-    acc_ref[:, :rank] += jnp.dot(feat, ci_ref[...], preferred_element_type=f32)
-    acc_ref[:, rank:] += jnp.dot(product, co_ref[...], preferred_element_type=f32)
-
-    @pl.when(step == pl.num_programs(0) - 1)
-    def _():
-        out_ref[...] = acc_ref[...].astype(out_ref.dtype)
-
-
-def rank_part(half, feat, cot, ci, co, dtype):
-    size = feat.shape[0] // NC
-    depth, rank = ci.shape
-    feat, cot, ci, co = (
-        pltpu.with_memory_space_constraint(a, pltpu.HBM) for a in (feat, cot, ci, co)
-    )
-    tile = depth // 4
+
+    def loads(k):
+        at = pl.ds(k * tile, tile)
+        return (
+            pltpu.make_async_copy(feat_ref.at[:, at], feat_buf.at[k], sem.at[0, k]),
+            pltpu.make_async_copy(ci_ref.at[at], ci_buf.at[k], sem.at[1, k]),
+            pltpu.make_async_copy(cot_ref.at[:, at], cot_buf.at[k], sem.at[2, k]),
+            pltpu.make_async_copy(co_ref.at[at], co_buf.at[k], sem.at[3, k]),
+        )
+
+    copies = [loads(k) for k in range(chunks)]
+    for four in copies:
+        for copy in four:
+            copy.start()
+    for k in range(chunks):
+        for copy in copies[k]:
+            copy.wait()
+        feat = feat_buf[k]
+        product = (cot_buf[k].astype(f32) * feat.astype(f32)).astype(bf)
+        left = jnp.dot(feat, ci_buf[k], preferred_element_type=f32)
+        right = jnp.dot(product, co_buf[k], preferred_element_type=f32)
+        if k:
+            acc_ref[:, :rank] += left
+            acc_ref[:, rank:] += right
+        else:
+            acc_ref[:, :rank] = left
+            acc_ref[:, rank:] = right
+    size = samples // (NC * NX)
+    for i, out in enumerate(outs):
+        c = at_ref[0] if i >= NX else 1 - at_ref[0]
+        row = (c * NX + (at_ref[1] + i % NX) % NX) * size
+        out[...] = acc_ref[pl.ds(pl.multiple_of(row, size), size), :].astype(out.dtype)
+
+
+def rank_parts(where, feat, cot, cross_in, cross_out):
+    samples, depth = feat.shape
+    rank = cross_in.shape[1]
+    chunks = 2
+    tile = depth // chunks
+    ins = [
+        pltpu.with_memory_space_constraint(a, pltpu.HBM)
+        for a in (feat, cot, cross_in, cross_out)
+    ]
+    shape = (samples // (NC * NX), 2 * rank)
     return pl.pallas_call(
         rank_kernel,
-        out_shape=jax.ShapeDtypeStruct((size, 2 * rank), dtype),
+        out_shape=(jax.ShapeDtypeStruct(shape, bf),) * NX
+        + (jax.ShapeDtypeStruct(shape, f32),) * NX,
         grid_spec=pltpu.PrefetchScalarGridSpec(
             num_scalar_prefetch=1,
-            grid=(depth // tile,),
-            in_specs=[
-                pl.BlockSpec((size, tile), lambda k, h: (h[0], k)),
-                pl.BlockSpec((size, tile), lambda k, h: (h[0], k)),
-                pl.BlockSpec((tile, rank), lambda k, h: (k, 0)),
-                pl.BlockSpec((tile, rank), lambda k, h: (k, 0)),
+            grid=(),
+            in_specs=[pl.BlockSpec(memory_space=pltpu.HBM)] * 4,
+            out_specs=[pl.BlockSpec(memory_space=pltpu.VMEM)] * (2 * NX),
+            scratch_shapes=[
+                pltpu.VMEM((chunks, samples, tile), bf),
+                pltpu.VMEM((chunks, samples, tile), bf),
+                pltpu.VMEM((chunks, tile, rank), bf),
+                pltpu.VMEM((chunks, tile, rank), bf),
+                pltpu.VMEM((samples, 2 * rank), f32),
+                pltpu.SemaphoreType.DMA((4, chunks)),
             ],
-            out_specs=pl.BlockSpec((size, 2 * rank), lambda k, h: (0, 0)),
-            scratch_shapes=[pltpu.VMEM((size, 2 * rank), f32)],
         ),
         cost_estimate=pl.CostEstimate(
-            flops=4 * size * depth * rank, bytes_accessed=4 << 20, transcendentals=0
-        ),
-        compiler_params=pltpu.CompilerParams(vmem_limit_bytes=12 << 20),
-        name="rank_part",
-    )(half, feat, cot, ci, co)
-
-
-def mix_kernel(x_ref, keep_ref, got_ref, *outs):
-    size = outs[0].shape[0]
-    for k, out in enumerate(outs):
-        at = pl.ds(pl.multiple_of((x_ref[0] + k) % NX * size, size), size)
-        out[...] = (keep_ref[at, :] + got_ref[at, :].astype(f32)).astype(bf)
-
-
-def mix(xi, keep, got):
-    piece = jax.ShapeDtypeStruct((keep.shape[0] // NX, keep.shape[1]), bf)
-    vmem = pl.BlockSpec(memory_space=pltpu.VMEM)
-    return pl.pallas_call(
-        mix_kernel,
-        out_shape=(piece,) * NX,
-        grid_spec=pltpu.PrefetchScalarGridSpec(
-            num_scalar_prefetch=1, grid=(), in_specs=[vmem] * 2, out_specs=[vmem] * NX
-        ),
-        compiler_params=pltpu.CompilerParams(vmem_limit_bytes=8 << 20),
-        name="mix",
-    )(xi, keep, got)
+            flops=4 * samples * depth * rank, bytes_accessed=8 << 20, transcendentals=0
+        ),
+        compiler_params=pltpu.CompilerParams(vmem_limit_bytes=16 << 20),
+        name="rank_parts",
+    )(where, *ins)
 
 
 def pooled_kernel(at_ref, *refs):
@@ -278,43 +283,40 @@
         store(half + p * size, sums[:, width:])
 
 
-def rem_kernel(
-    first, tables, where_ref, got_ref, slab_ref, r0, r1, r2, r3,
-    g_buf, pack_buf, slab_buf, sum_ref, sem, pack_sem,
-):
-    count, sources, cap, width = g_buf.shape
+def stage_kernel(from_ref, to_ref, sem):
+    copy = pltpu.make_async_copy(from_ref, to_ref, sem)
+    copy.start()
+    copy.wait()
+
+
+def stage(a):
+    return pl.pallas_call(
+        stage_kernel,
+        out_shape=pltpu.VMEM(a.shape, a.dtype),
+        in_specs=[pl.BlockSpec(memory_space=pltpu.HBM)],
+        out_specs=pl.BlockSpec(memory_space=pltpu.VMEM),
+        scratch_shapes=[pltpu.SemaphoreType.DMA],
+        cost_estimate=pl.CostEstimate(flops=0, bytes_accessed=2 * a.size, transcendentals=0),
+        compiler_params=pltpu.CompilerParams(vmem_limit_bytes=8 << 20),
+        name="stage",
+    )(pltpu.with_memory_space_constraint(a, pltpu.HBM))
+
+
+def rem_kernel(first, count, where_ref, got_ref, slab_ref, r0, r1, r2, r3, sum_ref):
+    tables, _, width = slab_ref.shape
+    sources, cap = got_ref.shape[0], CAP
     slots = sources * cap
     rem_rows = sum_ref.shape[0]
-    pack = pltpu.make_async_copy(
-        got_ref.at[:, pl.ds(tables * cap, KEY_ROWS)], pack_buf, pack_sem
-    )
-    pack.start()
-
-    def inputs(k):
-        return (
-            pltpu.make_async_copy(
-                got_ref.at[:, pl.ds((first + k) * cap, cap)], g_buf.at[k], sem.at[0, k]
-            ),
-            pltpu.make_async_copy(slab_ref.at[first + k], slab_buf.at[k], sem.at[1, k]),
-        )
-
-    copies = [inputs(k) for k in range(count)]
-    for pair in copies:
-        for copy in pair:
-            copy.start()
-    pack.wait()
-    keys = unpack_keys(pack_buf[...])
+    keys = unpack_keys(got_ref[:, tables * cap :])
     rows = key_rows(keys, tables)
     sub_rows = r0.shape[2]
     at = where_ref[1]
     along_z = where_ref[0] == 0
     for k in range(count):
-        for copy in copies[k]:
-            copy.wait()
         t = first + k
-        g = g_buf[k].reshape(slots, width).astype(f32)
+        g = got_ref[:, t * cap : (t + 1) * cap].reshape(slots, width).astype(f32)
         q, m = key_lanes(keys, t)
-        val = g * pick(q, slab_buf[k])
+        val = g * pick(q, slab_ref[t])
 
 
         def store(at, sums):
@@ -331,30 +333,18 @@
 
 def rem_parts(first, count, where, got, slab, rem_rows):
     sources, _, width = got.shape
-    tables, quot_rows, _ = slab.shape
     slots = sources * CAP
-    slab = pltpu.with_memory_space_constraint(slab, pltpu.HBM)
     sub = rem_rows // (NZ * NY)
     piece = jax.ShapeDtypeStruct((count, 4, sub, width), bf)
     return pl.pallas_call(
-        functools.partial(rem_kernel, first, tables),
+        functools.partial(rem_kernel, first, count),
         out_shape=(piece,) * 4,
         grid_spec=pltpu.PrefetchScalarGridSpec(
             num_scalar_prefetch=1,
             grid=(),
-            in_specs=[
-                pl.BlockSpec(memory_space=pl.ANY),
-                pl.BlockSpec(memory_space=pltpu.HBM),
-            ],
+            in_specs=[pl.BlockSpec(memory_space=pltpu.VMEM)] * 2,
             out_specs=[pl.BlockSpec(memory_space=pltpu.VMEM)] * 4,
-            scratch_shapes=[
-                pltpu.VMEM((count, sources, CAP, width), bf),
-                pltpu.VMEM((sources, KEY_ROWS, width), bf),
-                pltpu.VMEM((count, quot_rows, width), bf),
-                pltpu.VMEM((rem_rows, width), bf),
-                pltpu.SemaphoreType.DMA((2, count)),
-                pltpu.SemaphoreType.DMA,
-            ],
+            scratch_shapes=[pltpu.VMEM((rem_rows, width), bf)],
         ),
         cost_estimate=pl.CostEstimate(
             flops=count * 4 * slots * rem_rows * width, bytes_accessed=1 << 22, transcendentals=0
@@ -550,12 +540,12 @@
 
 
 def rank_sums(feat, cot, cross_in, cross_out, ready):
-    ci = lax.axis_index("c").astype(jnp.int32).reshape(1)
-    xi = lax.axis_index("x").astype(jnp.int32).reshape(1)
+    where = jnp.stack([lax.axis_index("c"), lax.axis_index("x")]).astype(jnp.int32)
     swap = lambda a: lax.ppermute(a, "c", [(0, 1), (1, 0)])
-    got = swap(rank_part(1 - ci, feat, cot, cross_in, cross_out, bf))
-    keep = rank_part(ci, feat, cot, cross_in, cross_out, f32)
-    parts = mix(xi, keep, got)
+    both = rank_parts(where, feat, cot, cross_in, cross_out)
+    parts = [None] * NX
+    for k in (2, 1, 3, 0):
+        parts[k] = add(both[NX + k], swap(both[k])).astype(bf)
     far = lax.ppermute(parts[2], "x", ring(NX, 2))
     nxt = lax.ppermute(parts[1], "x", ring(NX, 1))
     prev = lax.ppermute(parts[3], "x", ring(NX, 3))
@@ -636,13 +626,14 @@
         bias.reshape(1, -1), position, digits, rows, cap, width,
     )
     got = lax.all_to_all(send, ("z", "y"), split_axis=0, concat_axis=0, tiled=True)
+    slab = stage(quot_slab)
     along_z = ci == 0
     at_one = jnp.where(along_z, zi, yi)
     at_two = jnp.where(along_z, yi, zi)
     where = jnp.stack([ci, at_one, at_one]).astype(jnp.int32)
     half = tables // 2
-    low = rem_parts(0, half, where, got, quot_slab, rem_rows)
-    high = rem_parts(half, half, where, got, quot_slab, rem_rows)
+    low = rem_parts(0, half, where, got, slab, rem_rows)
+    high = rem_parts(half, half, where, got, slab, rem_rows)
 
     one_low, one_high = ring_scatter(low, high, False)
     ring_low, ring_high = ring_gather(one_low.astype(bf), one_high.astype(bf), True)

time: 164 us -> 159 us (0.970)
  Pallas kernels: 52.7 us -> 45.3 us
  starting transfers between devices: 36.6 us -> 39.5 us
  other arithmetic: 6.17 us -> 8.3 us
    pallas_call x5 -> x4, Pallas kernels: 21.6 us -> 17.7 us  [the longest x2 11.9 us: rem_parts(): pl.pallas_call(functools.partial(rem_kernel, first, count), out_shape=(pi...]
    pallas_call x2, Pallas kernels: 4.26 us -> 1.64 us  [update(): pl.pallas_call(update_kernel, out_shape=(jax.ShapeDtypeStruct(tab.shape,...]
    convert_element_type x0 -> x3, other arithmetic: none -> 2.04 us  [rank_sums(): parts[k] = add(both[NX + k], swap(both[k])).astype(bf)]
  transfers between devices with their start and end apart: 30 -> 33, of which waited for: 17 -> 15; matrix products, arithmetic and copies ran while one was open for 5% -> 6% of each run, Pallas kernels for 20% -> 17%
where the time goes in v5:
time: 159 us
  waiting for transfers between devices  61.9 us (39%)
  Pallas kernels  45.3 us (28%)
  starting transfers between devices  39.5 us (25%)
  other arithmetic  8.3 us (5%)
  local copies, waits for them, and re-layouts  2.35 us (1%)
    ppermute x18, waiting for transfers between devices, turn(): return lax.ppermute(a, CZY, turn_pairs(s, flip))  28.6 us
    all_to_all x1, waiting for transfers between devices, device_step(): lax.all_to_all(send, ('z', 'y'), split_axis=0, concat_axis=0, tiled=True)  24.4 us
    ppermute x18, starting transfers between devices, turn(): return lax.ppermute(a, CZY, turn_pairs(s, flip))  19.8 us
    pallas_call x2, Pallas kernels, quot_update(): pl.pallas_call(functools.partial(quot_kernel, first, tables), out_shape=(...  15.7 us
    pallas_call x2, Pallas kernels, rem_parts(): pl.pallas_call(functools.partial(rem_kernel, first, count), out_shape=(pi...  11.9 us
    all_to_all x1, starting transfers between devices, device_step(): lax.all_to_all(send, ('z', 'y'), split_axis=0, concat_axis=0, tiled=True)  8.1 us
    pallas_call x1, Pallas kernels, pooled_dispatch(): pl.pallas_call(pooled_kernel, out_shape=pltpu.HBM(out, bf), grid_spec=plt...  6.13 us
    pallas_call x1, Pallas kernels, rank_parts(): pl.pallas_call(rank_kernel, out_shape=(jax.ShapeDtypeStruct(shape, bf),)...  4.24 us
  transfers between devices with their start and end apart: 33, of which 15 were waited for; matrix products, arithmetic and copies ran while one was open for 6% of the time, Pallas kernels for 17%

profile of v5, /device:TPU:0, one launch (start us, length us, event | category | flops | bytes accessed | tf_op | source)
XLA Modules:
  0.0 158.8 jit_solution(6697585907943076723)
XLA Ops:
  0.7 4.2 %rank_parts.1 = (bf16[64,1024]{1,0:T(8,128)(2,1)}, bf16[64,1024]{1,0:T(8,128)(2,1)S(1)}, bf16[64,1024]{1,0:T(8,128)(2,1)S(1)}, bf16[64,1024]{1,0:T(8,128)(2,1)S(...) custom-call(s32[2]{0:T(128)S(1)} %pad_add_fusion.at_ref, ...), custom_call_target="tpu_custom_call" | custom-call | flops 1073741824 | bytes 8388608 | tf_op jit(solution)/shard_map/rank_parts/pallas_call | solution.py:90
  7.5 3.1 %collective-permute-start.2 = (bf16[64,1024]{1,0:T(8,128)(2,1)}, bf16[64,1024]{1,0:T(8,128)(2,1)}, u32[]{:S(2)}, u32[]{:S(2)}) collective-permute-start(bf16[64,1024]{1,0:T(8,128)(2,1)} %add_convert_fusion.7), channel_id=1, source_target_pairs={{0,64},{32,96},{64,0},{96,32},{1,65},{33,97},{65,1},{97,33},{2,66}... | collective-permute-start | bytes 393224 | tf_op jit(solution)/shard_map/ppermute | solution.py:549
  12.6 2.6 %collective-permute-start.6 = (bf16[64,1024]{1,0:T(8,128)(2,1)}, bf16[64,1024]{1,0:T(8,128)(2,1)}, u32[]{:S(2)}, u32[]{:S(2)}) collective-permute-start(bf16[64,1024]{1,0:T(8,128)(2,1)} %add_convert_fusion.5), channel_id=1, source_target_pairs={{0,96},{32,0},{64,32},{96,64},{1,97},{33,1},{65,33},{97,65},{2,98}... | collective-permute-start | bytes 393224 | tf_op jit(solution)/shard_map/ppermute | solution.py:551
  19.9 3.1 %collective-permute-start.9 = (bf16[64,1024]{1,0:T(8,128)(2,1)S(1)}, bf16[64,1024]{1,0:T(8,128)(2,1)S(1)}, u32[]{:S(2)}, u32[]{:S(2)}) collective-permute-start(bf16[64,1024]{1,0:T(8,128)(2,1)S(1)} %add_convert_fusion.4.refs_0_), channel_id=1, source_target_pairs={{0,96},{32,0},{64,32},{96,64},{1,97},{33,1},{65,33},{97,65},{2,98}... | collective-permute-start | bytes 393224 | tf_op jit(solution)/shard_map/ppermute | solution.py:556
  24.0 3.5 %collective-permute-done.9.refs_3_ = bf16[64,1024]{1,0:T(8,128)(2,1)S(1)} collective-permute-done((bf16[64,1024]{1,0:T(8,128)(2,1)S(1)}, bf16[64,1024]{1,0:T(8,128)(2,1)S(1)}, u32[]{:S(2)}, u32[]{:S(2)}) %collective-permute-start.9) | collective-permute-done | bytes 131104 | tf_op jit(solution)/shard_map/ppermute | solution.py:556
  27.5 2.3 %collective-permute-done.8.refs_2_ = bf16[64,1024]{1,0:T(8,128)(2,1)S(1)} collective-permute-done((bf16[64,1024]{1,0:T(8,128)(2,1)S(1)}, bf16[64,1024]{1,0:T(8,128)(2,1)S(1)}, u32[]{:S(2)}, u32[]{:S(2)}) %collective-permute-start.8) | collective-permute-done | bytes 131104 | tf_op jit(solution)/shard_map/ppermute | solution.py:554
  29.8 1.4 collective-permute-done.7.refs_1_
  31.2 1.3 collective-permute-done.11.refs_5_
  32.6 6.1 %pooled_dispatch.1 = bf16[16,400,128]{2,1,0:T(8,128)(2,1)} custom-call(s32[2]{0:T(128)S(1)} %pad_add_fusion.at_ref, bf16[64,1024]{1,0:T(8,128)(2,1)S(1)} %add_convert_fusion.4.refs_0_, bf16[64,1024]{1,0:T(8,128)(2,1)S(1)} %collective-permute-done.7.refs_1_, bf16[64,1024]{1,0:T(8,128)(2,1)S(1)} %collective-permute-done.8.refs_2_, ...), custom_call_target="tpu_custom_call" | custom-call | tf_op jit(solution)/shard_map/pooled_dispatch/pallas_call | solution.py:179
  38.7 8.1 %all-to-all-start = ((bf16[16,400,128]{2,1,0:T(8,128)(2,1)}), bf16[16,400,128]{2,1,0:T(8,128)(2,1)}, u32[]{:S(2)}, u32[]{:S(2)}) async-start(bf16[16,400,128]{2,1,0:T(8,128)(2,1)} %pooled_dispatch.1), calls=%async_computation | async-start | bytes 3276800 | tf_op jit(solution)/shard_map/all_to_all | solution.py:628
  46.8 1.6 %stage.1.slab_ref = bf16[8,1024,128]{2,1,0:T(8,128)(2,1)S(1)} custom-call(bf16[8,1024,128]{2,1,0:T(8,128)(2,1)} %from_ref.1), custom_call_target="tpu_custom_call" | custom-call | bytes 2097152 | tf_op jit(solution)/shard_map/stage/pallas_call | solution.py:293
  48.5 24.4 %all-to-all-done.g_ref.pack_ref.got_ref = bf16[16,400,128]{2,1,0:T(8,128)(2,1)} async-done(((bf16[16,400,128]{2,1,0:T(8,128)(2,1)}), bf16[16,400,128]{2,1,0:T(8,128)(2,1)}, u32[]{:S(2)}, u32[]{:S(2)}) %all-to-all-start) | async-done | bytes 1638432 | tf_op jit(solution)/shard_map/all_to_all | solution.py:628
  72.9 5.9 %rem_parts.2 = (bf16[4,4,128,128]{3,2,1,0:T(8,128)(2,1)S(1)}, bf16[4,4,128,128]{3,2,1,0:T(8,128)(2,1)S(1)}, bf16[4,4,128,128]{3,2,1,0:T(8,128)(2,1)S(1)}, bf16[4,4,128,128]{3,2,1,0:T(8,128)(2,1)S(1)}) custom-call(s32[3]{0:T(128)S(1)} %pad_add_fusion.1.where_ref, bf16[16,400,128]{2,1,0:T(8,128)(2,1)} %all-to-all-done.g_ref.pack_ref.got_ref, ...), custom_call_target="tpu_custom_call" | custom-call | flops 3221225472 | bytes 4194304 | tf_op jit(solution)/shard_map/rem_parts/pallas_call | solution.py:339
  79.5 5.9 %rem_parts.3 = (bf16[4,4,128,128]{3,2,1,0:T(8,128)(2,1)S(1)}, bf16[4,4,128,128]{3,2,1,0:T(8,128)(2,1)S(1)}, bf16[4,4,128,128]{3,2,1,0:T(8,128)(2,1)S(1)}, bf16[4,4,128,128]{3,2,1,0:T(8,128)(2,1)S(1)}) custom-call(s32[3]{0:T(128)S(1)} %pad_add_fusion.1.where_ref, bf16[16,400,128]{2,1,0:T(8,128)(2,1)} %all-to-all-done.g_ref.pack_ref.got_ref, ...), custom_call_target="tpu_custom_call" | custom-call | flops 3221225472 | bytes 4194304 | tf_op jit(solution)/shard_map/rem_parts/pallas_call | solution.py:339
  85.5 2.9 %collective-permute-start.23 = (bf16[4,4,128,128]{3,2,1,0:T(8,128)(2,1)S(1)}, bf16[4,4,128,128]{3,2,1,0:T(8,128)(2,1)S(1)}, u32[]{:S(2)}, u32[]{:S(2)}) collective-permute-start(bf16[4,4,128,128]{3,2,1,0:T(8,128)(2,1)S(1)} %get-tuple-element.54), channel_id=1, source_target_pairs={{0,12},{1,13},{2,14},{3,15},{4,0},{5,1},{6,2},{7,3},{8,4},{9,5},{1... | collective-permute-start | bytes 1572872 | tf_op jit(solution)/shard_map/ppermute | solution.py:456
  90.7 4.4 %collective-permute-done.23 = bf16[4,4,128,128]{3,2,1,0:T(8,128)(2,1)S(1)} collective-permute-done((bf16[4,4,128,128]{3,2,1,0:T(8,128)(2,1)S(1)}, bf16[4,4,128,128]{3,2,1,0:T(8,128)(2,1)S(1)}, u32[]{:S(2)}, u32[]{:S(2)}) %collective-permute-start.23) | collective-permute-done | bytes 524320 | tf_op jit(solution)/shard_map/ppermute | solution.py:456
  95.3 3.8 %collective-permute-start.24 = (bf16[4,4,128,128]{3,2,1,0:T(8,128)(2,1)S(1)}, bf16[4,4,128,128]{3,2,1,0:T(8,128)(2,1)S(1)}, u32[]{:S(2)}, u32[]{:S(2)}) collective-permute-start(bf16[4,4,128,128]{3,2,1,0:T(8,128)(2,1)S(1)} %add_convert_fusion.1), channel_id=1, source_target_pairs={{0,12},{1,13},{2,14},{3,15},{4,0},{5,1},{6,2},{7,3},{8,4},{9,5},{1... | collective-permute-start | bytes 1572872 | tf_op jit(solution)/shard_map/ppermute | solution.py:456
  99.0 1.7 %collective-permute-done.14 = bf16[4,4,128,128]{3,2,1,0:T(8,128)(2,1)S(1)} collective-permute-done((bf16[4,4,128,128]{3,2,1,0:T(8,128)(2,1)S(1)}, bf16[4,4,128,128]{3,2,1,0:T(8,128)(2,1)S(1)}, u32[]{:S(2)}, u32[]{:S(2)}) %collective-permute-start.14) | collective-permute-done | bytes 524320 | tf_op jit(solution)/shard_map/ppermute | solution.py:456
  101.0 7.8 %collective-permute-done.22 = bf16[4,4,128,128]{3,2,1,0:T(8,128)(2,1)S(1)} collective-permute-done((bf16[4,4,128,128]{3,2,1,0:T(8,128)(2,1)S(1)}, bf16[4,4,128,128]{3,2,1,0:T(8,128)(2,1)S(1)}, u32[]{:S(2)}, u32[]{:S(2)}) %collective-permute-start.22) | collective-permute-done | bytes 524320 | tf_op jit(solution)/shard_map/ppermute | solution.py:456
  109.2 2.0 %collective-permute-start.27 = (bf16[4,4,128,128]{3,2,1,0:T(8,128)(2,1)S(1)}, bf16[4,4,128,128]{3,2,1,0:T(8,128)(2,1)S(1)}, u32[]{:S(2)}, u32[]{:S(2)}) collective-permute-start(bf16[4,4,128,128]{3,2,1,0:T(8,128)(2,1)S(1)} %add_convert_fusion.own_ref), channel_id=1, source_target_pairs={{0,1},{1,2},{2,3},{3,0},{4,5},{5,6},{6,7},{7,4},{8,9},{9,10},{10,1... | collective-permute-start | bytes 1572872 | tf_op jit(solution)/shard_map/ppermute | solution.py:456
  111.4 1.8 %collective-permute-start.19 = (bf16[4,4,128,128]{3,2,1,0:T(8,128)(2,1)S(1)}, bf16[4,4,128,128]{3,2,1,0:T(8,128)(2,1)S(1)}, u32[]{:S(2)}, u32[]{:S(2)}) collective-permute-start(bf16[4,4,128,128]{3,2,1,0:T(8,128)(2,1)S(1)} %collective-permute-done.18.prev_ref), channel_id=1, source_target_pairs={{0,1},{1,2},{2,3},{3,0},{4,5},{5,6},{6,7},{7,4},{8,9},{9,10},{10,1... | collective-permute-start | bytes 1572872 | tf_op jit(solution)/shard_map/ppermute | solution.py:456
  113.2 5.0 %collective-permute-done.25.next_ref = bf16[4,4,128,128]{3,2,1,0:T(8,128)(2,1)S(1)} collective-permute-done((bf16[4,4,128,128]{3,2,1,0:T(8,128)(2,1)S(1)}, bf16[4,4,128,128]{3,2,1,0:T(8,128)(2,1)S(1)}, u32[]{:S(2)}, u32[]{:S(2)}) %collective-permute-start.25) | collective-permute-done | bytes 524320 | tf_op jit(solution)/shard_map/ppermute | solution.py:456
  119.4 1.7 %bitcast_select_fusion = bf16[8,4,128,128]{3,2,1,0:T(8,128)(2,1)S(1)} fusion(bf16[8,4,4,128,128]{4,3,2,1,0:T(8,128)(2,1)} %bitcast.56, s32[]{:T(128)S(6)} %select_n.69, s32[]{:T(128)S(6)} %select_n.68, pred[]{:T(512)S(6)} %eq.25), kind=kLoop, calls=%fused_computation.3 | loop fusion | flops 524288 | bytes 3145737 | tf_op jit(solution)/shard_map/jit(_where)/select_n | solution.py:645
  121.2 2.6 %collective-permute-done.17.next_ref = bf16[4,4,128,128]{3,2,1,0:T(8,128)(2,1)S(1)} collective-permute-done((bf16[4,4,128,128]{3,2,1,0:T(8,128)(2,1)S(1)}, bf16[4,4,128,128]{3,2,1,0:T(8,128)(2,1)S(1)}, u32[]{:S(2)}, u32[]{:S(2)}) %collective-permute-start.17) | collective-permute-done | bytes 524320 | tf_op jit(solution)/shard_map/ppermute | solution.py:456
  123.8 1.4 collective-permute-done.19.far_ref
  126.3 4.8 %collective-permute-done.26.far_ref = bf16[4,4,128,128]{3,2,1,0:T(8,128)(2,1)S(1)} collective-permute-done((bf16[4,4,128,128]{3,2,1,0:T(8,128)(2,1)S(1)}, bf16[4,4,128,128]{3,2,1,0:T(8,128)(2,1)S(1)}, u32[]{:S(2)}, u32[]{:S(2)}) %collective-permute-start.26) | collective-permute-done | bytes 524320 | tf_op jit(solution)/shard_map/ppermute | solution.py:456
  132.3 7.8 %quot_update.2 = (bf16[8,1024,128]{2,1,0:T(8,128)(2,1)}, f32[8,1024]{1,0:T(8,128)S(1)}) custom-call(bf16[16,400,128]{2,1,0:T(8,128)(2,1)} %all-to-all-done.g_ref.pack_ref.got_ref, bf16[16,400,128]{2,1,0:T(8,128)(2,1)} %all-to-all-done.g_ref.pack_ref.got_ref, bf16[8,2048,128]{2,1,0:T(8,128)(2,1)} %rtab_ref.3, bf16[8,1024,128]{2,1,0:T(8,128)(2,1)} %from_ref.1, ...), custom_call_target="tpu_custom_call" | custom-call | flops 3221225472 | bytes 8388608 | tf_op jit(solution)/shard_map/quot_update/pallas_call | solution.py:420
  140.1 2.0 %collective-permute-start.31 = (bf16[4,4,128,128]{3,2,1,0:T(8,128)(2,1)S(1)}, bf16[4,4,128,128]{3,2,1,0:T(8,128)(2,1)S(1)}, u32[]{:S(2)}, u32[]{:S(2)}) collective-permute-start(bf16[4,4,128,128]{3,2,1,0:T(8,128)(2,1)S(1)} %get-tuple-element.55.refs_1_), channel_id=1, source_target_pairs={{0,4},{1,5},{2,6},{3,7},{4,8},{5,9},{6,10},{7,11},{8,12},{9,13},{1... | collective-permute-start | bytes 1572872 | tf_op jit(solution)/shard_map/ppermute | solution.py:456
  142.1 2.0 %collective-permute-start.21 = (bf16[4,4,128,128]{3,2,1,0:T(8,128)(2,1)S(1)}, bf16[4,4,128,128]{3,2,1,0:T(8,128)(2,1)S(1)}, u32[]{:S(2)}, u32[]{:S(2)}) collective-permute-start(bf16[4,4,128,128]{3,2,1,0:T(8,128)(2,1)S(1)} %collective-permute-done.20.refs_4_), channel_id=1, source_target_pairs={{0,4},{1,5},{2,6},{3,7},{4,8},{5,9},{6,10},{7,11},{8,12},{9,13},{1... | collective-permute-start | bytes 1572872 | tf_op jit(solution)/shard_map/ppermute | solution.py:456
  145.4 7.8 %quot_update.3 = (bf16[8,1024,128]{2,1,0:T(8,128)(2,1)}, f32[8,1024]{1,0:T(8,128)S(1)}) custom-call(bf16[16,400,128]{2,1,0:T(8,128)(2,1)} %all-to-all-done.g_ref.pack_ref.got_ref, bf16[16,400,128]{2,1,0:T(8,128)(2,1)} %all-to-all-done.g_ref.pack_ref.got_ref, bf16[8,2048,128]{2,1,0:T(8,128)(2,1)} %rtab_ref.3, ...), custom_call_target="tpu_custom_call", output_to_operand_aliasing={{0}: (5, {})} | custom-call | flops 3221225472 | bytes 8388608 | tf_op jit(solution)/shard_map/quot_update/pallas_call | solution.py:420
  154.4 2.5 %place.2.refs_2_ = bf16[8,4,4,128,128]{4,3,2,1,0:T(8,128)(2,1)} custom-call(s32[3]{0:T(128)S(1)} %pad_add_fusion.1.where_ref, bf16[4,4,128,128]{3,2,1,0:T(8,128)(2,1)S(1)} %get-tuple-element.50.refs_0_, bf16[4,4,128,128]{3,2,1,0:T(8,128)(2,1)S(1)} %get-tuple-element.55.refs_1_, bf16[4,4,128,128]{3,2,1,0:T(8,128)(2,1)S(1)} %collective-permute-done.30.refs_2_, ...), custom_call_target="tpu_custom_call" | custom-call | bytes 6291456 | tf_op jit(solution)/shard_map/place/pallas_call | solution.py:521
  157.0 1.6 %place.3 = bf16[8,4,4,128,128]{4,3,2,1,0:T(8,128)(2,1)} custom-call(s32[3]{0:T(128)S(1)} %pad_add_fusion.1.where_ref, bf16[4,4,128,128]{3,2,1,0:T(8,128)(2,1)S(1)} %collective-permute-done.21.refs_0_, bf16[4,4,128,128]{3,2,1,0:T(8,128)(2,1)S(1)} %collective-permute-done.29.refs_1_, ...), custom_call_target="tpu_custom_call", output_to_operand_aliasing={{}: (3, {})} | custom-call | bytes 2097152 | tf_op jit(solution)/shard_map/place/pallas_call | solution.py:521
  (93 shorter events, 20.1 us)
Async XLA Ops:
  5.0 13.6 %collective-permute-start = (bf16[64,1024]{1,0:T(8,128)(2,1)}, bf16[64,1024]{1,0:T(8,128)(2,1)}, u32[]{:S(2)}, u32[]{:S(2)}) collective-permute-start(bf16[64,1024]{1,0:T(8,128)(2,1)} %get-tuple-element.32), channel_id=1, source_target_pairs={{0,16},{16,0},{1,17},{17,1},{2,18},{18,2},{3,19},{19,3},{4,20},{20... | collective-permute-start | bytes 393224 | tf_op jit(solution)/shard_map/ppermute | solution.py:544
  5.1 1.7 %collective-permute-start.1 = (bf16[64,1024]{1,0:T(8,128)(2,1)S(1)}, bf16[64,1024]{1,0:T(8,128)(2,1)S(1)}, u32[]{:S(2)}, u32[]{:S(2)}) collective-permute-start(bf16[64,1024]{1,0:T(8,128)(2,1)S(1)} %get-tuple-element.34), channel_id=1, source_target_pairs={{0,16},{16,0},{1,17},{17,1},{2,18},{18,2},{3,19},{19,3},{4,20},{20... | collective-permute-start | bytes 393224 | tf_op jit(solution)/shard_map/ppermute | solution.py:544
  5.6 5.1 %collective-permute-start.3 = (bf16[64,1024]{1,0:T(8,128)(2,1)S(1)}, bf16[64,1024]{1,0:T(8,128)(2,1)S(1)}, u32[]{:S(2)}, u32[]{:S(2)}) collective-permute-start(bf16[64,1024]{1,0:T(8,128)(2,1)S(1)} %get-tuple-element.36), channel_id=1, source_target_pairs={{0,16},{16,0},{1,17},{17,1},{2,18},{18,2},{3,19},{19,3},{4,20},{20... | collective-permute-start | bytes 393224 | tf_op jit(solution)/shard_map/ppermute | solution.py:544
  5.7 6.2 %collective-permute-start.5 = (bf16[64,1024]{1,0:T(8,128)(2,1)S(1)}, bf16[64,1024]{1,0:T(8,128)(2,1)S(1)}, u32[]{:S(2)}, u32[]{:S(2)}) collective-permute-start(bf16[64,1024]{1,0:T(8,128)(2,1)S(1)} %get-tuple-element.38), channel_id=1, source_target_pairs={{0,16},{16,0},{1,17},{17,1},{2,18},{18,2},{3,19},{19,3},{4,20},{20... | collective-permute-start | bytes 393224 | tf_op jit(solution)/shard_map/ppermute | solution.py:544
  7.5 11.1 %collective-permute-start.2 = (bf16[64,1024]{1,0:T(8,128)(2,1)}, bf16[64,1024]{1,0:T(8,128)(2,1)}, u32[]{:S(2)}, u32[]{:S(2)}) collective-permute-start(bf16[64,1024]{1,0:T(8,128)(2,1)} %add_convert_fusion.7), channel_id=1, source_target_pairs={{0,64},{32,96},{64,0},{96,32},{1,65},{33,97},{65,1},{97,33},{2,66}... | collective-permute-start | bytes 393224 | tf_op jit(solution)/shard_map/ppermute | solution.py:549
  11.4 7.3 %collective-permute-start.4 = (bf16[64,1024]{1,0:T(8,128)(2,1)}, bf16[64,1024]{1,0:T(8,128)(2,1)}, u32[]{:S(2)}, u32[]{:S(2)}) collective-permute-start(bf16[64,1024]{1,0:T(8,128)(2,1)} %add_convert_fusion.6), channel_id=1, source_target_pairs={{0,32},{32,64},{64,96},{96,0},{1,33},{33,65},{65,97},{97,1},{2,34}... | collective-permute-start | bytes 393224 | tf_op jit(solution)/shard_map/ppermute | solution.py:550
  12.6 6.1 %collective-permute-start.6 = (bf16[64,1024]{1,0:T(8,128)(2,1)}, bf16[64,1024]{1,0:T(8,128)(2,1)}, u32[]{:S(2)}, u32[]{:S(2)}) collective-permute-start(bf16[64,1024]{1,0:T(8,128)(2,1)} %add_convert_fusion.5), channel_id=1, source_target_pairs={{0,96},{32,0},{64,32},{96,64},{1,97},{33,1},{65,33},{97,65},{2,98}... | collective-permute-start | bytes 393224 | tf_op jit(solution)/shard_map/ppermute | solution.py:551
  19.9 7.6 %collective-permute-start.9 = (bf16[64,1024]{1,0:T(8,128)(2,1)S(1)}, bf16[64,1024]{1,0:T(8,128)(2,1)S(1)}, u32[]{:S(2)}, u32[]{:S(2)}) collective-permute-start(bf16[64,1024]{1,0:T(8,128)(2,1)S(1)} %add_convert_fusion.4.refs_0_), channel_id=1, source_target_pairs={{0,96},{32,0},{64,32},{96,64},{1,97},{33,1},{65,33},{97,65},{2,98}... | collective-permute-start | bytes 393224 | tf_op jit(solution)/shard_map/ppermute | solution.py:556
  23.0 6.7 %collective-permute-start.8 = (bf16[64,1024]{1,0:T(8,128)(2,1)S(1)}, bf16[64,1024]{1,0:T(8,128)(2,1)S(1)}, u32[]{:S(2)}, u32[]{:S(2)}) collective-permute-start(bf16[64,1024]{1,0:T(8,128)(2,1)S(1)} %add_convert_fusion.4.refs_0_), channel_id=1, source_target_pairs={{0,64},{32,96},{64,0},{96,32},{1,65},{33,97},{65,1},{97,33},{2,66}... | collective-permute-start | bytes 393224 | tf_op jit(solution)/shard_map/ppermute | solution.py:554
  23.0 8.1 %collective-permute-start.7 = (bf16[64,1024]{1,0:T(8,128)(2,1)S(1)}, bf16[64,1024]{1,0:T(8,128)(2,1)S(1)}, u32[]{:S(2)}, u32[]{:S(2)}) collective-permute-start(bf16[64,1024]{1,0:T(8,128)(2,1)S(1)} %add_convert_fusion.4.refs_0_), channel_id=1, source_target_pairs={{0,32},{32,64},{64,96},{96,0},{1,33},{33,65},{65,97},{97,1},{2,34}... | collective-permute-start | bytes 393224 | tf_op jit(solution)/shard_map/ppermute | solution.py:555
  24.0 7.2 %collective-permute-start.10 = (bf16[64,1024]{1,0:T(8,128)(2,1)S(1)}, bf16[64,1024]{1,0:T(8,128)(2,1)S(1)}, u32[]{:S(2)}, u32[]{:S(2)}) collective-permute-start(bf16[64,1024]{1,0:T(8,128)(2,1)S(1)} %add_convert_fusion.4.refs_0_), channel_id=1, source_target_pairs={{0,16},{16,0},{1,17},{17,1},{2,18},{18,2},{3,19},{19,3},{4,20},{20... | collective-permute-start | bytes 393224 | tf_op jit(solution)/shard_map/ppermute | solution.py:544
  27.5 3.7 %collective-permute-start.13 = (bf16[64,1024]{1,0:T(8,128)(2,1)S(1)}, bf16[64,1024]{1,0:T(8,128)(2,1)S(1)}, u32[]{:S(2)}, u32[]{:S(2)}) collective-permute-start(bf16[64,1024]{1,0:T(8,128)(2,1)S(1)} %collective-permute-done.9.refs_3_), channel_id=1, source_target_pairs={{0,16},{16,0},{1,17},{17,1},{2,18},{18,2},{3,19},{19,3},{4,20},{20... | collective-permute-start | bytes 393224 | tf_op jit(solution)/shard_map/ppermute | solution.py:544
  29.8 1.4 collective-permute-start.12
  38.7 34.2 %all-to-all-start = ((bf16[16,400,128]{2,1,0:T(8,128)(2,1)}), bf16[16,400,128]{2,1,0:T(8,128)(2,1)}, u32[]{:S(2)}, u32[]{:S(2)}) async-start(bf16[16,400,128]{2,1,0:T(8,128)(2,1)} %pooled_dispatch.1), calls=%async_computation | async-start | bytes 3276800 | tf_op jit(solution)/shard_map/all_to_all | solution.py:628
  78.9 10.6 %collective-permute-start.15 = (bf16[4,4,128,128]{3,2,1,0:T(8,128)(2,1)S(1)}, bf16[4,4,128,128]{3,2,1,0:T(8,128)(2,1)S(1)}, u32[]{:S(2)}, u32[]{:S(2)}) collective-permute-start(bf16[4,4,128,128]{3,2,1,0:T(8,128)(2,1)S(1)} %get-tuple-element.49), channel_id=1, source_target_pairs={{0,4},{1,5},{2,6},{3,7},{4,8},{5,9},{6,10},{7,11},{8,12},{9,13},{1... | collective-permute-start | bytes 1572872 | tf_op jit(solution)/shard_map/ppermute | solution.py:456
  85.5 9.6 %collective-permute-start.23 = (bf16[4,4,128,128]{3,2,1,0:T(8,128)(2,1)S(1)}, bf16[4,4,128,128]{3,2,1,0:T(8,128)(2,1)S(1)}, u32[]{:S(2)}, u32[]{:S(2)}) collective-permute-start(bf16[4,4,128,128]{3,2,1,0:T(8,128)(2,1)S(1)} %get-tuple-element.54), channel_id=1, source_target_pairs={{0,12},{1,13},{2,14},{3,15},{4,0},{5,1},{6,2},{7,3},{8,4},{9,5},{1... | collective-permute-start | bytes 1572872 | tf_op jit(solution)/shard_map/ppermute | solution.py:456
  88.4 12.3 %collective-permute-start.14 = (bf16[4,4,128,128]{3,2,1,0:T(8,128)(2,1)S(1)}, bf16[4,4,128,128]{3,2,1,0:T(8,128)(2,1)S(1)}, u32[]{:S(2)}, u32[]{:S(2)}) collective-permute-start(bf16[4,4,128,128]{3,2,1,0:T(8,128)(2,1)S(1)} %get-tuple-element.47), channel_id=1, source_target_pairs={{0,12},{1,13},{2,14},{3,15},{4,0},{5,1},{6,2},{7,3},{8,4},{9,5},{1... | collective-permute-start | bytes 1572872 | tf_op jit(solution)/shard_map/ppermute | solution.py:456
  89.7 11.0 %collective-permute-start.16 = (bf16[4,4,128,128]{3,2,1,0:T(8,128)(2,1)S(1)}, bf16[4,4,128,128]{3,2,1,0:T(8,128)(2,1)S(1)}, u32[]{:S(2)}, u32[]{:S(2)}) collective-permute-start(bf16[4,4,128,128]{3,2,1,0:T(8,128)(2,1)S(1)} %add_convert_fusion.3), channel_id=1, source_target_pairs={{0,4},{1,5},{2,6},{3,7},{4,8},{5,9},{6,10},{7,11},{8,12},{9,13},{1... | collective-permute-start | bytes 1572872 | tf_op jit(solution)/shard_map/ppermute | solution.py:456
  90.6 18.1 %collective-permute-start.22 = (bf16[4,4,128,128]{3,2,1,0:T(8,128)(2,1)S(1)}, bf16[4,4,128,128]{3,2,1,0:T(8,128)(2,1)S(1)}, u32[]{:S(2)}, u32[]{:S(2)}) collective-permute-start(bf16[4,4,128,128]{3,2,1,0:T(8,128)(2,1)S(1)} %get-tuple-element.52), channel_id=1, source_target_pairs={{0,4},{1,5},{2,6},{3,7},{4,8},{5,9},{6,10},{7,11},{8,12},{9,13},{1... | collective-permute-start | bytes 1572872 | tf_op jit(solution)/shard_map/ppermute | solution.py:456
  95.3 13.5 %collective-permute-start.24 = (bf16[4,4,128,128]{3,2,1,0:T(8,128)(2,1)S(1)}, bf16[4,4,128,128]{3,2,1,0:T(8,128)(2,1)S(1)}, u32[]{:S(2)}, u32[]{:S(2)}) collective-permute-start(bf16[4,4,128,128]{3,2,1,0:T(8,128)(2,1)S(1)} %add_convert_fusion.1), channel_id=1, source_target_pairs={{0,12},{1,13},{2,14},{3,15},{4,0},{5,1},{6,2},{7,3},{8,4},{9,5},{1... | collective-permute-start | bytes 1572872 | tf_op jit(solution)/shard_map/ppermute | solution.py:456
  100.9 10.5 %collective-permute-start.18 = (bf16[4,4,128,128]{3,2,1,0:T(8,128)(2,1)S(1)}, bf16[4,4,128,128]{3,2,1,0:T(8,128)(2,1)S(1)}, u32[]{:S(2)}, u32[]{:S(2)}) collective-permute-start(bf16[4,4,128,128]{3,2,1,0:T(8,128)(2,1)S(1)} %add_convert_fusion.2.own_ref), channel_id=1, source_target_pairs={{0,1},{1,2},{2,3},{3,0},{4,5},{5,6},{6,7},{7,4},{8,9},{9,10},{10,1... | collective-permute-start | bytes 1572872 | tf_op jit(solution)/shard_map/ppermute | solution.py:456
  109.0 9.2 %collective-permute-start.25 = (bf16[4,4,128,128]{3,2,1,0:T(8,128)(2,1)S(1)}, bf16[4,4,128,128]{3,2,1,0:T(8,128)(2,1)S(1)}, u32[]{:S(2)}, u32[]{:S(2)}) collective-permute-start(bf16[4,4,128,128]{3,2,1,0:T(8,128)(2,1)S(1)} %add_convert_fusion.own_ref), channel_id=1, source_target_pairs={{0,3},{1,0},{2,1},{3,2},{4,7},{5,4},{6,5},{7,6},{8,11},{9,8},{10,9... | collective-permute-start | bytes 1572872 | tf_op jit(solution)/shard_map/ppermute | solution.py:456
  109.1 14.7 %collective-permute-start.17 = (bf16[4,4,128,128]{3,2,1,0:T(8,128)(2,1)S(1)}, bf16[4,4,128,128]{3,2,1,0:T(8,128)(2,1)S(1)}, u32[]{:S(2)}, u32[]{:S(2)}) collective-permute-start(bf16[4,4,128,128]{3,2,1,0:T(8,128)(2,1)S(1)} %add_convert_fusion.2.own_ref), channel_id=1, source_target_pairs={{0,3},{1,0},{2,1},{3,2},{4,7},{5,4},{6,5},{7,6},{8,11},{9,8},{10,9... | collective-permute-start | bytes 1572872 | tf_op jit(solution)/shard_map/ppermute | solution.py:456
  109.2 17.1 %collective-permute-start.27 = (bf16[4,4,128,128]{3,2,1,0:T(8,128)(2,1)S(1)}, bf16[4,4,128,128]{3,2,1,0:T(8,128)(2,1)S(1)}, u32[]{:S(2)}, u32[]{:S(2)}) collective-permute-start(bf16[4,4,128,128]{3,2,1,0:T(8,128)(2,1)S(1)} %add_convert_fusion.own_ref), channel_id=1, source_target_pairs={{0,1},{1,2},{2,3},{3,0},{4,5},{5,6},{6,7},{7,4},{8,9},{9,10},{10,1... | collective-permute-start | bytes 1572872 | tf_op jit(solution)/shard_map/ppermute | solution.py:456
  111.4 13.9 %collective-permute-start.19 = (bf16[4,4,128,128]{3,2,1,0:T(8,128)(2,1)S(1)}, bf16[4,4,128,128]{3,2,1,0:T(8,128)(2,1)S(1)}, u32[]{:S(2)}, u32[]{:S(2)}) collective-permute-start(bf16[4,4,128,128]{3,2,1,0:T(8,128)(2,1)S(1)} %collective-permute-done.18.prev_ref), channel_id=1, source_target_pairs={{0,1},{1,2},{2,3},{3,0},{4,5},{5,6},{6,7},{7,4},{8,9},{9,10},{10,1... | collective-permute-start | bytes 1572872 | tf_op jit(solution)/shard_map/ppermute | solution.py:456
  118.2 12.9 %collective-permute-start.26 = (bf16[4,4,128,128]{3,2,1,0:T(8,128)(2,1)S(1)}, bf16[4,4,128,128]{3,2,1,0:T(8,128)(2,1)S(1)}, u32[]{:S(2)}, u32[]{:S(2)}) collective-permute-start(bf16[4,4,128,128]{3,2,1,0:T(8,128)(2,1)S(1)} %collective-permute-done.25.next_ref), channel_id=1, source_target_pairs={{0,3},{1,0},{2,1},{3,2},{4,7},{5,4},{6,5},{7,6},{8,11},{9,8},{10,9... | collective-permute-start | bytes 1572872 | tf_op jit(solution)/shard_map/ppermute | solution.py:456
  126.1 16.0 %collective-permute-start.20 = (bf16[4,4,128,128]{3,2,1,0:T(8,128)(2,1)S(1)}, bf16[4,4,128,128]{3,2,1,0:T(8,128)(2,1)S(1)}, u32[]{:S(2)}, u32[]{:S(2)}) collective-permute-start(bf16[4,4,128,128]{3,2,1,0:T(8,128)(2,1)S(1)} %get-tuple-element.50.refs_0_), channel_id=1, source_target_pairs={{0,4},{1,5},{2,6},{3,7},{4,8},{5,9},{6,10},{7,11},{8,12},{9,13},{1... | collective-permute-start | bytes 1572872 | tf_op jit(solution)/shard_map/ppermute | solution.py:456
  132.0 12.1 %collective-permute-start.28 = (bf16[4,4,128,128]{3,2,1,0:T(8,128)(2,1)S(1)}, bf16[4,4,128,128]{3,2,1,0:T(8,128)(2,1)S(1)}, u32[]{:S(2)}, u32[]{:S(2)}) collective-permute-start(bf16[4,4,128,128]{3,2,1,0:T(8,128)(2,1)S(1)} %get-tuple-element.55.refs_1_), channel_id=1, source_target_pairs={{0,12},{1,13},{2,14},{3,15},{4,0},{5,1},{6,2},{7,3},{8,4},{9,5},{1... | collective-permute-start | bytes 1572872 | tf_op jit(solution)/shard_map/ppermute | solution.py:456
  140.1 14.3 %collective-permute-start.30 = (bf16[4,4,128,128]{3,2,1,0:T(8,128)(2,1)S(1)}, bf16[4,4,128,128]{3,2,1,0:T(8,128)(2,1)S(1)}, u32[]{:S(2)}, u32[]{:S(2)}) collective-permute-start(bf16[4,4,128,128]{3,2,1,0:T(8,128)(2,1)S(1)} %get-tuple-element.50.refs_0_), channel_id=1, source_target_pairs={{0,12},{1,13},{2,14},{3,15},{4,0},{5,1},{6,2},{7,3},{8,4},{9,5},{1... | collective-permute-start | bytes 1572872 | tf_op jit(solution)/shard_map/ppermute | solution.py:456
  140.1 14.3 %collective-permute-start.31 = (bf16[4,4,128,128]{3,2,1,0:T(8,128)(2,1)S(1)}, bf16[4,4,128,128]{3,2,1,0:T(8,128)(2,1)S(1)}, u32[]{:S(2)}, u32[]{:S(2)}) collective-permute-start(bf16[4,4,128,128]{3,2,1,0:T(8,128)(2,1)S(1)} %get-tuple-element.55.refs_1_), channel_id=1, source_target_pairs={{0,4},{1,5},{2,6},{3,7},{4,8},{5,9},{6,10},{7,11},{8,12},{9,13},{1... | collective-permute-start | bytes 1572872 | tf_op jit(solution)/shard_map/ppermute | solution.py:456
  142.1 14.8 %collective-permute-start.21 = (bf16[4,4,128,128]{3,2,1,0:T(8,128)(2,1)S(1)}, bf16[4,4,128,128]{3,2,1,0:T(8,128)(2,1)S(1)}, u32[]{:S(2)}, u32[]{:S(2)}) collective-permute-start(bf16[4,4,128,128]{3,2,1,0:T(8,128)(2,1)S(1)} %collective-permute-done.20.refs_4_), channel_id=1, source_target_pairs={{0,4},{1,5},{2,6},{3,7},{4,8},{5,9},{6,10},{7,11},{8,12},{9,13},{1... | collective-permute-start | bytes 1572872 | tf_op jit(solution)/shard_map/ppermute | solution.py:456
  144.1 12.9 %collective-permute-start.29 = (bf16[4,4,128,128]{3,2,1,0:T(8,128)(2,1)S(1)}, bf16[4,4,128,128]{3,2,1,0:T(8,128)(2,1)S(1)}, u32[]{:S(2)}, u32[]{:S(2)}) collective-permute-start(bf16[4,4,128,128]{3,2,1,0:T(8,128)(2,1)S(1)} %collective-permute-done.28.refs_3_), channel_id=1, source_target_pairs={{0,12},{1,13},{2,14},{3,15},{4,0},{5,1},{6,2},{7,3},{8,4},{9,5},{1... | collective-permute-start | bytes 1572872 | tf_op jit(solution)/shard_map/ppermute | solution.py:456
  (10 other events, 243.8 us)

commit v6 on v5

--- a/solution.py
+++ b/solution.py
@@ -113,24 +113,37 @@
     )(where, *ins)
 
 
-def pooled_kernel(at_ref, *refs):
-    pieces, (cot_ref, co_ref, ci_ref, bias_ref, pos_ref, dig_ref, out_ref, key_ref, rank_ref) = (
-        refs[: NC * NX],
-        refs[NC * NX :],
-    )
+def join_kernel(at_ref, *refs):
+    pieces, rank_ref = refs[:-1], refs[-1]
+    size = pieces[0].shape[0]
+    for i, piece in enumerate(pieces):
+        c = at_ref[0] if i < NX else 1 - at_ref[0]
+        row = (c * NX + (at_ref[1] + NX - i % NX) % NX) * size
+        rank_ref[pl.ds(pl.multiple_of(row, size), size), :] = piece[...]
+
+
+def join(where, pieces):
+    size, width = pieces[0].shape
+    vmem = pl.BlockSpec(memory_space=pltpu.VMEM)
+    return pl.pallas_call(
+        join_kernel,
+        out_shape=pltpu.VMEM((len(pieces) * size, width), bf),
+        grid_spec=pltpu.PrefetchScalarGridSpec(
+            num_scalar_prefetch=1, grid=(), in_specs=[vmem] * len(pieces), out_specs=vmem
+        ),
+        compiler_params=pltpu.CompilerParams(vmem_limit_bytes=8 << 20),
+        name="join",
+    )(where, *pieces)
+
+
+def pooled_kernel(first, rank_ref, *refs):
+    cot_ref, co_ref, ci_ref, bias_ref, pos_ref, dig_ref = refs[:6]
+    outs, (key_ref,) = refs[6:10], refs[10:]
     rank = co_ref.shape[1]
     width, cap = key_ref.shape[1], CAP
 
-    @pl.when(pl.program_id(0) == 0)
-    def _():
-        size = pieces[0].shape[0]
-        for i, piece in enumerate(pieces):
-            c = at_ref[0] if i < NX else 1 - at_ref[0]
-            row = (c * NX + (at_ref[1] + NX - i % NX) % NX) * size
-            rank_ref[pl.ds(pl.multiple_of(row, size), size), :] = piece[...]
-
-    dests = out_ref.shape[0]
-    tables = (out_ref.shape[1] - KEY_ROWS) // cap
+    dests = 4 * outs[0].shape[0]
+    half = (outs[0].shape[1] - KEY_ROWS) // cap
     samples = cot_ref.shape[0]
     here = pos_ref.shape[0]
     step = pl.program_id(0)
@@ -146,11 +159,13 @@
     for k in range(here):
         t = step * here + k
         placed = jnp.where(slot == pos_ref[k], 1.0, 0.0).astype(bf)
-        digits = jnp.where(owner == t, dig_ref[...].astype(f32), 0.0).astype(bf)
+        digits = jnp.where(owner == first + t, dig_ref[...].astype(f32), 0.0).astype(bf)
         both = jnp.concatenate([pooled[:, k * width : (k + 1) * width], digits], axis=1)
         rows = jnp.dot(placed, both, preferred_element_type=f32)
         spot = pl.ds(pl.multiple_of(t * cap, KEY_ROWS), cap)
-        out_ref[:, spot] = rows[:, :width].astype(bf).reshape(dests, cap, width)
+        vals = rows[:, :width].astype(bf).reshape(4, dests // 4, cap, width)
+        for r, out in enumerate(outs):
+            out[:, spot] = vals[r]
         keys = keys + rows[:, width:]
 
     @pl.when(step == 0)
@@ -168,38 +183,38 @@
         packed = jnp.zeros((dests, KEY_ROWS, width), f32)
         for k in range(cap // KEY_ROWS):
             packed = jnp.where(group == k, parts[:, k], packed)
-        out_ref[:, tables * cap :] = packed.astype(bf)
-
-
-def pooled_dispatch(where, pieces, cot, co, ci, bias, pos, digits, dests, cap, width):
+        for r, out in enumerate(outs):
+            out[:, half * cap :] = packed[r * (dests // 4) : (r + 1) * (dests // 4)].astype(bf)
+
+
+def pooled_dispatch(first, count, rank, cot, co, ci, bias, pos, digits, dests, cap, width):
     samples = cot.shape[0]
-    tables = pos.shape[0]
     pair = 2
-    out = (dests, tables * cap + KEY_ROWS, width)
+    skip = first // pair
+    out = jax.ShapeDtypeStruct((dests // 4, count * cap + KEY_ROWS, width), bf)
     return pl.pallas_call(
-        pooled_kernel,
-        out_shape=pltpu.HBM(out, bf),
-        grid_spec=pltpu.PrefetchScalarGridSpec(
-            num_scalar_prefetch=1,
-            grid=(tables // pair,),
-            in_specs=[pl.BlockSpec(memory_space=pltpu.VMEM)] * len(pieces)
-            + [
-                pl.BlockSpec((samples, pair * width), lambda i, w: (0, i)),
-                pl.BlockSpec((pair * width, co.shape[1]), lambda i, w: (i, 0)),
-                pl.BlockSpec((pair * width, co.shape[1]), lambda i, w: (i, 0)),
-                pl.BlockSpec((1, pair * width), lambda i, w: (0, i)),
-                pl.BlockSpec((pair, 1, samples), lambda i, w: (i, 0, 0)),
-                pl.BlockSpec(digits.shape, lambda i, w: (0, 0)),
-            ],
-            out_specs=pl.BlockSpec(out, lambda i, w: (0, 0, 0)),
-            scratch_shapes=[
-                pltpu.VMEM((dests * cap, width), f32),
-                pltpu.VMEM((samples, pieces[0].shape[1]), bf),
-            ],
+        functools.partial(pooled_kernel, first),
+        out_shape=(out,) * 4,
+        grid=(count // pair,),
+        in_specs=[
+            pl.BlockSpec(memory_space=pltpu.VMEM),
+            pl.BlockSpec((samples, pair * width), lambda i: (0, skip + i)),
+            pl.BlockSpec((pair * width, co.shape[1]), lambda i: (skip + i, 0)),
+            pl.BlockSpec((pair * width, co.shape[1]), lambda i: (skip + i, 0)),
+            pl.BlockSpec((1, pair * width), lambda i: (0, skip + i)),
+            pl.BlockSpec((pair, 1, samples), lambda i: (skip + i, 0, 0)),
+            pl.BlockSpec(digits.shape, lambda i: (0, 0)),
+        ],
+        out_specs=[pl.BlockSpec(out.shape, lambda i: (0, 0, 0))] * 4,
+        scratch_shapes=[pltpu.VMEM((dests * cap, width), f32)],
+        cost_estimate=pl.CostEstimate(
+            flops=count * samples * width * 4 * (co.shape[1] + dests * cap),
+            bytes_accessed=4 << 20,
+            transcendentals=0,
         ),
         compiler_params=pltpu.CompilerParams(vmem_limit_bytes=12 << 20),
         name="pooled_dispatch",
-    )(where, *pieces, cot, co, ci, bias, pos, digits)
+    )(rank, cot, co, ci, bias, pos, digits)
 
 
 DIGITS, QB, MB, LANES, KEY_ROWS, CAP = 4, 32, 64, 32, 16, 48
@@ -283,38 +298,54 @@
         store(half + p * size, sums[:, width:])
 
 
-def stage_kernel(from_ref, to_ref, sem):
-    copy = pltpu.make_async_copy(from_ref, to_ref, sem)
-    copy.start()
-    copy.wait()
-
-
-def stage(a):
+def stage_kernel(*refs):
+    sem = refs[-1]
+    count = len(refs) // 2
+    copies = [pltpu.make_async_copy(refs[i], refs[count + i], sem.at[i]) for i in range(count)]
+    for copy in copies:
+        copy.start()
+    for copy in copies:
+        copy.wait()
+
+
+def stage(*arrays):
+    size = sum(a.size for a in arrays)
     return pl.pallas_call(
         stage_kernel,
-        out_shape=pltpu.VMEM(a.shape, a.dtype),
-        in_specs=[pl.BlockSpec(memory_space=pltpu.HBM)],
-        out_specs=pl.BlockSpec(memory_space=pltpu.VMEM),
-        scratch_shapes=[pltpu.SemaphoreType.DMA],
-        cost_estimate=pl.CostEstimate(flops=0, bytes_accessed=2 * a.size, transcendentals=0),
+        out_shape=[pltpu.VMEM(a.shape, a.dtype) for a in arrays],
+        in_specs=[pl.BlockSpec(memory_space=pltpu.HBM)] * len(arrays),
+        out_specs=[pl.BlockSpec(memory_space=pltpu.VMEM)] * len(arrays),
+        scratch_shapes=[pltpu.SemaphoreType.DMA((len(arrays),))],
+        cost_estimate=pl.CostEstimate(flops=0, bytes_accessed=4 * size, transcendentals=0),
         compiler_params=pltpu.CompilerParams(vmem_limit_bytes=8 << 20),
         name="stage",
-    )(pltpu.with_memory_space_constraint(a, pltpu.HBM))
-
-
-def rem_kernel(first, count, where_ref, got_ref, slab_ref, r0, r1, r2, r3, sum_ref):
-    tables, _, width = slab_ref.shape
-    sources, cap = got_ref.shape[0], CAP
-    slots = sources * cap
+    )(*[pltpu.with_memory_space_constraint(a, pltpu.HBM) for a in arrays])
+
+
+def all_keys(refs, at=None):
+    keys = [ref[...] if at is None else ref[:, at:] for ref in refs]
+    return unpack_keys(jnp.concatenate(keys, axis=0))
+
+
+def all_rows(refs, at, cap):
+    rows = [ref[:, at : at + cap] for ref in refs]
+    rows = [row.reshape(-1, row.shape[-1]) for row in rows]
+    return jnp.concatenate(rows, axis=0).astype(f32)
+
+
+def rem_kernel(first, count, where_ref, *refs):
+    (slab_ref, r0, r1, r2, r3, sum_ref), parts = refs[-6:], refs[:-6]
+    tables, _, _ = slab_ref.shape
+    cap = CAP
     rem_rows = sum_ref.shape[0]
-    keys = unpack_keys(got_ref[:, tables * cap :])
+    keys = all_keys(parts, count * cap)
     rows = key_rows(keys, tables)
     sub_rows = r0.shape[2]
     at = where_ref[1]
     along_z = where_ref[0] == 0
     for k in range(count):
         t = first + k
-        g = got_ref[:, t * cap : (t + 1) * cap].reshape(slots, width).astype(f32)
+        g = all_rows(parts[:4], k * cap, cap)
         q, m = key_lanes(keys, t)
         val = g * pick(q, slab_ref[t])
 
@@ -332,8 +363,9 @@
 
 
 def rem_parts(first, count, where, got, slab, rem_rows):
-    sources, _, width = got.shape
-    slots = sources * CAP
+    _, _, width = slab.shape
+    slots = NZ * NY * CAP
+    ins = got
     sub = rem_rows // (NZ * NY)
     piece = jax.ShapeDtypeStruct((count, 4, sub, width), bf)
     return pl.pallas_call(
@@ -342,7 +374,7 @@
         grid_spec=pltpu.PrefetchScalarGridSpec(
             num_scalar_prefetch=1,
             grid=(),
-            in_specs=[pl.BlockSpec(memory_space=pltpu.VMEM)] * 2,
+            in_specs=[pl.BlockSpec(memory_space=pltpu.VMEM)] * (len(ins) + 1),
             out_specs=[pl.BlockSpec(memory_space=pltpu.VMEM)] * 4,
             scratch_shapes=[pltpu.VMEM((rem_rows, width), bf)],
         ),
@@ -351,7 +383,7 @@
         ),
         compiler_params=pltpu.CompilerParams(vmem_limit_bytes=12 << 20),
         name="rem_parts",
-    )(where, got, slab)
+    )(where, *ins, slab)
 
 
 def lane_mean(x):
@@ -365,22 +397,22 @@
     )
 
 
-def quot_kernel(first, tables, g_ref, pack_ref, rtab_ref, slab_ref, acc_ref, *refs):
+def quot_kernel(first, tables, *refs):
+    parts, packs, (rtab_ref, slab_ref, acc_ref), refs = refs[:4], refs[4:8], refs[8:11], refs[11:]
     quot_ref, out_ref, key_ref, row_ref, sum_ref, col_ref, done_ref = refs[-7:]
-    sources, cap, width = g_ref.shape
-    slots = sources * cap
+    cap, width = parts[0].shape[1:]
     quot_rows = quot_ref.shape[1]
     step = pl.program_id(0)
     t = first + step
 
     @pl.when(step == 0)
     def _():
-        keys = unpack_keys(pack_ref[...])
+        keys = all_keys(packs)
         key_ref[...] = keys
         row_ref[...] = key_rows(keys, tables)
         col_ref[...] = acc_ref[...].T
 
-    g = g_ref[...].reshape(slots, width).astype(f32)
+    g = all_rows(parts, 0, cap)
     q, m = key_lanes(key_ref[...], t)
     val = g * pick(m, rtab_ref[0])
 
@@ -406,13 +438,12 @@
 
 
 def quot_update(first, count, got, rtab, slab, accum, old=None):
-    sources, _, width = got.shape
-    tables, rem_rows, _ = rtab.shape
+    tables, rem_rows, width = rtab.shape
     quot_rows = slab.shape[1]
-    slots = sources * CAP
+    slots = NZ * NY * CAP
     rtab = pltpu.with_memory_space_constraint(rtab, pltpu.HBM)
     slab = pltpu.with_memory_space_constraint(slab, pltpu.HBM)
-    ins, extra, alias = [got, got, rtab, slab, accum], [], {}
+    ins, extra, alias = [*got, *got, rtab, slab, accum], [], {}
     if old is not None:
         ins.append(old)
         extra = [pl.BlockSpec(memory_space=pltpu.HBM)]
@@ -425,8 +456,9 @@
         ),
         grid=(count,),
         in_specs=[
-            pl.BlockSpec((sources, CAP, width), lambda t: (0, first + t, 0)),
-            pl.BlockSpec((sources, KEY_ROWS, width), lambda t: (0, tables * CAP // KEY_ROWS, 0)),
+            *[pl.BlockSpec((4, CAP, width), lambda t: (0, t, 0))] * 4,
+            *[pl.BlockSpec((4, KEY_ROWS, width), lambda t: (0, count * CAP // KEY_ROWS, 0))]
+            * 4,
             pl.BlockSpec((1, rem_rows, width), lambda t: (first + t, 0, 0)),
             pl.BlockSpec((1, quot_rows, width), lambda t: (first + t, 0, 0)),
             pl.BlockSpec((tables, quot_rows), lambda t: (0, 0)),
@@ -461,6 +493,20 @@
     for p in parts[1:]:
         total = total + p.astype(f32)
     return total
+
+
+def swap_rows(low, high):
+    def first(parts):
+        far = turn(parts[2], 2, False)
+        return (parts[0], turn(parts[1], 1, False), far, turn(parts[3], 3, False))
+
+    def second(parts):
+        parts = [jnp.stack([part[j] for part in parts]) for j in range(4)]
+        far = turn(parts[2], 2, True)
+        return (parts[0], turn(parts[1], 1, True), far, turn(parts[3], 3, True))
+
+    low, high = first(low), first(high)
+    return second(low), second(high)
 
 
 def ring_scatter(low, high, flip):
@@ -605,7 +651,10 @@
     cap = CAP
     ci, zi, yi = lax.axis_index("c"), lax.axis_index("z"), lax.axis_index("y")
 
-    target = dest_shard[:, :, 0]
+    shard = dest_shard[:, :, 0]
+    far_z = (shard // NY - zi) & (NZ - 1)
+    far_y = (shard % NY - yi) & (NY - 1)
+    target = jnp.where(ci == 0, far_z * NY + far_y, far_y * NZ + far_z)
     onehot = target[:, :, None] == jnp.arange(rows, dtype=jnp.int32)[None, None, :]
     lower = (
         jnp.arange(samples, dtype=jnp.int32)[:, None]
@@ -621,19 +670,29 @@
         features, cotangent, cross_in, cross_out, (position, digits)
     )
     xi = lax.axis_index("x")
-    send = pooled_dispatch(
-        jnp.stack([ci, xi]).astype(jnp.int32), pieces, cotangent, cross_out, cross_in,
-        bias.reshape(1, -1), position, digits, rows, cap, width,
-    )
-    got = lax.all_to_all(send, ("z", "y"), split_axis=0, concat_axis=0, tiled=True)
-    slab = stage(quot_slab)
+    half = tables // 2
+    dense = [
+        pltpu.with_memory_space_constraint(a, pltpu.HBM)
+        for a in (cotangent, cross_out, cross_in)
+    ]
+    rank = join(jnp.stack([ci, xi]).astype(jnp.int32), pieces)
+    sends = []
+    for first in (0, half):
+        sends.append(
+            pooled_dispatch(
+                first, half, rank, *dense, bias.reshape(1, -1), position, digits,
+                rows, cap, width,
+            )
+        )
+    got_low, got_high = swap_rows(*sends)
+    (slab,) = stage(quot_slab)
     along_z = ci == 0
     at_one = jnp.where(along_z, zi, yi)
     at_two = jnp.where(along_z, yi, zi)
     where = jnp.stack([ci, at_one, at_one]).astype(jnp.int32)
     half = tables // 2
-    low = rem_parts(0, half, where, got, slab, rem_rows)
-    high = rem_parts(half, half, where, got, slab, rem_rows)
+    low = rem_parts(0, half, where, got_low, slab, rem_rows)
+    high = rem_parts(half, half, where, got_high, slab, rem_rows)
 
     one_low, one_high = ring_scatter(low, high, False)
     ring_low, ring_high = ring_gather(one_low.astype(bf), one_high.astype(bf), True)
@@ -660,8 +719,12 @@
     rem_out = place((2,), where, [(all_low[2], all_high[2])], shape, rem_out)
     rem_out = rem_out.reshape(tables, rem_rows, width)
 
-    quot_out, acc_low = quot_update(0, half, got, rem_table, quot_slab, quot_accum)
-    quot_out, acc_high = quot_update(half, half, got, rem_table, quot_slab, quot_accum, quot_out)
+    quot_out, acc_low = quot_update(
+        0, half, got_low, rem_table, quot_slab, quot_accum
+    )
+    quot_out, acc_high = quot_update(
+        half, half, got_high, rem_table, quot_slab, quot_accum, quot_out
+    )
     quot_acc_out = jnp.concatenate([acc_low[:half], acc_high[:half]], axis=0)
     return (quot_out, quot_acc_out, rem_out, rem_acc_out)
 

time: 159 us -> 161 us (1.013)
  starting transfers between devices: 39.5 us -> 65 us
  waiting for transfers between devices: 61.9 us -> 41.6 us
  other arithmetic: 8.3 us -> 4.7 us
  Pallas kernels: 45.3 us -> 43.4 us
    ppermute x18 -> x30, starting transfers between devices: 19.8 us -> 52.1 us  [turn(): return lax.ppermute(a, CZY, turn_pairs(s, flip))]
    all_to_all x1 -> x0, waiting for transfers between devices: 24.4 us -> none  [device_step(): lax.all_to_all(send, ('z', 'y'), split_axis=0, concat_axis=0, tiled=True)]
    all_to_all x1 -> x0, starting transfers between devices: 8.1 us -> none  [device_step(): lax.all_to_all(send, ('z', 'y'), split_axis=0, concat_axis=0, tiled=True)]
    ppermute x18 -> x30, waiting for transfers between devices: 28.6 us -> 33.2 us  [turn(): return lax.ppermute(a, CZY, turn_pairs(s, flip))]
    ppermute x1, waiting for transfers between devices: 3.52 us -> 0.06 us  [rank_sums(): nxt = lax.ppermute(mine, 'x', ring(NX, 3))]
    ppermute x1, starting transfers between devices: 0.01 us -> 3.11 us  [rank_sums(): far = lax.ppermute(mine, 'x', ring(NX, 2))]
    ppermute x1, starting transfers between devices: 3.14 us -> 0.22 us  [rank_sums(): nxt = lax.ppermute(mine, 'x', ring(NX, 3))]
    pallas_call x2, Pallas kernels: 11.9 us -> 9.06 us  [rem_parts(): pl.pallas_call(functools.partial(rem_kernel, first, count), out_shape=(pi...]
  transfers between devices with their start and end apart: 33 -> 44, of which waited for: 15 -> 16; matrix products, arithmetic and copies ran while one was open for 6% -> 3% of each run, Pallas kernels for 17% -> 20%
where the time goes in v6:
time: 161 us; the launch traced here: 160 us
  starting transfers between devices  65 us (40%)
  Pallas kernels  43.4 us (27%)
  waiting for transfers between devices  41.6 us (26%)
  other arithmetic  4.7 us (3%)
  local copies, waits for them, and re-layouts  3.22 us (2%)
    ppermute x30, starting transfers between devices, turn(): return lax.ppermute(a, CZY, turn_pairs(s, flip))  52.1 us
    ppermute x30, waiting for transfers between devices, turn(): return lax.ppermute(a, CZY, turn_pairs(s, flip))  33.2 us
    pallas_call x2, Pallas kernels, quot_update(): pl.pallas_call(functools.partial(quot_kernel, first, tables), out_shape=(...  16.3 us
    pallas_call x2, Pallas kernels, rem_parts(): pl.pallas_call(functools.partial(rem_kernel, first, count), out_shape=(pi...  9.06 us
    pallas_call x2, Pallas kernels, pooled_dispatch(): pl.pallas_call(functools.partial(pooled_kernel, first), out_shape=(out,)...  6.37 us
    pallas_call x2, Pallas kernels, place(): pl.pallas_call(functools.partial(place_kernel, rels), out_shape=jax.Shape...  4.16 us
    pallas_call x1, Pallas kernels, rank_parts(): pl.pallas_call(rank_kernel, out_shape=(jax.ShapeDtypeStruct(shape, bf),)...  3.59 us
  transfers between devices with their start and end apart: 44, of which 16 were waited for; matrix products, arithmetic and copies ran while one was open for 3% of the time, Pallas kernels for 20%

profile of v6, /device:TPU:0, one launch (start us, length us, event | category | flops | bytes accessed | tf_op | source)
XLA Modules:
  0.0 159.6 jit_solution(12497588264680789153)
XLA Ops:
  0.8 3.6 %rank_parts.1 = (bf16[64,1024]{1,0:T(8,128)(2,1)S(1)}, bf16[64,1024]{1,0:T(8,128)(2,1)S(1)}, bf16[64,1024]{1,0:T(8,128)(2,1)S(1)}, bf16[64,1024]{1,0:T(8,128)(2,...) custom-call(s32[2]{0:T(128)S(1)} %pad_add_fusion.at_ref, ...), custom_call_target="tpu_custom_call" | custom-call | flops 1073741824 | bytes 8388608 | tf_op jit(solution)/shard_map/rank_parts/pallas_call | solution.py:90
  6.2 3.2 %collective-permute-start.2 = (bf16[64,1024]{1,0:T(8,128)(2,1)S(1)}, bf16[64,1024]{1,0:T(8,128)(2,1)S(1)}, u32[]{:S(2)}, u32[]{:S(2)}) collective-permute-start(bf16[64,1024]{1,0:T(8,128)(2,1)S(1)} %add_convert_fusion.7), channel_id=1, source_target_pairs={{0,64},{32,96},{64,0},{96,32},{1,65},{33,97},{65,1},{97,33},{2,66}... | collective-permute-start | bytes 393224 | tf_op jit(solution)/shard_map/ppermute | solution.py:595
  10.2 2.7 %collective-permute-start.6 = (bf16[64,1024]{1,0:T(8,128)(2,1)S(1)}, bf16[64,1024]{1,0:T(8,128)(2,1)S(1)}, u32[]{:S(2)}, u32[]{:S(2)}) collective-permute-start(bf16[64,1024]{1,0:T(8,128)(2,1)S(1)} %add_convert_fusion.5), channel_id=1, source_target_pairs={{0,96},{32,0},{64,32},{96,64},{1,97},{33,1},{65,33},{97,65},{2,98}... | collective-permute-start | bytes 393224 | tf_op jit(solution)/shard_map/ppermute | solution.py:597
  14.1 2.3 %collective-permute-done.4 = bf16[64,1024]{1,0:T(8,128)(2,1)S(1)} collective-permute-done((bf16[64,1024]{1,0:T(8,128)(2,1)S(1)}, bf16[64,1024]{1,0:T(8,128)(2,1)S(1)}, u32[]{:S(2)}, u32[]{:S(2)}) %collective-permute-start.4) | collective-permute-done | bytes 131104 | tf_op jit(solution)/shard_map/ppermute | solution.py:596
  18.0 3.1 %collective-permute-start.8 = (bf16[64,1024]{1,0:T(8,128)(2,1)S(1)}, bf16[64,1024]{1,0:T(8,128)(2,1)S(1)}, u32[]{:S(2)}, u32[]{:S(2)}) collective-permute-start(bf16[64,1024]{1,0:T(8,128)(2,1)S(1)} %add_convert_fusion.4.refs_0_), channel_id=1, source_target_pairs={{0,64},{32,96},{64,0},{96,32},{1,65},{33,97},{65,1},{97,33},{2,66}... | collective-permute-start | bytes 393224 | tf_op jit(solution)/shard_map/ppermute | solution.py:600
  21.3 2.6 %collective-permute-done.7.refs_1_ = bf16[64,1024]{1,0:T(8,128)(2,1)S(1)} collective-permute-done((bf16[64,1024]{1,0:T(8,128)(2,1)S(1)}, bf16[64,1024]{1,0:T(8,128)(2,1)S(1)}, u32[]{:S(2)}, u32[]{:S(2)}) %collective-permute-start.7) | collective-permute-done | bytes 131104 | tf_op jit(solution)/shard_map/ppermute | solution.py:601
  23.9 2.5 %collective-permute-done.8.refs_2_ = bf16[64,1024]{1,0:T(8,128)(2,1)S(1)} collective-permute-done((bf16[64,1024]{1,0:T(8,128)(2,1)S(1)}, bf16[64,1024]{1,0:T(8,128)(2,1)S(1)}, u32[]{:S(2)}, u32[]{:S(2)}) %collective-permute-start.8) | collective-permute-done | bytes 131104 | tf_op jit(solution)/shard_map/ppermute | solution.py:600
  29.2 3.2 %pooled_dispatch.2 = (bf16[4,208,128]{2,1,0:T(8,128)(2,1)S(1)}, bf16[4,208,128]{2,1,0:T(8,128)(2,1)S(1)}, bf16[4,208,128]{2,1,0:T(8,128)(2,1)S(1)}, bf16[4,208,128]{2,1,0:T(8,128)(2,1)S(1)}) custom-call(bf16[512,1024]{1,0:T(8,128)(2,1)S(1)} %join.1.rank_ref, bf16[512,1024]{1,0:T(8,128)(2,1)} %refs_0_.4, bf16[1024,512]{1,0:T(8,128)(2,1)} %refs_1_.3, ...), custom_call_target="tpu_custom_call" | custom-call | flops 1342177280 | bytes 4194304 | tf_op jit(solution)/shard_map/pooled_dispatch/pallas_call | solution.py:195
  32.4 3.2 %pooled_dispatch.3 = (bf16[4,208,128]{2,1,0:T(8,128)(2,1)S(1)}, bf16[4,208,128]{2,1,0:T(8,128)(2,1)S(1)}, bf16[4,208,128]{2,1,0:T(8,128)(2,1)S(1)}, bf16[4,208,128]{2,1,0:T(8,128)(2,1)S(1)}) custom-call(bf16[512,1024]{1,0:T(8,128)(2,1)S(1)} %join.1.rank_ref, bf16[512,1024]{1,0:T(8,128)(2,1)} %refs_0_.4, bf16[1024,512]{1,0:T(8,128)(2,1)} %refs_1_.3, ...), custom_call_target="tpu_custom_call" | custom-call | flops 1342177280 | bytes 4194304 | tf_op jit(solution)/shard_map/pooled_dispatch/pallas_call | solution.py:195
  35.6 4.0 %collective-permute-start.15 = (bf16[4,208,128]{2,1,0:T(8,128)(2,1)S(1)}, bf16[4,208,128]{2,1,0:T(8,128)(2,1)S(1)}, u32[]{:S(2)}, u32[]{:S(2)}) collective-permute-start(bf16[4,208,128]{2,1,0:T(8,128)(2,1)S(1)} %get-tuple-element.52), channel_id=1, source_target_pairs={{0,8},{1,9},{2,10},{3,11},{4,12},{5,13},{6,14},{7,15},{8,0},{9,1},... | collective-permute-start | bytes 638984 | tf_op jit(solution)/shard_map/ppermute | solution.py:488
  42.7 2.4 %collective-permute-start.21 = (bf16[4,208,128]{2,1,0:T(8,128)(2,1)S(1)}, bf16[4,208,128]{2,1,0:T(8,128)(2,1)S(1)}, u32[]{:S(2)}, u32[]{:S(2)}) collective-permute-start(bf16[4,208,128]{2,1,0:T(8,128)(2,1)S(1)} %get-tuple-element.56), channel_id=1, source_target_pairs={{0,8},{1,9},{2,10},{3,11},{4,12},{5,13},{6,14},{7,15},{8,0},{9,1},... | collective-permute-start | bytes 638984 | tf_op jit(solution)/shard_map/ppermute | solution.py:488
  45.1 2.1 %collective-permute-start.22 = (bf16[4,208,128]{2,1,0:T(8,128)(2,1)S(1)}, bf16[4,208,128]{2,1,0:T(8,128)(2,1)S(1)}, u32[]{:S(2)}, u32[]{:S(2)}) collective-permute-start(bf16[4,208,128]{2,1,0:T(8,128)(2,1)S(1)} %get-tuple-element.57), channel_id=1, source_target_pairs={{0,12},{1,13},{2,14},{3,15},{4,0},{5,1},{6,2},{7,3},{8,4},{9,5},{1... | collective-permute-start | bytes 638984 | tf_op jit(solution)/shard_map/ppermute | solution.py:488
  47.4 3.1 %collective-permute-start.19 = (bf16[4,208,128]{2,1,0:T(8,128)(2,1)S(1)}, bf16[4,208,128]{2,1,0:T(8,128)(2,1)S(1)}, u32[]{:S(2)}, u32[]{:S(2)}) collective-permute-start(bf16[4,208,128]{2,1,0:T(8,128)(2,1)S(1)} %pad_maximum_fusion.3), channel_id=1, source_target_pairs={{0,3},{1,0},{2,1},{3,2},{4,7},{5,4},{6,5},{7,6},{8,11},{9,8},{10,9... | collective-permute-start | bytes 638984 | tf_op jit(solution)/shard_map/ppermute | solution.py:488
  55.4 4.3 %collective-permute-start.25 = (bf16[4,208,128]{2,1,0:T(8,128)(2,1)S(1)}, bf16[4,208,128]{2,1,0:T(8,128)(2,1)S(1)}, u32[]{:S(2)}, u32[]{:S(2)}) collective-permute-start(bf16[4,208,128]{2,1,0:T(8,128)(2,1)S(1)} %pad_maximum_fusion.7), channel_id=1, source_target_pairs={{0,3},{1,0},{2,1},{3,2},{4,7},{5,4},{6,5},{7,6},{8,11},{9,8},{10,9... | collective-permute-start | bytes 638984 | tf_op jit(solution)/shard_map/ppermute | solution.py:488
  61.6 4.5 %rem_parts.3 = (bf16[4,4,128,128]{3,2,1,0:T(8,128)(2,1)S(1)}, bf16[4,4,128,128]{3,2,1,0:T(8,128)(2,1)S(1)}, bf16[4,4,128,128]{3,2,1,0:T(8,128)(2,1)S(1)}, bf16[4,4,128,128]{3,2,1,0:T(8,128)(2,1)S(1)}) custom-call(s32[3]{0:T(128)S(1)} %pad_add_fusion.1.where_ref, bf16[4,208,128]{2,1,0:T(8,128)(2,1)S(1)} %pad_maximum_fusion.refs_0_.refs_4_, ...), custom_call_target="tpu_custom_call" | custom-call | flops 3221225472 | bytes 4194304 | tf_op jit(solution)/shard_map/rem_parts/pallas_call | solution.py:371
  66.2 3.5 %collective-permute-start.35 = (bf16[4,4,128,128]{3,2,1,0:T(8,128)(2,1)S(1)}, bf16[4,4,128,128]{3,2,1,0:T(8,128)(2,1)S(1)}, u32[]{:S(2)}, u32[]{:S(2)}) collective-permute-start(bf16[4,4,128,128]{3,2,1,0:T(8,128)(2,1)S(1)} %get-tuple-element.70), channel_id=1, source_target_pairs={{0,12},{1,13},{2,14},{3,15},{4,0},{5,1},{6,2},{7,3},{8,4},{9,5},{1... | collective-permute-start | bytes 1572872 | tf_op jit(solution)/shard_map/ppermute | solution.py:488
  69.7 4.5 %rem_parts.2 = (bf16[4,4,128,128]{3,2,1,0:T(8,128)(2,1)S(1)}, bf16[4,4,128,128]{3,2,1,0:T(8,128)(2,1)S(1)}, bf16[4,4,128,128]{3,2,1,0:T(8,128)(2,1)S(1)}, bf16[4,4,128,128]{3,2,1,0:T(8,128)(2,1)S(1)}) custom-call(s32[3]{0:T(128)S(1)} %pad_add_fusion.1.where_ref, bf16[4,208,128]{2,1,0:T(8,128)(2,1)S(1)} %pad_maximum_fusion.4.refs_0_.refs_4_, ...), custom_call_target="tpu_custom_call" | custom-call | flops 3221225472 | bytes 4194304 | tf_op jit(solution)/shard_map/rem_parts/pallas_call | solution.py:371
  76.5 3.8 %collective-permute-start.36 = (bf16[4,4,128,128]{3,2,1,0:T(8,128)(2,1)S(1)}, bf16[4,4,128,128]{3,2,1,0:T(8,128)(2,1)S(1)}, u32[]{:S(2)}, u32[]{:S(2)}) collective-permute-start(bf16[4,4,128,128]{3,2,1,0:T(8,128)(2,1)S(1)} %add_convert_fusion.1), channel_id=1, source_target_pairs={{0,12},{1,13},{2,14},{3,15},{4,0},{5,1},{6,2},{7,3},{8,4},{9,5},{1... | collective-permute-start | bytes 1572872 | tf_op jit(solution)/shard_map/ppermute | solution.py:488
  80.4 4.4 %collective-permute-done.27 = bf16[4,4,128,128]{3,2,1,0:T(8,128)(2,1)S(1)} collective-permute-done((bf16[4,4,128,128]{3,2,1,0:T(8,128)(2,1)S(1)}, bf16[4,4,128,128]{3,2,1,0:T(8,128)(2,1)S(1)}, u32[]{:S(2)}, u32[]{:S(2)}) %collective-permute-start.27) | collective-permute-done | bytes 524320 | tf_op jit(solution)/shard_map/ppermute | solution.py:488
  85.0 5.4 %collective-permute-done.34 = bf16[4,4,128,128]{3,2,1,0:T(8,128)(2,1)S(1)} collective-permute-done((bf16[4,4,128,128]{3,2,1,0:T(8,128)(2,1)S(1)}, bf16[4,4,128,128]{3,2,1,0:T(8,128)(2,1)S(1)}, u32[]{:S(2)}, u32[]{:S(2)}) %collective-permute-start.34) | collective-permute-done | bytes 524320 | tf_op jit(solution)/shard_map/ppermute | solution.py:488
  90.6 2.2 %collective-permute-start.37 = (bf16[4,4,128,128]{3,2,1,0:T(8,128)(2,1)S(1)}, bf16[4,4,128,128]{3,2,1,0:T(8,128)(2,1)S(1)}, u32[]{:S(2)}, u32[]{:S(2)}) collective-permute-start(bf16[4,4,128,128]{3,2,1,0:T(8,128)(2,1)S(1)} %add_convert_fusion.own_ref), channel_id=1, source_target_pairs={{0,3},{1,0},{2,1},{3,2},{4,7},{5,4},{6,5},{7,6},{8,11},{9,8},{10,9... | collective-permute-start | bytes 1572872 | tf_op jit(solution)/shard_map/ppermute | solution.py:488
  92.8 4.8 %collective-permute-done.26 = bf16[4,4,128,128]{3,2,1,0:T(8,128)(2,1)S(1)} collective-permute-done((bf16[4,4,128,128]{3,2,1,0:T(8,128)(2,1)S(1)}, bf16[4,4,128,128]{3,2,1,0:T(8,128)(2,1)S(1)}, u32[]{:S(2)}, u32[]{:S(2)}) %collective-permute-start.26) | collective-permute-done | bytes 524320 | tf_op jit(solution)/shard_map/ppermute | solution.py:488
  98.2 4.8 %collective-permute-start.30 = (bf16[4,4,128,128]{3,2,1,0:T(8,128)(2,1)S(1)}, bf16[4,4,128,128]{3,2,1,0:T(8,128)(2,1)S(1)}, u32[]{:S(2)}, u32[]{:S(2)}) collective-permute-start(bf16[4,4,128,128]{3,2,1,0:T(8,128)(2,1)S(1)} %add_convert_fusion.2.own_ref), channel_id=1, source_target_pairs={{0,1},{1,2},{2,3},{3,0},{4,5},{5,6},{6,7},{7,4},{8,9},{9,10},{10,1... | collective-permute-start | bytes 1572872 | tf_op jit(solution)/shard_map/ppermute | solution.py:488
  103.4 3.2 %collective-permute-start.29 = (bf16[4,4,128,128]{3,2,1,0:T(8,128)(2,1)S(1)}, bf16[4,4,128,128]{3,2,1,0:T(8,128)(2,1)S(1)}, u32[]{:S(2)}, u32[]{:S(2)}) collective-permute-start(bf16[4,4,128,128]{3,2,1,0:T(8,128)(2,1)S(1)} %add_convert_fusion.2.own_ref), channel_id=1, source_target_pairs={{0,3},{1,0},{2,1},{3,2},{4,7},{5,4},{6,5},{7,6},{8,11},{9,8},{10,9... | collective-permute-start | bytes 1572872 | tf_op jit(solution)/shard_map/ppermute | solution.py:488
  106.6 3.1 %collective-permute-done.30.prev_ref = bf16[4,4,128,128]{3,2,1,0:T(8,128)(2,1)S(1)} collective-permute-done((bf16[4,4,128,128]{3,2,1,0:T(8,128)(2,1)S(1)}, bf16[4,4,128,128]{3,2,1,0:T(8,128)(2,1)S(1)}, u32[]{:S(2)}, u32[]{:S(2)}) %collective-permute-start.30) | collective-permute-done | bytes 524320 | tf_op jit(solution)/shard_map/ppermute | solution.py:488
  109.8 2.5 %collective-permute-start.31 = (bf16[4,4,128,128]{3,2,1,0:T(8,128)(2,1)S(1)}, bf16[4,4,128,128]{3,2,1,0:T(8,128)(2,1)S(1)}, u32[]{:S(2)}, u32[]{:S(2)}) collective-permute-start(bf16[4,4,128,128]{3,2,1,0:T(8,128)(2,1)S(1)} %collective-permute-done.30.prev_ref), channel_id=1, source_target_pairs={{0,1},{1,2},{2,3},{3,0},{4,5},{5,6},{6,7},{7,4},{8,9},{9,10},{10,1... | collective-permute-start | bytes 1572872 | tf_op jit(solution)/shard_map/ppermute | solution.py:488
  115.4 9.2 %collective-permute-done.38.far_ref = bf16[4,4,128,128]{3,2,1,0:T(8,128)(2,1)S(1)} collective-permute-done((bf16[4,4,128,128]{3,2,1,0:T(8,128)(2,1)S(1)}, bf16[4,4,128,128]{3,2,1,0:T(8,128)(2,1)S(1)}, u32[]{:S(2)}, u32[]{:S(2)}) %collective-permute-start.38) | collective-permute-done | bytes 524320 | tf_op jit(solution)/shard_map/ppermute | solution.py:488
  125.4 3.3 %collective-permute-start.40 = (bf16[4,4,128,128]{3,2,1,0:T(8,128)(2,1)S(1)}, bf16[4,4,128,128]{3,2,1,0:T(8,128)(2,1)S(1)}, u32[]{:S(2)}, u32[]{:S(2)}) collective-permute-start(bf16[4,4,128,128]{3,2,1,0:T(8,128)(2,1)S(1)} %get-tuple-element.71.refs_1_), channel_id=1, source_target_pairs={{0,12},{1,13},{2,14},{3,15},{4,0},{5,1},{6,2},{7,3},{8,4},{9,5},{1... | collective-permute-start | bytes 1572872 | tf_op jit(solution)/shard_map/ppermute | solution.py:488
  132.4 8.2 %quot_update.2 = (bf16[8,1024,128]{2,1,0:T(8,128)(2,1)}, f32[8,1024]{1,0:T(8,128)S(1)}) custom-call(bf16[4,208,128]{2,1,0:T(8,128)(2,1)S(1)} %pad_maximum_fusion.4.refs_0_.refs_4_, bf16[4,208,128]{2,1,0:T(8,128)(2,1)S(1)} %copy-done.10, bf16[4,208,128]{2,1,0:T(8,128)(2,1)S(1)} %copy-done.8, bf16[4,208,128]{2,1,0:T(8,128)(2,1)S(1)} %copy-done.6, ...), custom_call_target="tpu_custom_call" | custom-call | flops 3221225472 | bytes 8388608 | tf_op jit(solution)/shard_map/quot_update/pallas_call | solution.py:451
  140.6 3.2 %collective-permute-start.42 = (bf16[4,4,128,128]{3,2,1,0:T(8,128)(2,1)S(1)}, bf16[4,4,128,128]{3,2,1,0:T(8,128)(2,1)S(1)}, u32[]{:S(2)}, u32[]{:S(2)}) collective-permute-start(bf16[4,4,128,128]{3,2,1,0:T(8,128)(2,1)S(1)} %get-tuple-element.66.refs_0_), channel_id=1, source_target_pairs={{0,12},{1,13},{2,14},{3,15},{4,0},{5,1},{6,2},{7,3},{8,4},{9,5},{1... | collective-permute-start | bytes 1572872 | tf_op jit(solution)/shard_map/ppermute | solution.py:488
  145.9 8.1 %quot_update.3 = (bf16[8,1024,128]{2,1,0:T(8,128)(2,1)}, f32[8,1024]{1,0:T(8,128)S(1)}) custom-call(bf16[4,208,128]{2,1,0:T(8,128)(2,1)S(1)} %pad_maximum_fusion.refs_0_.refs_4_, bf16[4,208,128]{2,1,0:T(8,128)(2,1)S(1)} %copy-done.4, bf16[4,208,128]{2,1,0:T(8,128)(2,1)S(1)} %copy-done.2, ...), custom_call_target="tpu_custom_call", output_to_operand_aliasing={{0}: (11, {})} | custom-call | flops 3221225472 | bytes 8388608 | tf_op jit(solution)/shard_map/quot_update/pallas_call | solution.py:451
  155.2 2.5 %place.2.refs_2_ = bf16[8,4,4,128,128]{4,3,2,1,0:T(8,128)(2,1)} custom-call(s32[3]{0:T(128)S(1)} %pad_add_fusion.1.where_ref, bf16[4,4,128,128]{3,2,1,0:T(8,128)(2,1)S(1)} %get-tuple-element.66.refs_0_, bf16[4,4,128,128]{3,2,1,0:T(8,128)(2,1)S(1)} %get-tuple-element.71.refs_1_, bf16[4,4,128,128]{3,2,1,0:T(8,128)(2,1)S(1)} %collective-permute-done.42.refs_2_, ...), custom_call_target="tpu_custom_call" | custom-call | bytes 6291456 | tf_op jit(solution)/shard_map/place/pallas_call | solution.py:567
  (148 shorter events, 34.7 us)
Async XLA Ops:
  5.0 8.2 %collective-permute-start = (bf16[64,1024]{1,0:T(8,128)(2,1)S(1)}, bf16[64,1024]{1,0:T(8,128)(2,1)S(1)}, u32[]{:S(2)}, u32[]{:S(2)}) collective-permute-start(bf16[64,1024]{1,0:T(8,128)(2,1)S(1)} %get-tuple-element.40), channel_id=1, source_target_pairs={{0,16},{16,0},{1,17},{17,1},{2,18},{18,2},{3,19},{19,3},{4,20},{20... | collective-permute-start | bytes 393224 | tf_op jit(solution)/shard_map/ppermute | solution.py:590
  6.2 7.9 %collective-permute-start.2 = (bf16[64,1024]{1,0:T(8,128)(2,1)S(1)}, bf16[64,1024]{1,0:T(8,128)(2,1)S(1)}, u32[]{:S(2)}, u32[]{:S(2)}) collective-permute-start(bf16[64,1024]{1,0:T(8,128)(2,1)S(1)} %add_convert_fusion.7), channel_id=1, source_target_pairs={{0,64},{32,96},{64,0},{96,32},{1,65},{33,97},{65,1},{97,33},{2,66}... | collective-permute-start | bytes 393224 | tf_op jit(solution)/shard_map/ppermute | solution.py:595
  18.0 8.4 %collective-permute-start.8 = (bf16[64,1024]{1,0:T(8,128)(2,1)S(1)}, bf16[64,1024]{1,0:T(8,128)(2,1)S(1)}, u32[]{:S(2)}, u32[]{:S(2)}) collective-permute-start(bf16[64,1024]{1,0:T(8,128)(2,1)S(1)} %add_convert_fusion.4.refs_0_), channel_id=1, source_target_pairs={{0,64},{32,96},{64,0},{96,32},{1,65},{33,97},{65,1},{97,33},{2,66}... | collective-permute-start | bytes 393224 | tf_op jit(solution)/shard_map/ppermute | solution.py:600
  35.6 9.5 %collective-permute-start.15 = (bf16[4,208,128]{2,1,0:T(8,128)(2,1)S(1)}, bf16[4,208,128]{2,1,0:T(8,128)(2,1)S(1)}, u32[]{:S(2)}, u32[]{:S(2)}) collective-permute-start(bf16[4,208,128]{2,1,0:T(8,128)(2,1)S(1)} %get-tuple-element.52), channel_id=1, source_target_pairs={{0,8},{1,9},{2,10},{3,11},{4,12},{5,13},{6,14},{7,15},{8,0},{9,1},... | collective-permute-start | bytes 638984 | tf_op jit(solution)/shard_map/ppermute | solution.py:488
  39.6 7.6 %collective-permute-start.16 = (bf16[4,208,128]{2,1,0:T(8,128)(2,1)S(1)}, bf16[4,208,128]{2,1,0:T(8,128)(2,1)S(1)}, u32[]{:S(2)}, u32[]{:S(2)}) collective-permute-start(bf16[4,208,128]{2,1,0:T(8,128)(2,1)S(1)} %get-tuple-element.53), channel_id=1, source_target_pairs={{0,12},{1,13},{2,14},{3,15},{4,0},{5,1},{6,2},{7,3},{8,4},{9,5},{1... | collective-permute-start | bytes 638984 | tf_op jit(solution)/shard_map/ppermute | solution.py:488
  41.6 10.3 %collective-permute-start.20 = (bf16[4,208,128]{2,1,0:T(8,128)(2,1)S(1)}, bf16[4,208,128]{2,1,0:T(8,128)(2,1)S(1)}, u32[]{:S(2)}, u32[]{:S(2)}) collective-permute-start(bf16[4,208,128]{2,1,0:T(8,128)(2,1)S(1)} %get-tuple-element.55), channel_id=1, source_target_pairs={{0,4},{1,5},{2,6},{3,7},{4,8},{5,9},{6,10},{7,11},{8,12},{9,13},{1... | collective-permute-start | bytes 638984 | tf_op jit(solution)/shard_map/ppermute | solution.py:488
  42.7 10.8 %collective-permute-start.21 = (bf16[4,208,128]{2,1,0:T(8,128)(2,1)S(1)}, bf16[4,208,128]{2,1,0:T(8,128)(2,1)S(1)}, u32[]{:S(2)}, u32[]{:S(2)}) collective-permute-start(bf16[4,208,128]{2,1,0:T(8,128)(2,1)S(1)} %get-tuple-element.56), channel_id=1, source_target_pairs={{0,8},{1,9},{2,10},{3,11},{4,12},{5,13},{6,14},{7,15},{8,0},{9,1},... | collective-permute-start | bytes 638984 | tf_op jit(solution)/shard_map/ppermute | solution.py:488
  45.1 10.3 %collective-permute-start.22 = (bf16[4,208,128]{2,1,0:T(8,128)(2,1)S(1)}, bf16[4,208,128]{2,1,0:T(8,128)(2,1)S(1)}, u32[]{:S(2)}, u32[]{:S(2)}) collective-permute-start(bf16[4,208,128]{2,1,0:T(8,128)(2,1)S(1)} %get-tuple-element.57), channel_id=1, source_target_pairs={{0,12},{1,13},{2,14},{3,15},{4,0},{5,1},{6,2},{7,3},{8,4},{9,5},{1... | collective-permute-start | bytes 638984 | tf_op jit(solution)/shard_map/ppermute | solution.py:488
  47.4 13.0 %collective-permute-start.19 = (bf16[4,208,128]{2,1,0:T(8,128)(2,1)S(1)}, bf16[4,208,128]{2,1,0:T(8,128)(2,1)S(1)}, u32[]{:S(2)}, u32[]{:S(2)}) collective-permute-start(bf16[4,208,128]{2,1,0:T(8,128)(2,1)S(1)} %pad_maximum_fusion.3), channel_id=1, source_target_pairs={{0,3},{1,0},{2,1},{3,2},{4,7},{5,4},{6,5},{7,6},{8,11},{9,8},{10,9... | collective-permute-start | bytes 638984 | tf_op jit(solution)/shard_map/ppermute | solution.py:488
  50.5 11.1 %collective-permute-start.18 = (bf16[4,208,128]{2,1,0:T(8,128)(2,1)S(1)}, bf16[4,208,128]{2,1,0:T(8,128)(2,1)S(1)}, u32[]{:S(2)}, u32[]{:S(2)}) collective-permute-start(bf16[4,208,128]{2,1,0:T(8,128)(2,1)S(1)} %pad_maximum_fusion.2), channel_id=1, source_target_pairs={{0,2},{1,3},{2,0},{3,1},{4,6},{5,7},{6,4},{7,5},{8,10},{9,11},{10,... | collective-permute-start | bytes 638984 | tf_op jit(solution)/shard_map/ppermute | solution.py:488
  51.9 9.7 %collective-permute-start.17 = (bf16[4,208,128]{2,1,0:T(8,128)(2,1)S(1)}, bf16[4,208,128]{2,1,0:T(8,128)(2,1)S(1)}, u32[]{:S(2)}, u32[]{:S(2)}) collective-permute-start(bf16[4,208,128]{2,1,0:T(8,128)(2,1)S(1)} %pad_maximum_fusion.1), channel_id=1, source_target_pairs={{0,1},{1,2},{2,3},{3,0},{4,5},{5,6},{6,7},{7,4},{8,9},{9,10},{10,1... | collective-permute-start | bytes 638984 | tf_op jit(solution)/shard_map/ppermute | solution.py:488
  55.4 14.2 %collective-permute-start.25 = (bf16[4,208,128]{2,1,0:T(8,128)(2,1)S(1)}, bf16[4,208,128]{2,1,0:T(8,128)(2,1)S(1)}, u32[]{:S(2)}, u32[]{:S(2)}) collective-permute-start(bf16[4,208,128]{2,1,0:T(8,128)(2,1)S(1)} %pad_maximum_fusion.7), channel_id=1, source_target_pairs={{0,3},{1,0},{2,1},{3,2},{4,7},{5,4},{6,5},{7,6},{8,11},{9,8},{10,9... | collective-permute-start | bytes 638984 | tf_op jit(solution)/shard_map/ppermute | solution.py:488
  59.8 9.9 %collective-permute-start.24 = (bf16[4,208,128]{2,1,0:T(8,128)(2,1)S(1)}, bf16[4,208,128]{2,1,0:T(8,128)(2,1)S(1)}, u32[]{:S(2)}, u32[]{:S(2)}) collective-permute-start(bf16[4,208,128]{2,1,0:T(8,128)(2,1)S(1)} %pad_maximum_fusion.6), channel_id=1, source_target_pairs={{0,2},{1,3},{2,0},{3,1},{4,6},{5,7},{6,4},{7,5},{8,10},{9,11},{10,... | collective-permute-start | bytes 638984 | tf_op jit(solution)/shard_map/ppermute | solution.py:488
  60.4 9.3 %collective-permute-start.23 = (bf16[4,208,128]{2,1,0:T(8,128)(2,1)S(1)}, bf16[4,208,128]{2,1,0:T(8,128)(2,1)S(1)}, u32[]{:S(2)}, u32[]{:S(2)}) collective-permute-start(bf16[4,208,128]{2,1,0:T(8,128)(2,1)S(1)} %pad_maximum_fusion.5), channel_id=1, source_target_pairs={{0,1},{1,2},{2,3},{3,0},{4,5},{5,6},{6,7},{7,4},{8,9},{9,10},{10,1... | collective-permute-start | bytes 638984 | tf_op jit(solution)/shard_map/ppermute | solution.py:488
  66.2 10.2 %collective-permute-start.35 = (bf16[4,4,128,128]{3,2,1,0:T(8,128)(2,1)S(1)}, bf16[4,4,128,128]{3,2,1,0:T(8,128)(2,1)S(1)}, u32[]{:S(2)}, u32[]{:S(2)}) collective-permute-start(bf16[4,4,128,128]{3,2,1,0:T(8,128)(2,1)S(1)} %get-tuple-element.70), channel_id=1, source_target_pairs={{0,12},{1,13},{2,14},{3,15},{4,0},{5,1},{6,2},{7,3},{8,4},{9,5},{1... | collective-permute-start | bytes 1572872 | tf_op jit(solution)/shard_map/ppermute | solution.py:488
  74.3 10.5 %collective-permute-start.27 = (bf16[4,4,128,128]{3,2,1,0:T(8,128)(2,1)S(1)}, bf16[4,4,128,128]{3,2,1,0:T(8,128)(2,1)S(1)}, u32[]{:S(2)}, u32[]{:S(2)}) collective-permute-start(bf16[4,4,128,128]{3,2,1,0:T(8,128)(2,1)S(1)} %get-tuple-element.65), channel_id=1, source_target_pairs={{0,4},{1,5},{2,6},{3,7},{4,8},{5,9},{6,10},{7,11},{8,12},{9,13},{1... | collective-permute-start | bytes 1572872 | tf_op jit(solution)/shard_map/ppermute | solution.py:488
  74.4 16.0 %collective-permute-start.34 = (bf16[4,4,128,128]{3,2,1,0:T(8,128)(2,1)S(1)}, bf16[4,4,128,128]{3,2,1,0:T(8,128)(2,1)S(1)}, u32[]{:S(2)}, u32[]{:S(2)}) collective-permute-start(bf16[4,4,128,128]{3,2,1,0:T(8,128)(2,1)S(1)} %get-tuple-element.68), channel_id=1, source_target_pairs={{0,4},{1,5},{2,6},{3,7},{4,8},{5,9},{6,10},{7,11},{8,12},{9,13},{1... | collective-permute-start | bytes 1572872 | tf_op jit(solution)/shard_map/ppermute | solution.py:488
  76.5 13.8 %collective-permute-start.36 = (bf16[4,4,128,128]{3,2,1,0:T(8,128)(2,1)S(1)}, bf16[4,4,128,128]{3,2,1,0:T(8,128)(2,1)S(1)}, u32[]{:S(2)}, u32[]{:S(2)}) collective-permute-start(bf16[4,4,128,128]{3,2,1,0:T(8,128)(2,1)S(1)} %add_convert_fusion.1), channel_id=1, source_target_pairs={{0,12},{1,13},{2,14},{3,15},{4,0},{5,1},{6,2},{7,3},{8,4},{9,5},{1... | collective-permute-start | bytes 1572872 | tf_op jit(solution)/shard_map/ppermute | solution.py:488
  80.3 17.3 %collective-permute-start.26 = (bf16[4,4,128,128]{3,2,1,0:T(8,128)(2,1)S(1)}, bf16[4,4,128,128]{3,2,1,0:T(8,128)(2,1)S(1)}, u32[]{:S(2)}, u32[]{:S(2)}) collective-permute-start(bf16[4,4,128,128]{3,2,1,0:T(8,128)(2,1)S(1)} %get-tuple-element.63), channel_id=1, source_target_pairs={{0,12},{1,13},{2,14},{3,15},{4,0},{5,1},{6,2},{7,3},{8,4},{9,5},{1... | collective-permute-start | bytes 1572872 | tf_op jit(solution)/shard_map/ppermute | solution.py:488
  84.9 13.1 %collective-permute-start.28 = (bf16[4,4,128,128]{3,2,1,0:T(8,128)(2,1)S(1)}, bf16[4,4,128,128]{3,2,1,0:T(8,128)(2,1)S(1)}, u32[]{:S(2)}, u32[]{:S(2)}) collective-permute-start(bf16[4,4,128,128]{3,2,1,0:T(8,128)(2,1)S(1)} %add_convert_fusion.3), channel_id=1, source_target_pairs={{0,4},{1,5},{2,6},{3,7},{4,8},{5,9},{6,10},{7,11},{8,12},{9,13},{1... | collective-permute-start | bytes 1572872 | tf_op jit(solution)/shard_map/ppermute | solution.py:488
  90.6 16.0 %collective-permute-start.37 = (bf16[4,4,128,128]{3,2,1,0:T(8,128)(2,1)S(1)}, bf16[4,4,128,128]{3,2,1,0:T(8,128)(2,1)S(1)}, u32[]{:S(2)}, u32[]{:S(2)}) collective-permute-start(bf16[4,4,128,128]{3,2,1,0:T(8,128)(2,1)S(1)} %add_convert_fusion.own_ref), channel_id=1, source_target_pairs={{0,3},{1,0},{2,1},{3,2},{4,7},{5,4},{6,5},{7,6},{8,11},{9,8},{10,9... | collective-permute-start | bytes 1572872 | tf_op jit(solution)/shard_map/ppermute | solution.py:488
  98.2 11.5 %collective-permute-start.30 = (bf16[4,4,128,128]{3,2,1,0:T(8,128)(2,1)S(1)}, bf16[4,4,128,128]{3,2,1,0:T(8,128)(2,1)S(1)}, u32[]{:S(2)}, u32[]{:S(2)}) collective-permute-start(bf16[4,4,128,128]{3,2,1,0:T(8,128)(2,1)S(1)} %add_convert_fusion.2.own_ref), channel_id=1, source_target_pairs={{0,1},{1,2},{2,3},{3,0},{4,5},{5,6},{6,7},{7,4},{8,9},{9,10},{10,1... | collective-permute-start | bytes 1572872 | tf_op jit(solution)/shard_map/ppermute | solution.py:488
  103.1 12.3 %collective-permute-start.39 = (bf16[4,4,128,128]{3,2,1,0:T(8,128)(2,1)S(1)}, bf16[4,4,128,128]{3,2,1,0:T(8,128)(2,1)S(1)}, u32[]{:S(2)}, u32[]{:S(2)}) collective-permute-start(bf16[4,4,128,128]{3,2,1,0:T(8,128)(2,1)S(1)} %add_convert_fusion.own_ref), channel_id=1, source_target_pairs={{0,1},{1,2},{2,3},{3,0},{4,5},{5,6},{6,7},{7,4},{8,9},{9,10},{10,1... | collective-permute-start | bytes 1572872 | tf_op jit(solution)/shard_map/ppermute | solution.py:488
  103.4 25.3 %collective-permute-start.29 = (bf16[4,4,128,128]{3,2,1,0:T(8,128)(2,1)S(1)}, bf16[4,4,128,128]{3,2,1,0:T(8,128)(2,1)S(1)}, u32[]{:S(2)}, u32[]{:S(2)}) collective-permute-start(bf16[4,4,128,128]{3,2,1,0:T(8,128)(2,1)S(1)} %add_convert_fusion.2.own_ref), channel_id=1, source_target_pairs={{0,3},{1,0},{2,1},{3,2},{4,7},{5,4},{6,5},{7,6},{8,11},{9,8},{10,9... | collective-permute-start | bytes 1572872 | tf_op jit(solution)/shard_map/ppermute | solution.py:488
  106.6 17.9 %collective-permute-start.38 = (bf16[4,4,128,128]{3,2,1,0:T(8,128)(2,1)S(1)}, bf16[4,4,128,128]{3,2,1,0:T(8,128)(2,1)S(1)}, u32[]{:S(2)}, u32[]{:S(2)}) collective-permute-start(bf16[4,4,128,128]{3,2,1,0:T(8,128)(2,1)S(1)} %collective-permute-done.37.next_ref), channel_id=1, source_target_pairs={{0,3},{1,0},{2,1},{3,2},{4,7},{5,4},{6,5},{7,6},{8,11},{9,8},{10,9... | collective-permute-start | bytes 1572872 | tf_op jit(solution)/shard_map/ppermute | solution.py:488
  109.8 18.9 %collective-permute-start.31 = (bf16[4,4,128,128]{3,2,1,0:T(8,128)(2,1)S(1)}, bf16[4,4,128,128]{3,2,1,0:T(8,128)(2,1)S(1)}, u32[]{:S(2)}, u32[]{:S(2)}) collective-permute-start(bf16[4,4,128,128]{3,2,1,0:T(8,128)(2,1)S(1)} %collective-permute-done.30.prev_ref), channel_id=1, source_target_pairs={{0,1},{1,2},{2,3},{3,0},{4,5},{5,6},{6,7},{7,4},{8,9},{9,10},{10,1... | collective-permute-start | bytes 1572872 | tf_op jit(solution)/shard_map/ppermute | solution.py:488
  125.4 18.4 %collective-permute-start.40 = (bf16[4,4,128,128]{3,2,1,0:T(8,128)(2,1)S(1)}, bf16[4,4,128,128]{3,2,1,0:T(8,128)(2,1)S(1)}, u32[]{:S(2)}, u32[]{:S(2)}) collective-permute-start(bf16[4,4,128,128]{3,2,1,0:T(8,128)(2,1)S(1)} %get-tuple-element.71.refs_1_), channel_id=1, source_target_pairs={{0,12},{1,13},{2,14},{3,15},{4,0},{5,1},{6,2},{7,3},{8,4},{9,5},{1... | collective-permute-start | bytes 1572872 | tf_op jit(solution)/shard_map/ppermute | solution.py:488
  129.5 16.3 %collective-permute-start.32 = (bf16[4,4,128,128]{3,2,1,0:T(8,128)(2,1)S(1)}, bf16[4,4,128,128]{3,2,1,0:T(8,128)(2,1)S(1)}, u32[]{:S(2)}, u32[]{:S(2)}) collective-permute-start(bf16[4,4,128,128]{3,2,1,0:T(8,128)(2,1)S(1)} %get-tuple-element.66.refs_0_), channel_id=1, source_target_pairs={{0,4},{1,5},{2,6},{3,7},{4,8},{5,9},{6,10},{7,11},{8,12},{9,13},{1... | collective-permute-start | bytes 1572872 | tf_op jit(solution)/shard_map/ppermute | solution.py:488
  140.6 14.7 %collective-permute-start.43 = (bf16[4,4,128,128]{3,2,1,0:T(8,128)(2,1)S(1)}, bf16[4,4,128,128]{3,2,1,0:T(8,128)(2,1)S(1)}, u32[]{:S(2)}, u32[]{:S(2)}) collective-permute-start(bf16[4,4,128,128]{3,2,1,0:T(8,128)(2,1)S(1)} %get-tuple-element.71.refs_1_), channel_id=1, source_target_pairs={{0,4},{1,5},{2,6},{3,7},{4,8},{5,9},{6,10},{7,11},{8,12},{9,13},{1... | collective-permute-start | bytes 1572872 | tf_op jit(solution)/shard_map/ppermute | solution.py:488
  140.6 14.7 %collective-permute-start.42 = (bf16[4,4,128,128]{3,2,1,0:T(8,128)(2,1)S(1)}, bf16[4,4,128,128]{3,2,1,0:T(8,128)(2,1)S(1)}, u32[]{:S(2)}, u32[]{:S(2)}) collective-permute-start(bf16[4,4,128,128]{3,2,1,0:T(8,128)(2,1)S(1)} %get-tuple-element.66.refs_0_), channel_id=1, source_target_pairs={{0,12},{1,13},{2,14},{3,15},{4,0},{5,1},{6,2},{7,3},{8,4},{9,5},{1... | collective-permute-start | bytes 1572872 | tf_op jit(solution)/shard_map/ppermute | solution.py:488
  143.8 14.0 %collective-permute-start.41 = (bf16[4,4,128,128]{3,2,1,0:T(8,128)(2,1)S(1)}, bf16[4,4,128,128]{3,2,1,0:T(8,128)(2,1)S(1)}, u32[]{:S(2)}, u32[]{:S(2)}) collective-permute-start(bf16[4,4,128,128]{3,2,1,0:T(8,128)(2,1)S(1)} %collective-permute-done.40.refs_3_), channel_id=1, source_target_pairs={{0,12},{1,13},{2,14},{3,15},{4,0},{5,1},{6,2},{7,3},{8,4},{9,5},{1... | collective-permute-start | bytes 1572872 | tf_op jit(solution)/shard_map/ppermute | solution.py:488
  145.8 12.0 %collective-permute-start.33 = (bf16[4,4,128,128]{3,2,1,0:T(8,128)(2,1)S(1)}, bf16[4,4,128,128]{3,2,1,0:T(8,128)(2,1)S(1)}, u32[]{:S(2)}, u32[]{:S(2)}) collective-permute-start(bf16[4,4,128,128]{3,2,1,0:T(8,128)(2,1)S(1)} %collective-permute-done.32.refs_4_), channel_id=1, source_target_pairs={{0,4},{1,5},{2,6},{3,7},{4,8},{5,9},{6,10},{7,11},{8,12},{9,13},{1... | collective-permute-start | bytes 1572872 | tf_op jit(solution)/shard_map/ppermute | solution.py:488
  (28 other events, 266.4 us)
